TPU v7x, 512 devices: a whole 4x8x8 slice. The times are simulated.
512 devices in a mesh: tm: 32 (over y_hi, z, core), space: 16 (over y_lo, x).
Axes of the slice: x: 4, y: 8 (y_hi: 2, y_lo: 4; y = y_hi * 4 + y_lo), z: 8, core: 2. Of those that a mesh axis runs over, the one named last changes fastest.
Arguments:
- iterate: float32 [256, 16, 128, 128], P('tm', 'space'), may hold values from -6 to 6
- forcing: float32 [256, 16, 128, 128], P('tm', 'space'), may hold values from -6 to 6
- start_field: float32 [16, 128, 128], P('space'), may hold values from -6 to 6
- classes: int32 [16, 128, 128], P('space'), may hold values from 0 to 7
- open_mask: int32 [16, 128, 128], P('space'), may hold values 0 or 1
- diffusivity: float32 [8], replicated, may hold values from 0.3 to 3
- drift: float32 [3, 8], replicated, may hold values from -0.9 to 0.9
Outputs:
- residual: float32 [256, 16, 128, 128], P('tm', 'space')
- corrected: float32 [256, 16, 128, 128], P('tm', 'space')
All inputs are finite; a program needn't handle non-finite values. No bound on the sum of `open_mask` on one device may be relied on, other than what follows from the above.
Results may differ from a plain program's by a relative error of at most 0.0003.
Values sent between devices are 32-bit elements; how exact they have to be, the bound alone decides.
No kernel may reach another device: no remote copies, remote signals or barrier semaphores. Data moves between devices by JAX's collectives and lax.ppermute only.
A program may use at most 64 MiB of HBM per device.

v0:
```python
import math

import jax
import jax.numpy as jnp
from jax import lax
from jax.sharding import PartitionSpec as P

SWEEPS = 4


ALPHA = 0.1


def with_halo(value, sides, width):
    for axis, dim in sides:
        count, length = (lax.axis_size(axis), value.shape[dim])
        up = [(i, (i + 1) % count) for i in range(count - 1)]
        down = [(j, i) for i, j in up]
        last = lax.slice_in_dim(value, length - width, length, axis=dim)
        initial = lax.slice_in_dim(value, 0, width, axis=dim)
        before = lax.ppermute(last, axis, up)
        after = lax.ppermute(initial, axis, down)
        value = jnp.concatenate([before, value, after], axis=dim)
    return value


def shifted(value, axis, by):
    count = lax.axis_size(axis)
    pairs = [(i, i + by) for i in range(count) if 0 <= i + by < count]
    return lax.ppermute(value, axis, pairs)


def step_tables(length):
    index = jnp.arange(length, dtype=jnp.int32)
    folded = index[:, None] * index[None, :] % length
    angle = folded.astype(jnp.float32) * (2.0 * math.pi / length)
    cosine = jnp.cos(angle)
    sine = jnp.sin(angle)
    ramp = jnp.exp(index.astype(jnp.float32) * (math.log(ALPHA) / length))
    forward_re = cosine * ramp[None, :]
    forward_im = -sine * ramp[None, :]
    back_re = cosine / (ramp[:, None] * length)
    back_im = -sine / (ramp[:, None] * length)
    root = math.exp(math.log(ALPHA) / length)
    base = index.astype(jnp.float32) * (2.0 * math.pi / length)
    shift_re = 1.0 - root * jnp.cos(base)
    shift_im = root * jnp.sin(base)
    return (forward_re, forward_im, back_re, back_im, shift_re, shift_im)


def coefficients(classes, open_mask, diffusivity, drift):
    kappa = jnp.zeros(classes.shape, jnp.float32)
    tilt_x = jnp.zeros(classes.shape, jnp.float32)
    tilt_y = jnp.zeros(classes.shape, jnp.float32)
    tilt_z = jnp.zeros(classes.shape, jnp.float32)
    for level in range(diffusivity.shape[0]):
        match = classes == level
        kappa = jnp.where(match, diffusivity[level], kappa)
        tilt_x = jnp.where(match, drift[0, level], tilt_x)
        tilt_y = jnp.where(match, drift[1, level], tilt_y)
        tilt_z = jnp.where(match, drift[2, level], tilt_z)
    weight = open_mask.astype(jnp.float32)
    return (weight, kappa, kappa * tilt_x, kappa * tilt_y, kappa * tilt_z)


def couple(padded, kappa, flow_x, flow_y, flow_z):
    east = padded[..., 2:, 1:-1, 1:-1]
    west = padded[..., :-2, 1:-1, 1:-1]
    north = padded[..., 1:-1, 2:, 1:-1]
    south = padded[..., 1:-1, :-2, 1:-1]
    upper = padded[..., 1:-1, 1:-1, 2:]
    lower = padded[..., 1:-1, 1:-1, :-2]
    total = kappa * (east + west + north + south + upper + lower)
    return total - flow_x * (east - west) - flow_y * (north - south) - flow_z * (upper - lower)


def solve(source, shift_re, shift_im, weight, kappa, flow_x, flow_y, flow_z, extend):
    real_part = shift_re + 6.0 * kappa
    norm = real_part * real_part + shift_im * shift_im
    inv_re = real_part / norm
    inv_im = -shift_im / norm

    def update(total):
        return jnp.stack(
            [
                weight * (total[0] * inv_re - total[1] * inv_im),
                weight * (total[0] * inv_im + total[1] * inv_re),
            ]
        )

    field = update(source)
    for sweep in range(SWEEPS):
        field = update(source + couple(extend(field), kappa, flow_x, flow_y, flow_z))
    return field


def slab_extend(field):
    padded = with_halo(field, (("space", 2),), 1)
    return jnp.pad(padded, ((0, 0), (0, 0), (0, 0), (1, 1), (1, 1)))


def local(iterate, forcing, start_field, classes, open_mask, diffusivity, drift):
    steps = iterate.shape[0]
    groups = lax.axis_size("tm")
    length = steps * groups
    position = lax.axis_index("tm")
    weight, kappa, flow_x, flow_y, flow_z = coefficients(classes, open_mask, diffusivity, drift)
    arrived = shifted(iterate[-1], "tm", 1)
    first = jnp.where(position == 0, start_field, arrived)
    previous = jnp.concatenate([first[None], iterate[:-1]], axis=0)
    masked = iterate * weight
    padded = with_halo(masked, (("space", 1),), 1)
    padded = jnp.pad(padded, ((0, 0), (0, 0), (1, 1), (1, 1)))
    applied = weight * (6.0 * kappa * masked - couple(padded, kappa, flow_x, flow_y, flow_z))
    residual = weight * (forcing + previous - iterate) - applied
    forward_re, forward_im, back_re, back_im, shift_re, shift_im = step_tables(length)
    cells = lax.all_to_all(residual, "tm", split_axis=2, concat_axis=0, tiled=True)
    flat = cells.reshape(length, -1)
    spec_re = jnp.dot(forward_re, flat, precision=lax.Precision.HIGHEST).reshape(cells.shape)
    spec_im = jnp.dot(forward_im, flat, precision=lax.Precision.HIGHEST).reshape(cells.shape)
    spectrum = jnp.stack([spec_re, spec_im])
    frequencies = lax.all_to_all(spectrum, "tm", split_axis=1, concat_axis=3, tiled=True)
    offset = position * steps
    local_re = lax.dynamic_slice_in_dim(shift_re, offset, steps, 0).reshape(steps, 1, 1, 1)
    local_im = lax.dynamic_slice_in_dim(shift_im, offset, steps, 0).reshape(steps, 1, 1, 1)
    local_solved = solve(
        frequencies, local_re, local_im, weight, kappa, flow_x, flow_y, flow_z, slab_extend
    )
    solved = lax.all_to_all(local_solved, "tm", split_axis=3, concat_axis=1, tiled=True)
    part_re = solved[0].reshape(length, -1)
    part_im = solved[1].reshape(length, -1)
    combined = jnp.dot(back_re, part_re, precision=lax.Precision.HIGHEST) + jnp.dot(
        back_im, part_im, precision=lax.Precision.HIGHEST
    )
    combined = combined.reshape(solved.shape[1:])
    corrected = lax.all_to_all(combined, "tm", split_axis=0, concat_axis=2, tiled=True)
    return (residual, corrected)


def solution(mesh):
    placed = (
        P("tm", "space", None, None),
        P("tm", "space", None, None),
        P("space", None, None),
        P("space", None, None),
        P("space", None, None),
        P(),
        P(),
    )
    return jax.shard_map(
        local,
        mesh=mesh,
        in_specs=placed,
        out_specs=(P("tm", "space", None, None), P("tm", "space", None, None)),
        check_vma=False,
    )
```

profile of v0, /device:TPU:22, one launch (start us, length us, event | category | flops | bytes accessed | tf_op | source)
XLA Modules:
  0.0 355.3 jit_solution(13985828133663914772)
XLA Ops:
  2.7 2.7 collective-permute-start.1
  5.4 5.2 %collective-permute-start.2 = (f32[8,1,128,128]{3,2,1,0:T(8,128)S(1)}, f32[8,1,128,128]{3,2,1,0:T(8,128)S(1)}, u32[]{:S(2)}, u32[]{:S(2)}) collective-permute-start(f32[8,1,128,128]{3,2,1,0:T(8,128)S(1)} %broadcast_multiply_fusion), channel_id=1, source_target_pairs={{0,1},{1,2},{2,3},{3,4},{4,5},{5,6},{6,7},{7,8},{8,9},{9,10},{10,1... | collective-permute-start | bytes 1572872 | tf_op jit(solution)/shard_map/ppermute | solution.py:21
  12.8 2.1 fusion.62
  18.0 6.0 %multiply_bitcast_fusion.3 = (f32[128,128]{1,0:T(8,128)S(1)}, pred[1,128,128]{2,1,0:T(8,128)(4,1)S(1)}, pred[1,128,128]{2,1,0:T(8,128)(4,1)S(1)}, pred[1,128,128...) fusion(f32[]{:T(128)} %bitcast.10, f32[]{:T(128)} %bitcast.9, ...), kind=kLoop, calls=%fused_computation.101 | loop fusion | flops 278528 | bytes 262176 | tf_op jit(solution)/shard_map/mul | solution.py:114
  24.0 5.1 %fusion.60 = f32[128,128]{1,0:T(8,128)S(1)} fusion(pred[1,128,128]{2,1,0:T(8,128)(4,1)S(1)} %get-tuple-element.14, pred[1,128,128]{2,1,0:T(8,128)(4,1)S(1)} %get-tuple-element.13, pred[1,128,128]{2,1,0:T(8,128)(4,1)S(1)} %get-tuple-element.12, pred[1,128,128]{2,1,0:T(8,128)(4,1)S(1)} %get-tuple-element.11, pred[1,128,128]{2,1,0:T(8,128)(4,1)S(1)} %get-tuple-element.10, ...), kind=kLoop, calls=%fused_computation.137 | loop fusion | flops 131072 | bytes 196640 | tf_op jit(solution)/shard_map/mul | solution.py:73
  29.1 10.2 %multiply_bitcast_fusion.1 = f32[128,128]{1,0:T(8,128)S(1)} fusion(pred[1,128,128]{2,1,0:T(8,128)(4,1)S(1)} %get-tuple-element.14, pred[1,128,128]{2,1,0:T(8,128)(4,1)S(1)} %get-tuple-element.13, pred[1,128,128]{2,1,0:T(8,128)(4,1)S(1)} %get-tuple-element.12, pred[1,128,128]{2,1,0:T(8,128)(4,1)S(1)} %get-tuple-element.11, ...), kind=kLoop, calls=%fused_computation.99 | loop fusion | flops 278528 | bytes 196672 | tf_op jit(solution)/shard_map/mul | solution.py:74
  39.3 10.0 %multiply_bitcast_fusion = f32[128,128]{1,0:T(8,128)S(1)} fusion(pred[1,128,128]{2,1,0:T(8,128)(4,1)S(1)} %get-tuple-element.14, pred[1,128,128]{2,1,0:T(8,128)(4,1)S(1)} %get-tuple-element.13, pred[1,128,128]{2,1,0:T(8,128)(4,1)S(1)} %get-tuple-element.12, pred[1,128,128]{2,1,0:T(8,128)(4,1)S(1)} %get-tuple-element.11, ...), kind=kLoop, calls=%fused_computation.98 | loop fusion | flops 278528 | bytes 196672 | tf_op jit(solution)/shard_map/mul | solution.py:74
  49.3 10.0 %multiply_bitcast_fusion.2 = f32[128,128]{1,0:T(8,128)S(1)} fusion(pred[1,128,128]{2,1,0:T(8,128)(4,1)S(1)} %get-tuple-element.14, pred[1,128,128]{2,1,0:T(8,128)(4,1)S(1)} %get-tuple-element.13, pred[1,128,128]{2,1,0:T(8,128)(4,1)S(1)} %get-tuple-element.12, pred[1,128,128]{2,1,0:T(8,128)(4,1)S(1)} %get-tuple-element.11, ...), kind=kLoop, calls=%fused_computation.100 | loop fusion | flops 278528 | bytes 196672 | tf_op jit(solution)/shard_map/mul | solution.py:74
  64.7 15.1 %all-to-all-start = ((f32[8,1,128,128]{3,0,1,2:T(8,128)}), f32[8,1,128,128]{3,0,1,2:T(8,128)S(1)}, u32[]{:S(2)}, u32[]{:S(2)}) async-start(f32[8,1,128,128]{3,0,1,2:T(8,128)} %copy.54), calls=%async_computation | async-start | bytes 1048576 | tf_op jit(solution)/shard_map/all_to_all | solution.py:117
  79.9 22.8 %all-to-all-done = f32[8,1,128,128]{3,0,1,2:T(8,128)S(1)} async-done(((f32[8,1,128,128]{3,0,1,2:T(8,128)}), f32[8,1,128,128]{3,0,1,2:T(8,128)S(1)}, u32[]{:S(2)}, u32[]{:S(2)}) %all-to-all-start) | async-done | bytes 524320 | tf_op jit(solution)/shard_map/all_to_all | solution.py:117
  108.0 3.9 %all-to-all-start.1 = ((f32[2,256,1,4,128]{4,3,2,0,1:T(4,128)}), f32[2,256,1,4,128]{4,3,2,0,1:T(4,128)S(1)}, u32[]{:S(2)}, u32[]{:S(2)}) async-start(f32[2,256,1,4,128]{4,3,2,0,1:T(4,128)} %copy.56), calls=%async_computation.1 | async-start | bytes 2097152 | tf_op jit(solution)/shard_map/all_to_all | solution.py:122
  112.2 33.1 %all-to-all-done.1 = f32[2,256,1,4,128]{4,3,2,0,1:T(4,128)S(1)} async-done(((f32[2,256,1,4,128]{4,3,2,0,1:T(4,128)}), f32[2,256,1,4,128]{4,3,2,0,1:T(4,128)S(1)}, u32[]{:S(2)}, u32[]{:S(2)}) %all-to-all-start.1) | async-done | bytes 1048608 | tf_op jit(solution)/shard_map/all_to_all | solution.py:122
  146.1 1.9 collective-permute-start.3
  148.1 6.2 %collective-permute-start.4 = (f32[2,8,1,128,128]{4,1,3,0,2:T(8,128)S(1)}, f32[2,8,1,128,128]{4,1,3,0,2:T(8,128)S(1)}, u32[]{:S(2)}, u32[]{:S(2)}) collective-permute-start(f32[2,8,1,128,128]{4,1,3,0,2:T(8,128)S(1)} %pad_maximum_fusion.1), channel_id=1, source_target_pairs={{0,1},{1,2},{2,3},{3,4},{4,5},{5,6},{6,7},{7,8},{8,9},{9,10},{10,1... | collective-permute-start | bytes 3145736 | tf_op jit(solution)/shard_map/ppermute | solution.py:21
  154.4 20.3 %collective-permute-done.3 = f32[2,8,1,128,128]{4,1,3,0,2:T(8,128)S(1)} collective-permute-done((f32[2,8,1,128,128]{4,1,3,0,2:T(8,128)S(1)}, f32[2,8,1,128,128]{4,1,3,0,2:T(8,128)S(1)}, u32[]{:S(2)}, u32[]{:S(2)}) %collective-permute-start.3) | collective-permute-done | bytes 1048608 | tf_op jit(solution)/shard_map/ppermute | solution.py:22
  175.9 3.3 select_maximum_fusion.9
  180.6 1.9 collective-permute-start.5
  182.6 6.5 %collective-permute-start.6 = (f32[2,8,1,128,128]{4,1,3,0,2:T(8,128)S(1)}, f32[2,8,1,128,128]{4,1,3,0,2:T(8,128)S(1)}, u32[]{:S(2)}, u32[]{:S(2)}) collective-permute-start(f32[2,8,1,128,128]{4,1,3,0,2:T(8,128)S(1)} %pad_maximum_fusion.2), channel_id=1, source_target_pairs={{0,1},{1,2},{2,3},{3,4},{4,5},{5,6},{6,7},{7,8},{8,9},{9,10},{10,1... | collective-permute-start | bytes 3145736 | tf_op jit(solution)/shard_map/ppermute | solution.py:21
  189.1 19.8 %collective-permute-done.5 = f32[2,8,1,128,128]{4,1,3,0,2:T(8,128)S(1)} collective-permute-done((f32[2,8,1,128,128]{4,1,3,0,2:T(8,128)S(1)}, f32[2,8,1,128,128]{4,1,3,0,2:T(8,128)S(1)}, u32[]{:S(2)}, u32[]{:S(2)}) %collective-permute-start.5) | collective-permute-done | bytes 1048608 | tf_op jit(solution)/shard_map/ppermute | solution.py:22
  210.0 3.3 select_maximum_fusion.6
  214.8 1.9 collective-permute-start.7
  216.7 6.5 %collective-permute-start.8 = (f32[2,8,1,128,128]{4,1,3,0,2:T(8,128)S(1)}, f32[2,8,1,128,128]{4,1,3,0,2:T(8,128)S(1)}, u32[]{:S(2)}, u32[]{:S(2)}) collective-permute-start(f32[2,8,1,128,128]{4,1,3,0,2:T(8,128)S(1)} %pad_maximum_fusion.3), channel_id=1, source_target_pairs={{0,1},{1,2},{2,3},{3,4},{4,5},{5,6},{6,7},{7,8},{8,9},{9,10},{10,1... | collective-permute-start | bytes 3145736 | tf_op jit(solution)/shard_map/ppermute | solution.py:21
  223.2 18.9 %collective-permute-done.7 = f32[2,8,1,128,128]{4,1,3,0,2:T(8,128)S(1)} collective-permute-done((f32[2,8,1,128,128]{4,1,3,0,2:T(8,128)S(1)}, f32[2,8,1,128,128]{4,1,3,0,2:T(8,128)S(1)}, u32[]{:S(2)}, u32[]{:S(2)}) %collective-permute-start.7) | collective-permute-done | bytes 1048608 | tf_op jit(solution)/shard_map/ppermute | solution.py:22
  243.3 3.3 select_maximum_fusion.3
  248.0 6.5 %collective-permute-start.10 = (f32[2,8,1,128,128]{4,1,3,0,2:T(8,128)S(1)}, f32[2,8,1,128,128]{4,1,3,0,2:T(8,128)S(1)}, u32[]{:S(2)}, u32[]{:S(2)}) collective-permute-start(f32[2,8,1,128,128]{4,1,3,0,2:T(8,128)S(1)} %pad_maximum_fusion.4), channel_id=1, source_target_pairs={{0,1},{1,2},{2,3},{3,4},{4,5},{5,6},{6,7},{7,8},{8,9},{9,10},{10,1... | collective-permute-start | bytes 3145736 | tf_op jit(solution)/shard_map/ppermute | solution.py:21
  254.5 2.1 collective-permute-start.9
  256.7 17.1 %collective-permute-done.10 = f32[2,8,1,128,128]{4,1,3,0,2:T(8,128)S(1)} collective-permute-done((f32[2,8,1,128,128]{4,1,3,0,2:T(8,128)S(1)}, f32[2,8,1,128,128]{4,1,3,0,2:T(8,128)S(1)}, u32[]{:S(2)}, u32[]{:S(2)}) %collective-permute-start.10) | collective-permute-done | bytes 1048608 | tf_op jit(solution)/shard_map/ppermute | solution.py:21
  273.8 6.2 %collective-permute-done.9 = f32[2,8,1,128,128]{4,1,3,0,2:T(8,128)S(1)} collective-permute-done((f32[2,8,1,128,128]{4,1,3,0,2:T(8,128)S(1)}, f32[2,8,1,128,128]{4,1,3,0,2:T(8,128)S(1)}, u32[]{:S(2)}, u32[]{:S(2)}) %collective-permute-start.9) | collective-permute-done | bytes 1048608 | tf_op jit(solution)/shard_map/ppermute | solution.py:22
  280.0 3.3 select_maximum_fusion
  285.8 6.8 %all-to-all-start.2 = ((f32[2,8,1,128,128]{4,1,0,2,3:T(8,128)}), f32[2,8,1,128,128]{4,1,0,2,3:T(8,128)S(1)}, u32[]{:S(2)}, u32[]{:S(2)}) async-start(f32[2,8,1,128,128]{4,1,0,2,3:T(8,128)} %copy.65), calls=%async_computation.2 | async-start | bytes 2097152 | tf_op jit(solution)/shard_map/all_to_all | solution.py:129
  292.6 33.1 %all-to-all-done.2 = f32[2,8,1,128,128]{4,1,0,2,3:T(8,128)S(1)} async-done(((f32[2,8,1,128,128]{4,1,0,2,3:T(8,128)}), f32[2,8,1,128,128]{4,1,0,2,3:T(8,128)S(1)}, u32[]{:S(2)}, u32[]{:S(2)}) %all-to-all-start.2) | async-done | bytes 1048608 | tf_op jit(solution)/shard_map/all_to_all | solution.py:129
  329.3 25.1 %all_to_all.66 = f32[256,1,4,128]{3,2,1,0:T(4,128)S(1)} all-to-all(f32[256,1,4,128]{3,2,1,0:T(4,128)S(1)} %bitcast.109), channel_id=1, replica_groups=mesh['tm'=32,'space'=16] {'tm'}, dimensions={0} | all-to-all | bytes 1048576 | tf_op jit(solution)/shard_map/all_to_all | solution.py:136
  (58 shorter events, 33.5 us)
Async XLA Ops:
  0.6 61.2 %copy-start = (f32[8,1,128,128]{3,2,1,0:T(8,128)S(1)}, f32[8,1,128,128]{3,2,1,0:T(8,128)}, u32[]{:S(2)}) copy-start(f32[8,1,128,128]{3,2,1,0:T(8,128)} %param.7) | copy-start | bytes 1572868
  0.6 61.2 %slice-start = ((f32[8,1,128,128]{3,2,1,0:T(8,128)}), f32[7,1,128,128]{3,2,1,0:T(8,128)S(1)}, s32[]{:S(2)}) async-start(f32[8,1,128,128]{3,2,1,0:T(8,128)} %param.7), calls=%async_computation.4 | async-start | bytes 917504 | tf_op jit(solution)/shard_map/slice | solution.py:110
  2.7 57.6 %collective-permute-start.1 = (f32[8,1,128,128]{3,2,1,0:T(8,128)S(1)}, f32[8,1,128,128]{3,2,1,0:T(8,128)S(1)}, u32[]{:S(2)}, u32[]{:S(2)}) collective-permute-start(f32[8,1,128,128]{3,2,1,0:T(8,128)S(1)} %broadcast_multiply_fusion), channel_id=1, source_target_pairs={{1,0},{2,1},{3,2},{4,3},{5,4},{6,5},{7,6},{8,7},{9,8},{10,9},{11,1... | collective-permute-start | bytes 1572872 | tf_op jit(solution)/shard_map/ppermute | solution.py:22
  5.4 54.8 %collective-permute-start.2 = (f32[8,1,128,128]{3,2,1,0:T(8,128)S(1)}, f32[8,1,128,128]{3,2,1,0:T(8,128)S(1)}, u32[]{:S(2)}, u32[]{:S(2)}) collective-permute-start(f32[8,1,128,128]{3,2,1,0:T(8,128)S(1)} %broadcast_multiply_fusion), channel_id=1, source_target_pairs={{0,1},{1,2},{2,3},{3,4},{4,5},{5,6},{6,7},{7,8},{8,9},{9,10},{10,1... | collective-permute-start | bytes 1572872 | tf_op jit(solution)/shard_map/ppermute | solution.py:21
  11.5 47.9 %collective-permute-start = (f32[1,128,128]{2,1,0:T(8,128)S(1)}, f32[1,128,128]{2,1,0:T(8,128)S(1)}, u32[]{:S(2)}, u32[]{:S(2)}) collective-permute-start(f32[1,128,128]{2,1,0:T(8,128)S(1)} %slice_bitcast_fusion.4), channel_id=1, source_target_pairs={{0,16},{16,32},{32,48},{48,64},{64,80},{80,96},{96,112},{112,128},... | collective-permute-start | bytes 196616 | tf_op jit(solution)/shard_map/ppermute | solution.py:30
  63.6 81.9 %copy-start.1 = (f32[8,1,128,128]{3,2,1,0:T(8,128)}, f32[8,1,128,128]{3,2,1,0:T(8,128)S(1)}, u32[]{:S(2)}) copy-start(f32[8,1,128,128]{3,2,1,0:T(8,128)S(1)} %fusion.11) | copy-start | bytes 1572868
  64.7 38.0 %all-to-all-start = ((f32[8,1,128,128]{3,0,1,2:T(8,128)}), f32[8,1,128,128]{3,0,1,2:T(8,128)S(1)}, u32[]{:S(2)}, u32[]{:S(2)}) async-start(f32[8,1,128,128]{3,0,1,2:T(8,128)} %copy.54), calls=%async_computation | async-start | bytes 1048576 | tf_op jit(solution)/shard_map/all_to_all | solution.py:117
  108.0 37.3 %all-to-all-start.1 = ((f32[2,256,1,4,128]{4,3,2,0,1:T(4,128)}), f32[2,256,1,4,128]{4,3,2,0,1:T(4,128)S(1)}, u32[]{:S(2)}, u32[]{:S(2)}) async-start(f32[2,256,1,4,128]{4,3,2,0,1:T(4,128)} %copy.56), calls=%async_computation.1 | async-start | bytes 2097152 | tf_op jit(solution)/shard_map/all_to_all | solution.py:122
  146.1 28.6 %collective-permute-start.3 = (f32[2,8,1,128,128]{4,1,3,0,2:T(8,128)S(1)}, f32[2,8,1,128,128]{4,1,3,0,2:T(8,128)S(1)}, u32[]{:S(2)}, u32[]{:S(2)}) collective-permute-start(f32[2,8,1,128,128]{4,1,3,0,2:T(8,128)S(1)} %pad_maximum_fusion.1), channel_id=1, source_target_pairs={{1,0},{2,1},{3,2},{4,3},{5,4},{6,5},{7,6},{8,7},{9,8},{10,9},{11,1... | collective-permute-start | bytes 3145736 | tf_op jit(solution)/shard_map/ppermute | solution.py:22
  148.1 27.8 %collective-permute-start.4 = (f32[2,8,1,128,128]{4,1,3,0,2:T(8,128)S(1)}, f32[2,8,1,128,128]{4,1,3,0,2:T(8,128)S(1)}, u32[]{:S(2)}, u32[]{:S(2)}) collective-permute-start(f32[2,8,1,128,128]{4,1,3,0,2:T(8,128)S(1)} %pad_maximum_fusion.1), channel_id=1, source_target_pairs={{0,1},{1,2},{2,3},{3,4},{4,5},{5,6},{6,7},{7,8},{8,9},{9,10},{10,1... | collective-permute-start | bytes 3145736 | tf_op jit(solution)/shard_map/ppermute | solution.py:21
  180.6 28.2 %collective-permute-start.5 = (f32[2,8,1,128,128]{4,1,3,0,2:T(8,128)S(1)}, f32[2,8,1,128,128]{4,1,3,0,2:T(8,128)S(1)}, u32[]{:S(2)}, u32[]{:S(2)}) collective-permute-start(f32[2,8,1,128,128]{4,1,3,0,2:T(8,128)S(1)} %pad_maximum_fusion.2), channel_id=1, source_target_pairs={{1,0},{2,1},{3,2},{4,3},{5,4},{6,5},{7,6},{8,7},{9,8},{10,9},{11,1... | collective-permute-start | bytes 3145736 | tf_op jit(solution)/shard_map/ppermute | solution.py:22
  182.6 27.4 %collective-permute-start.6 = (f32[2,8,1,128,128]{4,1,3,0,2:T(8,128)S(1)}, f32[2,8,1,128,128]{4,1,3,0,2:T(8,128)S(1)}, u32[]{:S(2)}, u32[]{:S(2)}) collective-permute-start(f32[2,8,1,128,128]{4,1,3,0,2:T(8,128)S(1)} %pad_maximum_fusion.2), channel_id=1, source_target_pairs={{0,1},{1,2},{2,3},{3,4},{4,5},{5,6},{6,7},{7,8},{8,9},{9,10},{10,1... | collective-permute-start | bytes 3145736 | tf_op jit(solution)/shard_map/ppermute | solution.py:21
  214.8 27.3 %collective-permute-start.7 = (f32[2,8,1,128,128]{4,1,3,0,2:T(8,128)S(1)}, f32[2,8,1,128,128]{4,1,3,0,2:T(8,128)S(1)}, u32[]{:S(2)}, u32[]{:S(2)}) collective-permute-start(f32[2,8,1,128,128]{4,1,3,0,2:T(8,128)S(1)} %pad_maximum_fusion.3), channel_id=1, source_target_pairs={{1,0},{2,1},{3,2},{4,3},{5,4},{6,5},{7,6},{8,7},{9,8},{10,9},{11,1... | collective-permute-start | bytes 3145736 | tf_op jit(solution)/shard_map/ppermute | solution.py:22
  216.7 26.6 %collective-permute-start.8 = (f32[2,8,1,128,128]{4,1,3,0,2:T(8,128)S(1)}, f32[2,8,1,128,128]{4,1,3,0,2:T(8,128)S(1)}, u32[]{:S(2)}, u32[]{:S(2)}) collective-permute-start(f32[2,8,1,128,128]{4,1,3,0,2:T(8,128)S(1)} %pad_maximum_fusion.3), channel_id=1, source_target_pairs={{0,1},{1,2},{2,3},{3,4},{4,5},{5,6},{6,7},{7,8},{8,9},{9,10},{10,1... | collective-permute-start | bytes 3145736 | tf_op jit(solution)/shard_map/ppermute | solution.py:21
  248.0 25.7 %collective-permute-start.10 = (f32[2,8,1,128,128]{4,1,3,0,2:T(8,128)S(1)}, f32[2,8,1,128,128]{4,1,3,0,2:T(8,128)S(1)}, u32[]{:S(2)}, u32[]{:S(2)}) collective-permute-start(f32[2,8,1,128,128]{4,1,3,0,2:T(8,128)S(1)} %pad_maximum_fusion.4), channel_id=1, source_target_pairs={{0,1},{1,2},{2,3},{3,4},{4,5},{5,6},{6,7},{7,8},{8,9},{9,10},{10,1... | collective-permute-start | bytes 3145736 | tf_op jit(solution)/shard_map/ppermute | solution.py:21
  254.5 25.5 %collective-permute-start.9 = (f32[2,8,1,128,128]{4,1,3,0,2:T(8,128)S(1)}, f32[2,8,1,128,128]{4,1,3,0,2:T(8,128)S(1)}, u32[]{:S(2)}, u32[]{:S(2)}) collective-permute-start(f32[2,8,1,128,128]{4,1,3,0,2:T(8,128)S(1)} %pad_maximum_fusion.4), channel_id=1, source_target_pairs={{1,0},{2,1},{3,2},{4,3},{5,4},{6,5},{7,6},{8,7},{9,8},{10,9},{11,1... | collective-permute-start | bytes 3145736 | tf_op jit(solution)/shard_map/ppermute | solution.py:22
  285.8 40.0 %all-to-all-start.2 = ((f32[2,8,1,128,128]{4,1,0,2,3:T(8,128)}), f32[2,8,1,128,128]{4,1,0,2,3:T(8,128)S(1)}, u32[]{:S(2)}, u32[]{:S(2)}) async-start(f32[2,8,1,128,128]{4,1,0,2,3:T(8,128)} %copy.65), calls=%async_computation.2 | async-start | bytes 2097152 | tf_op jit(solution)/shard_map/all_to_all | solution.py:129
where the time goes:
time: 357 us; the launch traced here: 355 us
  waiting for transfers between devices  175 us (49%)
  starting transfers between devices  68.8 us (19%)
  other arithmetic  67.1 us (19%)
  blocking collectives  25.1 us (7%)
  local copies, waits for them, and re-layouts  11.8 us (3%)
  matrix products  6.53 us (2%)
    ppermute x5, waiting for transfers between devices, with_halo(): after = lax.ppermute(initial, axis, down)  65.2 us
    all_to_all x1, waiting for transfers between devices, local(): lax.all_to_all(local_solved, 'tm', split_axis=3, concat_axis=1, tiled=True)  33.1 us
    all_to_all x1, waiting for transfers between devices, local(): lax.all_to_all(spectrum, 'tm', split_axis=1, concat_axis=3, tiled=True)  33.1 us
    ppermute x5, starting transfers between devices, with_halo(): before = lax.ppermute(last, axis, up)  30.9 us
    all_to_all x1, blocking collectives, local(): lax.all_to_all(combined, 'tm', split_axis=0, concat_axis=2, tiled=True)  25.1 us
    all_to_all x1, waiting for transfers between devices, local(): lax.all_to_all(residual, 'tm', split_axis=2, concat_axis=0, tiled=True)  22.8 us
    ppermute x5, waiting for transfers between devices, with_halo(): before = lax.ppermute(last, axis, up)  20.6 us
    all_to_all x1, starting transfers between devices, local(): lax.all_to_all(residual, 'tm', split_axis=2, concat_axis=0, tiled=True)  15.1 us
  transfers between devices with their start and end apart: 14, of which 11 were waited for; matrix products, arithmetic and copies ran while one was open for 14% of the time, Pallas kernels for 0%

commit v1 on v0

v1 whole, which is shorter than its diff:
```python
import functools
import math

import jax
import jax.numpy as jnp
import numpy as np
from jax import lax
from jax.experimental import pallas as pl
from jax.experimental.pallas import tpu as pltpu
from jax.sharding import Mesh
from jax.sharding import PartitionSpec as P

SWEEPS = 4
ALPHA = 0.1
STEPS = 256
GROUPS = 32
LOCAL = STEPS // GROUPS
NX, NY, NZ = 16, 128, 128
QUARTERS = 4
MEMBERS = GROUPS // QUARTERS
SPAN = NY // QUARTERS
HALO = SWEEPS
WIDE = SPAN + 2 * HALO
WIDE_EACH = WIDE // MEMBERS
EACH = SPAN // MEMBERS
SLOTS = STEPS // 2
CLASSES = 8

AXES = ("yh", "zh", "zl", "core", "yl", "x")
TM = ("yh", "zh", "zl", "core")
SPACE = ("yl", "x")
BLOCK = ("zl", "core", "yl", "x")

VMEM = pl.BlockSpec(memory_space=pltpu.VMEM)
SMEM = pl.BlockSpec(memory_space=pltpu.SMEM)
F32 = jnp.float32


def tables():
    n = np.arange(STEPS, dtype=np.float64)
    k = np.arange(SLOTS, dtype=np.float64)
    ramp = ALPHA ** (n / STEPS)
    angle = 2.0 * np.pi * ((n[None, :] * k[:, None]) % STEPS) / STEPS
    cosine, sine = np.cos(angle), np.sin(angle)
    alternate = np.where(np.arange(STEPS) % 2 == 0, 1.0, -1.0)
    real, imag = cosine.copy(), -sine
    imag[0] = alternate
    forward = np.stack([real, imag], axis=1) * ramp
    forward = forward.reshape(STEPS, STEPS)
    real, imag = 2.0 * cosine, -2.0 * sine
    real[0] = 1.0
    imag[0] = alternate
    back = np.concatenate([real, imag], axis=0) / (ramp * STEPS)
    root = ALPHA ** (1.0 / STEPS)
    base = 2.0 * np.pi * k / STEPS
    first = 1.0 - root * np.cos(base)
    second = first.copy()
    second[0] = 1.0 + root
    turn = root * np.sin(base)
    shift = np.stack([first, second, turn, np.zeros_like(turn)], axis=1)
    return forward.astype(np.float32), back.T.astype(np.float32).copy(), shift.astype(np.float32)


def look_up(classes, kappa_ref, drift_ref):
    kappa = jnp.full(classes.shape, kappa_ref[0], F32)
    flows = [jnp.full(classes.shape, drift_ref[axis, 0], F32) for axis in range(3)]
    for level in range(1, CLASSES):
        match = classes == level
        kappa = jnp.where(match, kappa_ref[level], kappa)
        flows = [jnp.where(match, drift_ref[axis, level], flows[axis]) for axis in range(3)]
    return kappa, [kappa * flow for flow in flows]


def local_terms(masked_ref, forcing_ref, classes_ref, mask_ref, kappa_ref, drift_ref, part_ref, side_ref):
    weight = mask_ref[...].astype(F32)
    kappa, (flow_x, flow_y, flow_z) = look_up(classes_ref[...], kappa_ref, drift_ref)
    row = lax.broadcasted_iota(jnp.int32, (NY, NZ), 0)
    lane = lax.broadcasted_iota(jnp.int32, (NY, NZ), 1)
    side_ref[0] = weight * (kappa - flow_x)
    side_ref[1] = weight * (kappa + flow_x)
    side_ref[2] = weight
    north = jnp.where(row == NY - 1, 0.0, weight * (kappa - flow_y))
    south = jnp.where(row == 0, 0.0, weight * (kappa + flow_y))
    upper = jnp.where(lane == NZ - 1, 0.0, weight * (kappa - flow_z))
    lower = jnp.where(lane == 0, 0.0, weight * (kappa + flow_z))
    middle = 1.0 + 6.0 * kappa
    for n in range(LOCAL):
        here = masked_ref[n]
        total = weight * forcing_ref[n] - middle * here
        total += north * pltpu.roll(here, NY - 1, 0) + south * pltpu.roll(here, 1, 0)
        total += upper * pltpu.roll(here, NZ - 1, 1) + lower * pltpu.roll(here, 1, 1)
        if n:
            total += masked_ref[n - 1]
        part_ref[n] = total


def finish_residual(part_ref, side_ref, east_ref, west_ref, start_ref, arrived_ref, first_ref, residual_ref, sent_ref):
    east, west, weight = side_ref[0], side_ref[1], side_ref[2]
    begins = first_ref[0]
    step_before = weight * jnp.where(begins == 1, start_ref[...], arrived_ref[...])
    for n in range(LOCAL):
        total = part_ref[n] + east * east_ref[n] + west * west_ref[n]
        if n == 0:
            total += step_before
        residual_ref[n] = total
        for quarter in range(QUARTERS):
            low = max(quarter * SPAN - HALO, 0)
            high = min((quarter + 1) * SPAN + HALO, NY)
            at = quarter * WIDE + low - (quarter * SPAN - HALO)
            sent_ref[pl.ds(at * LOCAL + n, high - low, stride=LOCAL), :] = total[low:high]
    outside = jnp.zeros((HALO * LOCAL, NZ), F32)
    sent_ref[0 : HALO * LOCAL, :] = outside
    sent_ref[(QUARTERS * WIDE - HALO) * LOCAL :, :] = outside


def to_frequencies(steps_ref, table_ref, sent_ref):
    fields = [steps_ref[:, row].reshape(STEPS, NZ) for row in range(WIDE_EACH)]
    spectrum = jnp.dot(
        table_ref[...],
        jnp.concatenate(fields, axis=1),
        precision=lax.Precision.HIGHEST,
        preferred_element_type=F32,
    )
    for row in range(WIDE_EACH):
        sent_ref[pl.ds(row, STEPS, stride=WIDE_EACH), :] = spectrum[:, row * NZ : (row + 1) * NZ]


def to_steps(slots_ref, table_ref, sent_ref):
    columns = []
    for row in range(EACH):
        parts = [slots_ref[pl.ds(part * EACH + row, SLOTS, stride=2 * EACH), :] for part in range(2)]
        columns.append(jnp.concatenate(parts, axis=0))
    steps = jnp.dot(
        table_ref[...],
        jnp.concatenate(columns, axis=1),
        precision=lax.Precision.HIGHEST,
        preferred_element_type=F32,
    )
    for row in range(EACH):
        sent_ref[:, row] = steps[:, row * NZ : (row + 1) * NZ].reshape(GROUPS, LOCAL, NZ)


def to_grid(rows_ref, out_ref):
    for n in range(LOCAL):
        out_ref[n] = rows_ref[pl.ds(n, NY, stride=LOCAL), :]


def solve_slot(spectrum_ref, cells_ref, kappa_ref, drift_ref, shift_ref, sent_ref, source, field, coefficient):
    edge = lax.broadcasted_iota(jnp.int32, (NX, NZ), 0)
    lane = lax.broadcasted_iota(jnp.int32, (NX, NZ), 1)
    first, second, turn = shift_ref[0], shift_ref[1], shift_ref[2]
    for member in range(MEMBERS):
        for row in range(WIDE_EACH):
            for part in range(2):
                at = member * NX * 2 * WIDE_EACH + part * WIDE_EACH + row
                source[part, member * WIDE_EACH + row] = spectrum_ref[pl.ds(at, NX, stride=2 * WIDE_EACH), :]

    def prepare(y, carry):
        classes = cells_ref[pl.ds(y, NX, stride=2 * WIDE), :]
        weight = cells_ref[pl.ds(WIDE + y, NX, stride=2 * WIDE), :].astype(F32)
        kappa, (flow_x, flow_y, flow_z) = look_up(classes, kappa_ref, drift_ref)
        coefficient[0, y] = jnp.where(edge == NX - 1, 0.0, kappa - flow_x)
        coefficient[1, y] = jnp.where(edge == 0, 0.0, kappa + flow_x)
        coefficient[2, y] = kappa - flow_y
        coefficient[3, y] = kappa + flow_y
        coefficient[4, y] = jnp.where(lane == NZ - 1, 0.0, kappa - flow_z)
        coefficient[5, y] = jnp.where(lane == 0, 0.0, kappa + flow_z)
        real_first = first + 6.0 * kappa
        real_second = second + 6.0 * kappa
        over_first = weight / (real_first * real_first + turn * turn)
        over_second = weight / (real_second * real_second + turn * turn)
        a, b, c = real_first * over_first, turn * over_first, real_second * over_second
        coefficient[6, y] = a
        coefficient[7, y] = b
        coefficient[8, y] = c
        one, two = source[0, y], source[1, y]
        field[0, 0, y] = a * one + b * two
        field[0, 1, y] = c * two - b * one
        return carry

    lax.fori_loop(0, WIDE, prepare, 0, unroll=2)

    for sweep in range(SWEEPS):
        now, later = sweep % 2, (sweep + 1) % 2

        def row(y, carry):
            totals = []
            for part in range(2):
                here = field[now, part, y]
                total = source[part, y]
                total += coefficient[0, y] * pltpu.roll(here, NX - 1, 0) + coefficient[1, y] * pltpu.roll(here, 1, 0)
                total += coefficient[2, y] * field[now, part, y + 1] + coefficient[3, y] * field[now, part, y - 1]
                total += coefficient[4, y] * pltpu.roll(here, NZ - 1, 1) + coefficient[5, y] * pltpu.roll(here, 1, 1)
                totals.append(total)
            one, two = totals
            a, b, c = coefficient[6, y], coefficient[7, y], coefficient[8, y]
            field[later, 0, y] = a * one + b * two
            field[later, 1, y] = c * two - b * one
            return carry

        lax.fori_loop(sweep + 1, WIDE - 1 - sweep, row, 0, unroll=2)

    for member in range(MEMBERS):
        for row in range(EACH):
            for part in range(2):
                at = member * NX * 2 * EACH + part * EACH + row
                sent_ref[pl.ds(at, NX, stride=2 * EACH), :] = field[SWEEPS % 2, part, HALO + member * EACH + row]


def call(kernel, out_shape, in_specs, scratch=(), flops=1_000_000, moved=2_000_000):
    return pl.pallas_call(
        kernel,
        out_shape=out_shape,
        in_specs=in_specs,
        out_specs=jax.tree.map(lambda _: VMEM, out_shape),
        scratch_shapes=scratch,
        cost_estimate=pl.CostEstimate(flops=flops, bytes_accessed=moved, transcendentals=0),
    )


def shape(*dims):
    return jax.ShapeDtypeStruct(dims, F32)


def exchange(value, axes):
    return lax.all_to_all(value, axes, split_axis=0, concat_axis=0, tiled=True)


def local(iterate, forcing, start_field, classes, open_mask, diffusivity, drift):
    forward, back, shift = tables()
    iterate = iterate.reshape(LOCAL, NY, NZ)
    forcing = forcing.reshape(LOCAL, NY, NZ)
    start_field = start_field.reshape(NY, NZ)
    classes = classes.reshape(NY, NZ)
    open_mask = open_mask.reshape(NY, NZ)

    masked = iterate * open_mask.astype(F32)
    up = [(i, i + 1) for i in range(NX - 1)]
    down = [(j, i) for i, j in up]
    west = lax.ppermute(masked, SPACE, up)
    east = lax.ppermute(masked, SPACE, down)
    arrived = lax.ppermute(masked[LOCAL - 1], TM, [(i, i + 1) for i in range(GROUPS - 1)])

    quarter = lax.axis_index(("yh", "zh"))
    pad = ((HALO, HALO), (0, 0))
    cells = jnp.concatenate(
        [
            lax.dynamic_slice_in_dim(jnp.pad(plane, pad), quarter * SPAN, WIDE, 0)
            for plane in (classes, open_mask)
        ]
    )
    cells = jnp.broadcast_to(cells[None], (NX, 2 * WIDE, NZ)).reshape(NX * 2 * WIDE, NZ)
    cells = exchange(cells, SPACE)

    part, side = call(
        local_terms,
        (shape(LOCAL, NY, NZ), shape(3, NY, NZ)),
        [VMEM] * 4 + [SMEM] * 2,
    )(masked, forcing, classes, open_mask, diffusivity, drift)
    first = (lax.axis_index(TM) == 0).astype(jnp.int32).reshape(1)
    residual, sent = call(
        finish_residual,
        (shape(LOCAL, NY, NZ), shape(QUARTERS * WIDE * LOCAL, NZ)),
        [VMEM] * 6 + [SMEM],
    )(part, side, east, west, start_field, arrived, first)

    steps = exchange(sent, TM).reshape(GROUPS, WIDE_EACH, LOCAL, NZ)
    sent = call(to_frequencies, shape(SLOTS * 2 * WIDE_EACH, NZ), [VMEM] * 2)(steps, jnp.asarray(forward))
    spectrum = exchange(sent, BLOCK)
    mine = lax.dynamic_slice_in_dim(jnp.asarray(shift), lax.axis_index(BLOCK), 1, 0).reshape(4)
    sent = call(
        solve_slot,
        shape(SLOTS * 2 * EACH, NZ),
        [VMEM] * 2 + [SMEM] * 3,
        scratch=[
            pltpu.VMEM((2, WIDE, NX, NZ), F32),
            pltpu.VMEM((2, 2, WIDE, NX, NZ), F32),
            pltpu.VMEM((9, WIDE, NX, NZ), F32),
        ],
    )(spectrum, cells, diffusivity, drift, mine)
    solved = exchange(sent, BLOCK)
    sent = call(to_steps, shape(GROUPS, EACH, LOCAL, NZ), [VMEM] * 2)(solved, jnp.asarray(back))
    rows = exchange(sent.reshape(GROUPS * EACH * LOCAL, NZ), TM)
    corrected = call(to_grid, shape(LOCAL, NY, NZ), [VMEM])(rows)
    grid = (LOCAL, 1, NY, NZ)
    return residual.reshape(grid), corrected.reshape(grid)


def solution(mesh):
    fine = Mesh(mesh.devices.reshape(2, 2, 4, 2, 4, 4), AXES)
    big = P(TM, SPACE, None, None)
    plane = P(SPACE, None, None)
    return jax.shard_map(
        local,
        mesh=fine,
        in_specs=(big, big, plane, plane, plane, P(), P()),
        out_specs=(big, big),
        check_vma=False,
    )
```

time: 357 us -> 202 us (0.57)
  the two profiles are of different devices: /device:TPU:22 before, /device:TPU:8 now
where the time goes in v1:
time: 202 us; the launch traced here: 201 us
  blocking collectives  94.2 us (47%)
  waiting for transfers between devices  54.2 us (27%)
  Pallas kernels  22.5 us (11%)
  starting transfers between devices  20.1 us (10%)
  local copies, waits for them, and re-layouts  7.69 us (4%)
    all_to_all x3, blocking collectives, exchange(): return lax.all_to_all(value, axes, split_axis=0, concat_axis=0, tiled=True)  94.2 us
    all_to_all x2, waiting for transfers between devices, exchange(): return lax.all_to_all(value, axes, split_axis=0, concat_axis=0, tiled=True)  42.8 us
    all_to_all x2, starting transfers between devices, exchange(): return lax.all_to_all(value, axes, split_axis=0, concat_axis=0, tiled=True)  12.1 us
    pallas_call x1, Pallas kernels, local(): call(solve_slot, shape(SLOTS * 2 * EACH, NZ), [VMEM] * 2 + [SMEM] * 3, sc...  9.97 us
    ppermute x1, waiting for transfers between devices, local(): west = lax.ppermute(masked, SPACE, up)  6.22 us
    ppermute x1, waiting for transfers between devices, local(): east = lax.ppermute(masked, SPACE, down)  5.17 us
    ppermute x1, starting transfers between devices, local(): east = lax.ppermute(masked, SPACE, down)  4.55 us
  transfers between devices with their start and end apart: 5, of which 4 were waited for; matrix products, arithmetic and copies ran while one was open for 1% of the time, Pallas kernels for 1%

profile of v1, /device:TPU:8, one launch (start us, length us, event | category | flops | bytes accessed | tf_op | source)
XLA Modules:
  0.0 201.3 jit_solution(831077282323471755)
XLA Ops:
  0.6 0.8 convert_bitcast_fusion
  1.5 1.1 bitcast_multiply_fusion.masked_ref
  2.6 0.0 copy-start.1
  2.6 4.6 %collective-permute-start = (f32[8,128,128]{2,1,0:T(8,128)S(1)}, f32[8,128,128]{2,1,0:T(8,128)S(1)}, u32[]{:S(2)}, u32[]{:S(2)}) collective-permute-start(f32[8,128,128]{2,1,0:T(8,128)S(1)} %bitcast_multiply_fusion.masked_ref), channel_id=1, source_target_pairs={{1,0},{2,1},{3,2},{4,3},{5,4},{6,5},{7,6},{8,7},{9,8},{10,9},{11,1... | collective-permute-start | bytes 1572872 | tf_op jit(solution)/shard_map/ppermute | solution.py:241
  7.1 1.9 collective-permute-start.1
  9.1 1.5 collective-permute-start.2
  10.6 0.0 copy-done.1
  10.6 2.5 %shard_map.113 = (f32[8,128,128]{2,1,0:T(8,128)}, f32[3,128,128]{2,1,0:T(8,128)}) custom-call(f32[8,128,128]{2,1,0:T(8,128)} %copy-done.1, f32[8,128,128]{2,1,0:T(8,128)} %bitcast.35, s32[128,128]{1,0:T(8,128)} %bitcast.37, s32[128,128]{1,0:T(8,128)} %bitcast.33, f32[8]{0:T(128)} %kappa_ref.3, f32[3,8]{1,0:T(4,128)} %drift_ref.3), custom_call_target="tpu_custom_call" | custom-call | flops 1000000 | bytes 2000000 | tf_op jit(solution)/shard_map/pallas_call | solution.py:255
  13.1 0.0 collective-permute-done.2.arrived_ref
  13.1 5.2 %collective-permute-done.east_ref = f32[8,128,128]{2,1,0:T(8,128)S(1)} collective-permute-done((f32[8,128,128]{2,1,0:T(8,128)S(1)}, f32[8,128,128]{2,1,0:T(8,128)S(1)}, u32[]{:S(2)}, u32[]{:S(2)}) %collective-permute-start) | collective-permute-done | bytes 524320 | tf_op jit(solution)/shard_map/ppermute | solution.py:241
  18.3 6.2 %collective-permute-done.1.west_ref = f32[8,128,128]{2,1,0:T(8,128)S(1)} collective-permute-done((f32[8,128,128]{2,1,0:T(8,128)S(1)}, f32[8,128,128]{2,1,0:T(8,128)S(1)}, u32[]{:S(2)}, u32[]{:S(2)}) %collective-permute-start.1) | collective-permute-done | bytes 524320 | tf_op jit(solution)/shard_map/ppermute | solution.py:240
  24.5 0.0 copy-done.6
  24.5 0.8 copy-done.4
  25.3 2.7 %shard_map.114 = (f32[8,128,128]{2,1,0:T(8,128)}, f32[1280,128]{1,0:T(8,128)}) custom-call(f32[8,128,128]{2,1,0:T(8,128)} %get-tuple-element.6.part_ref, f32[3,128,128]{2,1,0:T(8,128)} %get-tuple-element.7.side_ref, f32[8,128,128]{2,1,0:T(8,128)} %copy-done.3, f32[8,128,128]{2,1,0:T(8,128)} %copy-done.4, f32[128,128]{1,0:T(8,128)} %bitcast.39, ...), custom_call_target="tpu_custom_call" | custom-call | flops 1000000 | bytes 2000000 | tf_op jit(solution)/shard_map/pallas_call | solution.py:261
  28.0 41.4 %all_to_all.50 = f32[32,40,128]{2,1,0:T(8,128)} all-to-all(f32[32,40,128]{2,1,0:T(8,128)} %bitcast.32), channel_id=1, replica_groups=mesh['yh'=2,'zh'=2,'zl'=4,'core'=2,'yl'=4,'x'=4] {'yh','zh','zl','core'}, dimensions={0} | all-to-all | bytes 1310720 | tf_op jit(solution)/shard_map/all_to_all | solution.py:226
  69.4 2.8 %shard_map.115 = f32[1280,128]{1,0:T(8,128)} custom-call(f32[32,5,8,128]{3,2,1,0:T(8,128)} %bitcast.27, f32[256,256]{1,0:T(8,128)} %constant.47.clone.table_ref), custom_call_target="tpu_custom_call" | custom-call | flops 1000000 | bytes 2000000 | tf_op jit(solution)/shard_map/pallas_call | solution.py:268
  72.2 2.1 %all_to_all.34 = f32[128,10,128]{2,1,0:T(8,128)} reshape(f32[1280,128]{1,0:T(8,128)} %shard_map.115) | data formatting | bytes 1310720 | tf_op jit(solution)/shard_map/all_to_all | solution.py:226
  74.4 5.9 %all-to-all-start.1 = ((f32[128,10,128]{2,1,0:T(8,128)}), f32[128,10,128]{2,1,0:T(8,128)S(1)}, u32[]{:S(2)}, u32[]{:S(2)}) async-start(f32[128,10,128]{2,1,0:T(8,128)} %all_to_all.34), calls=%async_computation.1 | async-start | bytes 2097152 | tf_op jit(solution)/shard_map/all_to_all | solution.py:226
  80.3 0.0 copy-start.5
  80.3 0.8 copy-done.5
  81.1 27.6 %all-to-all-done.1 = f32[128,10,128]{2,1,0:T(8,128)S(1)} async-done(((f32[128,10,128]{2,1,0:T(8,128)}), f32[128,10,128]{2,1,0:T(8,128)S(1)}, u32[]{:S(2)}, u32[]{:S(2)}) %all-to-all-start.1) | async-done | bytes 655392 | tf_op jit(solution)/shard_map/all_to_all | solution.py:226
  108.8 0.9 broadcast_in_dim.2
  109.7 6.2 %all-to-all-start.2 = ((s32[16,80,128]{2,1,0:T(8,128)}), s32[16,80,128]{2,1,0:T(8,128)S(1)}, u32[]{:S(2)}, u32[]{:S(2)}) async-start(s32[16,80,128]{2,1,0:T(8,128)} %broadcast_in_dim.2), calls=%async_computation.2 | async-start | bytes 1310720 | tf_op jit(solution)/shard_map/all_to_all | solution.py:226
  115.9 1.2 fusion.shift_ref
  117.1 0.9 all_to_all.36.spectrum_ref
  118.0 15.2 %all-to-all-done.2 = s32[16,80,128]{2,1,0:T(8,128)S(1)} async-done(((s32[16,80,128]{2,1,0:T(8,128)}), s32[16,80,128]{2,1,0:T(8,128)S(1)}, u32[]{:S(2)}, u32[]{:S(2)}) %all-to-all-start.2) | async-done | bytes 655392 | tf_op jit(solution)/shard_map/all_to_all | solution.py:226
  133.2 0.9 copy-done
  134.1 10.0 %shard_map.116 = f32[1024,128]{1,0:T(8,128)} custom-call(f32[1280,128]{1,0:T(8,128)} %all_to_all.36.spectrum_ref, s32[1280,128]{1,0:T(8,128)} %bitcast.26, f32[8]{0:T(128)} %kappa_ref.3, f32[3,8]{1,0:T(4,128)} %drift_ref.3, f32[4]{0:T(128)} %fusion.shift_ref), custom_call_target="tpu_custom_call" | custom-call | flops 1000000 | bytes 2000000 | tf_op jit(solution)/shard_map/pallas_call | solution.py:271
  144.0 24.6 %all_to_all.51 = f32[128,8,128]{2,1,0:T(8,128)} all-to-all(f32[128,8,128]{2,1,0:T(8,128)} %bitcast.31), channel_id=1, replica_groups=mesh['yh'=2,'zh'=2,'zl'=4,'core'=2,'yl'=4,'x'=4] {'zl','core','yl','x'}, dimensions={0} | all-to-all | bytes 1048576 | tf_op jit(solution)/shard_map/all_to_all | solution.py:226
  168.6 2.6 %shard_map.117 = f32[32,4,8,128]{3,2,1,0:T(8,128)} custom-call(f32[1024,128]{1,0:T(8,128)} %bitcast.28, f32[256,256]{1,0:T(8,128)} %constant.49.clone.table_ref), custom_call_target="tpu_custom_call" | custom-call | flops 1000000 | bytes 2000000 | tf_op jit(solution)/shard_map/pallas_call | solution.py:282
  171.2 28.2 %all_to_all.52 = f32[32,32,128]{2,1,0:T(8,128)} all-to-all(f32[32,32,128]{2,1,0:T(8,128)} %bitcast.29), channel_id=1, replica_groups=mesh['yh'=2,'zh'=2,'zl'=4,'core'=2,'yl'=4,'x'=4] {'yh','zh','zl','core'}, dimensions={0} | all-to-all | bytes 1048576 | tf_op jit(solution)/shard_map/all_to_all | solution.py:226
  199.4 1.9 shard_map.118
  (11 shorter events, 0.1 us)
Async XLA Ops:
  2.6 8.0 %copy-start.1 = (f32[8,128,128]{2,1,0:T(8,128)}, f32[8,128,128]{2,1,0:T(8,128)S(1)}, u32[]{:S(2)}) copy-start(f32[8,128,128]{2,1,0:T(8,128)S(1)} %bitcast_multiply_fusion.masked_ref) | copy-start | bytes 1572868
  2.6 15.7 %collective-permute-start = (f32[8,128,128]{2,1,0:T(8,128)S(1)}, f32[8,128,128]{2,1,0:T(8,128)S(1)}, u32[]{:S(2)}, u32[]{:S(2)}) collective-permute-start(f32[8,128,128]{2,1,0:T(8,128)S(1)} %bitcast_multiply_fusion.masked_ref), channel_id=1, source_target_pairs={{1,0},{2,1},{3,2},{4,3},{5,4},{6,5},{7,6},{8,7},{9,8},{10,9},{11,1... | collective-permute-start | bytes 1572872 | tf_op jit(solution)/shard_map/ppermute | solution.py:241
  7.1 17.4 %collective-permute-start.1 = (f32[8,128,128]{2,1,0:T(8,128)S(1)}, f32[8,128,128]{2,1,0:T(8,128)S(1)}, u32[]{:S(2)}, u32[]{:S(2)}) collective-permute-start(f32[8,128,128]{2,1,0:T(8,128)S(1)} %bitcast_multiply_fusion.masked_ref), channel_id=1, source_target_pairs={{0,1},{1,2},{2,3},{3,4},{4,5},{5,6},{6,7},{7,8},{8,9},{9,10},{10,1... | collective-permute-start | bytes 1572872 | tf_op jit(solution)/shard_map/ppermute | solution.py:240
  9.1 4.0 %collective-permute-start.2 = (f32[128,128]{1,0:T(8,128)S(1)}, f32[128,128]{1,0:T(8,128)S(1)}, u32[]{:S(2)}, u32[]{:S(2)}) collective-permute-start(f32[128,128]{1,0:T(8,128)S(1)} %slice_bitcast_fusion), channel_id=1, source_target_pairs={{0,16},{16,32},{32,48},{48,64},{64,80},{80,96},{96,112},{112,128},... | collective-permute-start | bytes 196616 | tf_op jit(solution)/shard_map/ppermute | solution.py:242
  13.1 11.4 %copy-start.6 = (f32[128,128]{1,0:T(8,128)}, f32[128,128]{1,0:T(8,128)S(1)}, u32[]{:S(2)}) copy-start(f32[128,128]{1,0:T(8,128)S(1)} %collective-permute-done.2.arrived_ref) | copy-start | bytes 196612
  18.3 6.2 %copy-start.3 = (f32[8,128,128]{2,1,0:T(8,128)}, f32[8,128,128]{2,1,0:T(8,128)S(1)}, u32[]{:S(2)}) copy-start(f32[8,128,128]{2,1,0:T(8,128)S(1)} %collective-permute-done.east_ref) | copy-start | bytes 1572868
  24.5 0.8 copy-start.4
  74.4 5.9 %copy-start.2 = (s32[1,128,128]{2,1,0:T(8,128)S(1)}, s32[1,128,128]{2,1,0:T(8,128)}, u32[]{:S(2)}) copy-start(s32[1,128,128]{2,1,0:T(8,128)} %param.14) | copy-start | bytes 196612
  74.4 34.4 %all-to-all-start.1 = ((f32[128,10,128]{2,1,0:T(8,128)}), f32[128,10,128]{2,1,0:T(8,128)S(1)}, u32[]{:S(2)}, u32[]{:S(2)}) async-start(f32[128,10,128]{2,1,0:T(8,128)} %all_to_all.34), calls=%async_computation.1 | async-start | bytes 2097152 | tf_op jit(solution)/shard_map/all_to_all | solution.py:226
  80.3 0.8 copy-start.5
  109.7 23.5 %all-to-all-start.2 = ((s32[16,80,128]{2,1,0:T(8,128)}), s32[16,80,128]{2,1,0:T(8,128)S(1)}, u32[]{:S(2)}, u32[]{:S(2)}) async-start(s32[16,80,128]{2,1,0:T(8,128)} %broadcast_in_dim.2), calls=%async_computation.2 | async-start | bytes 1310720 | tf_op jit(solution)/shard_map/all_to_all | solution.py:226
  133.2 0.9 copy-start

commit v2 on v1

--- a/solution.py
+++ b/solution.py
@@ -25,12 +25,15 @@
 EACH = SPAN // MEMBERS
 SLOTS = STEPS // 2
 CLASSES = 8
+SOLID = CLASSES
+SENT = 16
 
 AXES = ("yh", "zh", "zl", "core", "yl", "x")
 TM = ("yh", "zh", "zl", "core")
 SPACE = ("yl", "x")
 BLOCK = ("zl", "core", "yl", "x")
 
+GRANT = 24 << 20
 VMEM = pl.BlockSpec(memory_space=pltpu.VMEM)
 SMEM = pl.BlockSpec(memory_space=pltpu.SMEM)
 F32 = jnp.float32
@@ -45,8 +48,7 @@
     alternate = np.where(np.arange(STEPS) % 2 == 0, 1.0, -1.0)
     real, imag = cosine.copy(), -sine
     imag[0] = alternate
-    forward = np.stack([real, imag], axis=1) * ramp
-    forward = forward.reshape(STEPS, STEPS)
+    forward = np.concatenate([real, imag], axis=0) * ramp
     real, imag = 2.0 * cosine, -2.0 * sine
     real[0] = 1.0
     imag[0] = alternate
@@ -113,7 +115,7 @@
     sent_ref[(QUARTERS * WIDE - HALO) * LOCAL :, :] = outside
 
 
-def to_frequencies(steps_ref, table_ref, sent_ref):
+def to_frequencies(steps_ref, cells_ref, table_ref, sent_ref):
     fields = [steps_ref[:, row].reshape(STEPS, NZ) for row in range(WIDE_EACH)]
     spectrum = jnp.dot(
         table_ref[...],
@@ -122,7 +124,14 @@
         preferred_element_type=F32,
     )
     for row in range(WIDE_EACH):
-        sent_ref[pl.ds(row, STEPS, stride=WIDE_EACH), :] = spectrum[:, row * NZ : (row + 1) * NZ]
+        columns = spectrum[:, row * NZ : (row + 1) * NZ]
+        for part in range(2):
+            rows = columns[part * SLOTS : (part + 1) * SLOTS]
+            sent_ref[pl.ds(part * WIDE_EACH + row, SLOTS, stride=SENT), :] = rows
+        cells = jnp.broadcast_to(cells_ref[row : row + 1, :], (SLOTS, NZ))
+        sent_ref[pl.ds(2 * WIDE_EACH + row, SLOTS, stride=SENT), :] = cells
+    for row in range(3 * WIDE_EACH, SENT):
+        sent_ref[pl.ds(row, SLOTS, stride=SENT), :] = jnp.zeros((SLOTS, NZ), F32)
 
 
 def to_steps(slots_ref, table_ref, sent_ref):
@@ -145,19 +154,20 @@
         out_ref[n] = rows_ref[pl.ds(n, NY, stride=LOCAL), :]
 
 
-def solve_slot(spectrum_ref, cells_ref, kappa_ref, drift_ref, shift_ref, sent_ref, source, field, coefficient):
+def solve_slot(spectrum_ref, kappa_ref, drift_ref, shift_ref, sent_ref, source, cells, field, coefficient):
     edge = lax.broadcasted_iota(jnp.int32, (NX, NZ), 0)
     lane = lax.broadcasted_iota(jnp.int32, (NX, NZ), 1)
     first, second, turn = shift_ref[0], shift_ref[1], shift_ref[2]
     for member in range(MEMBERS):
         for row in range(WIDE_EACH):
+            at = member * NX * SENT + row
             for part in range(2):
-                at = member * NX * 2 * WIDE_EACH + part * WIDE_EACH + row
-                source[part, member * WIDE_EACH + row] = spectrum_ref[pl.ds(at, NX, stride=2 * WIDE_EACH), :]
+                source[part, member * WIDE_EACH + row] = spectrum_ref[pl.ds(at + part * WIDE_EACH, NX, stride=SENT), :]
+            cells[member * WIDE_EACH + row] = spectrum_ref[pl.ds(at + 2 * WIDE_EACH, NX, stride=SENT), :]
 
     def prepare(y, carry):
-        classes = cells_ref[pl.ds(y, NX, stride=2 * WIDE), :]
-        weight = cells_ref[pl.ds(WIDE + y, NX, stride=2 * WIDE), :].astype(F32)
+        classes = cells[y].astype(jnp.int32)
+        weight = jnp.where(classes == SOLID, 0.0, 1.0)
         kappa, (flow_x, flow_y, flow_z) = look_up(classes, kappa_ref, drift_ref)
         coefficient[0, y] = jnp.where(edge == NX - 1, 0.0, kappa - flow_x)
         coefficient[1, y] = jnp.where(edge == 0, 0.0, kappa + flow_x)
@@ -215,6 +225,7 @@
         out_specs=jax.tree.map(lambda _: VMEM, out_shape),
         scratch_shapes=scratch,
         cost_estimate=pl.CostEstimate(flops=flops, bytes_accessed=moved, transcendentals=0),
+        compiler_params=pltpu.CompilerParams(vmem_limit_bytes=GRANT),
     )
 
 
@@ -241,16 +252,9 @@
     east = lax.ppermute(masked, SPACE, down)
     arrived = lax.ppermute(masked[LOCAL - 1], TM, [(i, i + 1) for i in range(GROUPS - 1)])
 
-    quarter = lax.axis_index(("yh", "zh"))
-    pad = ((HALO, HALO), (0, 0))
-    cells = jnp.concatenate(
-        [
-            lax.dynamic_slice_in_dim(jnp.pad(plane, pad), quarter * SPAN, WIDE, 0)
-            for plane in (classes, open_mask)
-        ]
-    )
-    cells = jnp.broadcast_to(cells[None], (NX, 2 * WIDE, NZ)).reshape(NX * 2 * WIDE, NZ)
-    cells = exchange(cells, SPACE)
+    cells = jnp.pad(jnp.where(open_mask == 1, classes, SOLID), ((HALO, HALO), (0, 0)), constant_values=SOLID)
+    row = lax.axis_index(("yh", "zh")) * SPAN + lax.axis_index(("zl", "core")) * WIDE_EACH
+    cells = lax.dynamic_slice_in_dim(cells, row, WIDE_EACH, 0).astype(F32)
 
     part, side = call(
         local_terms,
@@ -265,19 +269,20 @@
     )(part, side, east, west, start_field, arrived, first)
 
     steps = exchange(sent, TM).reshape(GROUPS, WIDE_EACH, LOCAL, NZ)
-    sent = call(to_frequencies, shape(SLOTS * 2 * WIDE_EACH, NZ), [VMEM] * 2)(steps, jnp.asarray(forward))
+    sent = call(to_frequencies, shape(SLOTS * SENT, NZ), [VMEM] * 3)(steps, cells, jnp.asarray(forward))
     spectrum = exchange(sent, BLOCK)
     mine = lax.dynamic_slice_in_dim(jnp.asarray(shift), lax.axis_index(BLOCK), 1, 0).reshape(4)
     sent = call(
         solve_slot,
         shape(SLOTS * 2 * EACH, NZ),
-        [VMEM] * 2 + [SMEM] * 3,
+        [VMEM] + [SMEM] * 3,
         scratch=[
             pltpu.VMEM((2, WIDE, NX, NZ), F32),
+            pltpu.VMEM((WIDE, NX, NZ), F32),
             pltpu.VMEM((2, 2, WIDE, NX, NZ), F32),
             pltpu.VMEM((9, WIDE, NX, NZ), F32),
         ],
-    )(spectrum, cells, diffusivity, drift, mine)
+    )(spectrum, diffusivity, drift, mine)
     solved = exchange(sent, BLOCK)
     sent = call(to_steps, shape(GROUPS, EACH, LOCAL, NZ), [VMEM] * 2)(solved, jnp.asarray(back))
     rows = exchange(sent.reshape(GROUPS * EACH * LOCAL, NZ), TM)

time: 202 us -> 167 us (0.83)
  blocking collectives: 94.2 us -> 53.2 us
  starting transfers between devices: 20.1 us -> 30.5 us
  waiting for transfers between devices: 54.2 us -> 64.5 us
  Pallas kernels: 22.5 us -> 14.5 us
  local copies, waits for them, and re-layouts: 7.69 us -> 1.38 us
    all_to_all x3 -> x2, blocking collectives: 94.2 us -> 53.2 us  [exchange(): return lax.all_to_all(value, axes, split_axis=0, concat_axis=0, tiled=True)]
    all_to_all x2, starting transfers between devices: 12.1 us -> 22.4 us  [exchange(): return lax.all_to_all(value, axes, split_axis=0, concat_axis=0, tiled=True)]
    all_to_all x2, waiting for transfers between devices: 42.8 us -> 52.4 us  [exchange(): return lax.all_to_all(value, axes, split_axis=0, concat_axis=0, tiled=True)]
    all_to_all x2 -> x0, local copies, waits for them, and re-layouts: 3.05 us -> none  [exchange(): return lax.all_to_all(value, axes, split_axis=0, concat_axis=0, tiled=True)]
    pallas_call x2, Pallas kernels: 12.8 us -> 10.6 us  [the longest x1 8.62 us: local(): call(solve_slot, shape(SLOTS * 2 * EACH, NZ), [VMEM] + [SMEM] * 3, scratc...]
  transfers between devices with their start and end apart: 5 -> 5, of which waited for: 4 -> 4; matrix products, arithmetic and copies ran while one was open for 1% -> 0% of each run, Pallas kernels for 1% -> 1%
where the time goes in v2:
time: 167 us
  waiting for transfers between devices  64.5 us (39%)
  blocking collectives  53.2 us (32%)
  starting transfers between devices  30.5 us (18%)
  Pallas kernels  14.5 us (9%)
  other arithmetic  2.01 us (1%)
    all_to_all x2, blocking collectives, exchange(): return lax.all_to_all(value, axes, split_axis=0, concat_axis=0, tiled=True)  53.2 us
    all_to_all x2, waiting for transfers between devices, exchange(): return lax.all_to_all(value, axes, split_axis=0, concat_axis=0, tiled=True)  52.4 us
    all_to_all x2, starting transfers between devices, exchange(): return lax.all_to_all(value, axes, split_axis=0, concat_axis=0, tiled=True)  22.4 us
    pallas_call x1, Pallas kernels, local(): call(solve_slot, shape(SLOTS * 2 * EACH, NZ), [VMEM] + [SMEM] * 3, scratc...  8.62 us
    ppermute x1, waiting for transfers between devices, local(): west = lax.ppermute(masked, SPACE, up)  6.23 us
    ppermute x1, waiting for transfers between devices, local(): east = lax.ppermute(masked, SPACE, down)  5.95 us
    ppermute x1, starting transfers between devices, local(): east = lax.ppermute(masked, SPACE, down)  4.68 us
  transfers between devices with their start and end apart: 5, of which 4 were waited for; matrix products, arithmetic and copies ran while one was open for 0% of the time, Pallas kernels for 1%

profile of v2, /device:TPU:8, one launch (start us, length us, event | category | flops | bytes accessed | tf_op | source)
XLA Modules:
  0.0 166.9 jit_solution(7056432072817909568)
XLA Ops:
  0.6 0.8 convert_bitcast_fusion
  1.5 1.1 bitcast_multiply_fusion.masked_ref
  2.6 0.0 copy-start
  2.6 0.0 copy-start.4
  2.6 4.7 %collective-permute-start = (f32[8,128,128]{2,1,0:T(8,128)S(1)}, f32[8,128,128]{2,1,0:T(8,128)S(1)}, u32[]{:S(2)}, u32[]{:S(2)}) collective-permute-start(f32[8,128,128]{2,1,0:T(8,128)S(1)} %bitcast_multiply_fusion.masked_ref), channel_id=1, source_target_pairs={{1,0},{2,1},{3,2},{4,3},{5,4},{6,5},{7,6},{8,7},{9,8},{10,9},{11,1... | collective-permute-start | bytes 1572872 | tf_op jit(solution)/shard_map/ppermute | solution.py:252
  7.3 1.9 %collective-permute-start.1 = (f32[8,128,128]{2,1,0:T(8,128)S(1)}, f32[8,128,128]{2,1,0:T(8,128)S(1)}, u32[]{:S(2)}, u32[]{:S(2)}) collective-permute-start(f32[8,128,128]{2,1,0:T(8,128)S(1)} %bitcast_multiply_fusion.masked_ref), channel_id=1, source_target_pairs={{0,1},{1,2},{2,3},{3,4},{4,5},{5,6},{6,7},{7,8},{8,9},{9,10},{10,1... | collective-permute-start | bytes 1572872 | tf_op jit(solution)/shard_map/ppermute | solution.py:251
  9.3 1.5 collective-permute-start.2
  10.8 0.0 copy-start.6
  10.8 0.0 copy-start.7
  10.8 0.0 copy-done.1
  10.8 0.0 copy-done
  10.8 0.6 copy-done.6
  11.5 1.1 shard_map.113
  12.5 0.0 collective-permute-done.2.arrived_ref
  12.5 5.9 %collective-permute-done.east_ref = f32[8,128,128]{2,1,0:T(8,128)S(1)} collective-permute-done((f32[8,128,128]{2,1,0:T(8,128)S(1)}, f32[8,128,128]{2,1,0:T(8,128)S(1)}, u32[]{:S(2)}, u32[]{:S(2)}) %collective-permute-start) | collective-permute-done | bytes 524320 | tf_op jit(solution)/shard_map/ppermute | solution.py:252
  18.5 6.2 %collective-permute-done.1.west_ref = f32[8,128,128]{2,1,0:T(8,128)S(1)} collective-permute-done((f32[8,128,128]{2,1,0:T(8,128)S(1)}, f32[8,128,128]{2,1,0:T(8,128)S(1)}, u32[]{:S(2)}, u32[]{:S(2)}) %collective-permute-start.1) | collective-permute-done | bytes 524320 | tf_op jit(solution)/shard_map/ppermute | solution.py:251
  24.7 0.0 copy-done.5
  24.7 1.3 shard_map.114
  26.0 16.7 %all-to-all-start = ((f32[32,40,128]{2,1,0:T(8,128)}), f32[32,40,128]{2,1,0:T(8,128)S(1)}, u32[]{:S(2)}, u32[]{:S(2)}) async-start(f32[32,40,128]{2,1,0:T(8,128)} %bitcast.10), calls=%async_computation | async-start | bytes 1310720 | tf_op jit(solution)/shard_map/all_to_all | solution.py:237
  42.7 0.0 copy-start.3
  42.7 24.6 %all-to-all-done = f32[32,40,128]{2,1,0:T(8,128)S(1)} async-done(((f32[32,40,128]{2,1,0:T(8,128)}), f32[32,40,128]{2,1,0:T(8,128)S(1)}, u32[]{:S(2)}, u32[]{:S(2)}) %all-to-all-start) | async-done | bytes 655392 | tf_op jit(solution)/shard_map/all_to_all | solution.py:237
  67.3 1.9 %shard_map.115 = f32[2048,128]{1,0:T(8,128)} custom-call(f32[32,5,8,128]{3,2,1,0:T(8,128)S(1)} %bitcast.30, f32[5,128]{1,0:T(8,128)S(1)} %fusion.cells_ref, f32[256,256]{1,0:T(8,128)S(1)} %copy-done.3), custom_call_target="tpu_custom_call" | custom-call | flops 1000000 | bytes 2000000 | tf_op jit(solution)/shard_map/pallas_call | solution.py:272
  69.2 5.8 %all-to-all-start.1 = ((f32[128,16,128]{2,1,0:T(8,128)}), f32[128,16,128]{2,1,0:T(8,128)S(1)}, u32[]{:S(2)}, u32[]{:S(2)}) async-start(f32[128,16,128]{2,1,0:T(8,128)} %bitcast.12), calls=%async_computation.1 | async-start | bytes 2097152 | tf_op jit(solution)/shard_map/all_to_all | solution.py:237
  75.0 0.7 dynamic-slice_bitcast_fusion.shift_ref
  75.7 27.8 %all-to-all-done.1 = f32[128,16,128]{2,1,0:T(8,128)S(1)} async-done(((f32[128,16,128]{2,1,0:T(8,128)}), f32[128,16,128]{2,1,0:T(8,128)S(1)}, u32[]{:S(2)}, u32[]{:S(2)}) %all-to-all-start.1) | async-done | bytes 1048608 | tf_op jit(solution)/shard_map/all_to_all | solution.py:237
  103.5 8.6 %shard_map.116 = f32[1024,128]{1,0:T(8,128)S(1)} custom-call(f32[2048,128]{1,0:T(8,128)S(1)} %bitcast.29, f32[8]{0:T(128)S(1)} %copy-done.7, f32[3,8]{1,0:T(4,128)S(1)} %copy-done.6, f32[4]{0:T(128)S(1)} %dynamic-slice_bitcast_fusion.shift_ref), custom_call_target="tpu_custom_call" | custom-call | flops 1000000 | bytes 2000000 | tf_op jit(solution)/shard_map/pallas_call | solution.py:275
  112.1 0.0 copy-start.2
  112.1 25.3 %all_to_all.42 = f32[128,8,128]{2,1,0:T(8,128)S(1)} all-to-all(f32[128,8,128]{2,1,0:T(8,128)S(1)} %bitcast.31), channel_id=1, replica_groups=mesh['yh'=2,'zh'=2,'zl'=4,'core'=2,'yl'=4,'x'=4] {'zl','core','yl','x'}, dimensions={0} | all-to-all | bytes 1048576 | tf_op jit(solution)/shard_map/all_to_all | solution.py:237
  137.5 0.0 copy-done.2
  137.5 0.7 shard_map.117
  138.2 27.9 %all_to_all.43 = f32[32,32,128]{2,1,0:T(8,128)S(1)} all-to-all(f32[32,32,128]{2,1,0:T(8,128)S(1)} %bitcast.33), channel_id=1, replica_groups=mesh['yh'=2,'zh'=2,'zl'=4,'core'=2,'yl'=4,'x'=4] {'yh','zh','zl','core'}, dimensions={0} | all-to-all | bytes 1048576 | tf_op jit(solution)/shard_map/all_to_all | solution.py:237
  166.0 0.9 shard_map.118
  (8 shorter events, 0.0 us)
Async XLA Ops:
  1.5 9.3 %copy-start.1 = (f32[8,1,128,128]{3,2,1,0:T(8,128)S(1)}, f32[8,1,128,128]{3,2,1,0:T(8,128)}, u32[]{:S(2)}) copy-start(f32[8,1,128,128]{3,2,1,0:T(8,128)} %param.11) | copy-start | bytes 1572868
  2.6 8.2 %copy-start = (s32[1,128,128]{2,1,0:T(8,128)S(1)}, s32[1,128,128]{2,1,0:T(8,128)}, u32[]{:S(2)}) copy-start(s32[1,128,128]{2,1,0:T(8,128)} %param.14) | copy-start | bytes 196612
  2.6 8.2 %copy-start.4 = (s32[1,128,128]{2,1,0:T(8,128)S(1)}, s32[1,128,128]{2,1,0:T(8,128)}, u32[]{:S(2)}) copy-start(s32[1,128,128]{2,1,0:T(8,128)} %param.13) | copy-start | bytes 196612
  2.6 15.9 %collective-permute-start = (f32[8,128,128]{2,1,0:T(8,128)S(1)}, f32[8,128,128]{2,1,0:T(8,128)S(1)}, u32[]{:S(2)}, u32[]{:S(2)}) collective-permute-start(f32[8,128,128]{2,1,0:T(8,128)S(1)} %bitcast_multiply_fusion.masked_ref), channel_id=1, source_target_pairs={{1,0},{2,1},{3,2},{4,3},{5,4},{6,5},{7,6},{8,7},{9,8},{10,9},{11,1... | collective-permute-start | bytes 1572872 | tf_op jit(solution)/shard_map/ppermute | solution.py:252
  7.3 17.4 %collective-permute-start.1 = (f32[8,128,128]{2,1,0:T(8,128)S(1)}, f32[8,128,128]{2,1,0:T(8,128)S(1)}, u32[]{:S(2)}, u32[]{:S(2)}) collective-permute-start(f32[8,128,128]{2,1,0:T(8,128)S(1)} %bitcast_multiply_fusion.masked_ref), channel_id=1, source_target_pairs={{0,1},{1,2},{2,3},{3,4},{4,5},{5,6},{6,7},{7,8},{8,9},{9,10},{10,1... | collective-permute-start | bytes 1572872 | tf_op jit(solution)/shard_map/ppermute | solution.py:251
  9.3 3.3 %collective-permute-start.2 = (f32[128,128]{1,0:T(8,128)S(1)}, f32[128,128]{1,0:T(8,128)S(1)}, u32[]{:S(2)}, u32[]{:S(2)}) collective-permute-start(f32[128,128]{1,0:T(8,128)S(1)} %slice_bitcast_fusion), channel_id=1, source_target_pairs={{0,16},{16,32},{32,48},{48,64},{64,80},{80,96},{96,112},{112,128},... | collective-permute-start | bytes 196616 | tf_op jit(solution)/shard_map/ppermute | solution.py:253
  10.8 0.7 copy-start.6
  10.8 0.7 copy-start.7
  11.5 13.3 %copy-start.5 = (f32[1,128,128]{2,1,0:T(8,128)S(1)}, f32[1,128,128]{2,1,0:T(8,128)}, u32[]{:S(2)}) copy-start(f32[1,128,128]{2,1,0:T(8,128)} %param.12) | copy-start | bytes 196612
  26.0 41.3 %all-to-all-start = ((f32[32,40,128]{2,1,0:T(8,128)}), f32[32,40,128]{2,1,0:T(8,128)S(1)}, u32[]{:S(2)}, u32[]{:S(2)}) async-start(f32[32,40,128]{2,1,0:T(8,128)} %bitcast.10), calls=%async_computation | async-start | bytes 1310720 | tf_op jit(solution)/shard_map/all_to_all | solution.py:237
  42.7 24.6 %copy-start.3 = (f32[256,256]{1,0:T(8,128)S(1)}, f32[256,256]{1,0:T(8,128)}, u32[]{:S(2)}) copy-start(f32[256,256]{1,0:T(8,128)} %constant.51.clone.table_ref) | copy-start | bytes 786436
  69.2 34.3 %all-to-all-start.1 = ((f32[128,16,128]{2,1,0:T(8,128)}), f32[128,16,128]{2,1,0:T(8,128)S(1)}, u32[]{:S(2)}, u32[]{:S(2)}) async-start(f32[128,16,128]{2,1,0:T(8,128)} %bitcast.12), calls=%async_computation.1 | async-start | bytes 2097152 | tf_op jit(solution)/shard_map/all_to_all | solution.py:237
  112.1 25.4 %copy-start.2 = (f32[256,256]{1,0:T(8,128)S(1)}, f32[256,256]{1,0:T(8,128)}, u32[]{:S(2)}) copy-start(f32[256,256]{1,0:T(8,128)} %constant.53.clone.table_ref) | copy-start | bytes 786436

commit v3 on v2

--- a/solution.py
+++ b/solution.py
@@ -1,6 +1,3 @@
-import functools
-import math
-
 import jax
 import jax.numpy as jnp
 import numpy as np
@@ -9,6 +6,7 @@
 from jax.experimental.pallas import tpu as pltpu
 from jax.sharding import Mesh
 from jax.sharding import PartitionSpec as P
+
 
 SWEEPS = 4
 ALPHA = 0.1
@@ -26,7 +24,6 @@
 SLOTS = STEPS // 2
 CLASSES = 8
 SOLID = CLASSES
-SENT = 16
 
 AXES = ("yh", "zh", "zl", "core", "yl", "x")
 TM = ("yh", "zh", "zl", "core")
@@ -115,7 +112,7 @@
     sent_ref[(QUARTERS * WIDE - HALO) * LOCAL :, :] = outside
 
 
-def to_frequencies(steps_ref, cells_ref, table_ref, sent_ref):
+def to_frequencies(steps_ref, table_ref, sent_ref):
     fields = [steps_ref[:, row].reshape(STEPS, NZ) for row in range(WIDE_EACH)]
     spectrum = jnp.dot(
         table_ref[...],
@@ -127,11 +124,7 @@
         columns = spectrum[:, row * NZ : (row + 1) * NZ]
         for part in range(2):
             rows = columns[part * SLOTS : (part + 1) * SLOTS]
-            sent_ref[pl.ds(part * WIDE_EACH + row, SLOTS, stride=SENT), :] = rows
-        cells = jnp.broadcast_to(cells_ref[row : row + 1, :], (SLOTS, NZ))
-        sent_ref[pl.ds(2 * WIDE_EACH + row, SLOTS, stride=SENT), :] = cells
-    for row in range(3 * WIDE_EACH, SENT):
-        sent_ref[pl.ds(row, SLOTS, stride=SENT), :] = jnp.zeros((SLOTS, NZ), F32)
+            sent_ref[pl.ds(part * WIDE_EACH + row, SLOTS, stride=2 * WIDE_EACH), :] = rows
 
 
 def to_steps(slots_ref, table_ref, sent_ref):
@@ -154,19 +147,19 @@
         out_ref[n] = rows_ref[pl.ds(n, NY, stride=LOCAL), :]
 
 
-def solve_slot(spectrum_ref, kappa_ref, drift_ref, shift_ref, sent_ref, source, cells, field, coefficient):
+def solve_slot(spectrum_ref, cells_ref, kappa_ref, drift_ref, shift_ref, sent_ref, source, field, coefficient):
     edge = lax.broadcasted_iota(jnp.int32, (NX, NZ), 0)
     lane = lax.broadcasted_iota(jnp.int32, (NX, NZ), 1)
     first, second, turn = shift_ref[0], shift_ref[1], shift_ref[2]
     for member in range(MEMBERS):
         for row in range(WIDE_EACH):
-            at = member * NX * SENT + row
+            at = member * NX * 2 * WIDE_EACH + row
             for part in range(2):
-                source[part, member * WIDE_EACH + row] = spectrum_ref[pl.ds(at + part * WIDE_EACH, NX, stride=SENT), :]
-            cells[member * WIDE_EACH + row] = spectrum_ref[pl.ds(at + 2 * WIDE_EACH, NX, stride=SENT), :]
+                rows = pl.ds(at + part * WIDE_EACH, NX, stride=2 * WIDE_EACH)
+                source[part, member * WIDE_EACH + row] = spectrum_ref[rows, :]
 
     def prepare(y, carry):
-        classes = cells[y].astype(jnp.int32)
+        classes = cells_ref[pl.ds(y, NX, stride=WIDE), :]
         weight = jnp.where(classes == SOLID, 0.0, 1.0)
         kappa, (flow_x, flow_y, flow_z) = look_up(classes, kappa_ref, drift_ref)
         coefficient[0, y] = jnp.where(edge == NX - 1, 0.0, kappa - flow_x)
@@ -253,8 +246,14 @@
     arrived = lax.ppermute(masked[LOCAL - 1], TM, [(i, i + 1) for i in range(GROUPS - 1)])
 
     cells = jnp.pad(jnp.where(open_mask == 1, classes, SOLID), ((HALO, HALO), (0, 0)), constant_values=SOLID)
-    row = lax.axis_index(("yh", "zh")) * SPAN + lax.axis_index(("zl", "core")) * WIDE_EACH
-    cells = lax.dynamic_slice_in_dim(cells, row, WIDE_EACH, 0).astype(F32)
+    cells = lax.dynamic_slice_in_dim(cells, lax.axis_index(("yh", "zh")) * SPAN, WIDE, 0)
+    cells = cells.reshape(1, 1, WIDE, NZ)
+    for axis, dim, bit in (("yl", 0, 1), ("yl", 0, 2), ("x", 1, 1), ("x", 1, 2)):
+        other = lax.ppermute(cells, axis, [(i, i ^ bit) for i in range(4)])
+        upper = (lax.axis_index(axis) & bit) != 0
+        pair = [jnp.where(upper, other, cells), jnp.where(upper, cells, other)]
+        cells = jnp.concatenate(pair, axis=dim)
+    cells = cells.reshape(NX * WIDE, NZ)
 
     part, side = call(
         local_terms,
@@ -269,20 +268,19 @@
     )(part, side, east, west, start_field, arrived, first)
 
     steps = exchange(sent, TM).reshape(GROUPS, WIDE_EACH, LOCAL, NZ)
-    sent = call(to_frequencies, shape(SLOTS * SENT, NZ), [VMEM] * 3)(steps, cells, jnp.asarray(forward))
-    spectrum = exchange(sent, BLOCK)
+    sent = call(to_frequencies, shape(SLOTS * 2 * WIDE_EACH, NZ), [VMEM] * 2)(steps, jnp.asarray(forward))
+    spectrum = exchange(sent.reshape(SLOTS, 1, 2 * WIDE_EACH * NZ), BLOCK).reshape(SLOTS * 2 * WIDE_EACH, NZ)
     mine = lax.dynamic_slice_in_dim(jnp.asarray(shift), lax.axis_index(BLOCK), 1, 0).reshape(4)
     sent = call(
         solve_slot,
         shape(SLOTS * 2 * EACH, NZ),
-        [VMEM] + [SMEM] * 3,
+        [VMEM] * 2 + [SMEM] * 3,
         scratch=[
             pltpu.VMEM((2, WIDE, NX, NZ), F32),
-            pltpu.VMEM((WIDE, NX, NZ), F32),
             pltpu.VMEM((2, 2, WIDE, NX, NZ), F32),
             pltpu.VMEM((9, WIDE, NX, NZ), F32),
         ],
-    )(spectrum, diffusivity, drift, mine)
+    )(spectrum, cells, diffusivity, drift, mine)
     solved = exchange(sent, BLOCK)
     sent = call(to_steps, shape(GROUPS, EACH, LOCAL, NZ), [VMEM] * 2)(solved, jnp.asarray(back))
     rows = exchange(sent.reshape(GROUPS * EACH * LOCAL, NZ), TM)
@@ -295,6 +293,7 @@
     fine = Mesh(mesh.devices.reshape(2, 2, 4, 2, 4, 4), AXES)
     big = P(TM, SPACE, None, None)
     plane = P(SPACE, None, None)
+
     return jax.shard_map(
         local,
         mesh=fine,

time: 167 us -> 163 us (0.976)
  waiting for transfers between devices: 64.5 us -> 44.1 us
  starting transfers between devices: 30.5 us -> 42.3 us
  blocking collectives: 53.2 us -> 57.6 us
    all_to_all x2, waiting for transfers between devices: 52.4 us -> 8.61 us  [exchange(): return lax.all_to_all(value, axes, split_axis=0, concat_axis=0, tiled=True)]
    ppermute x0 -> x4, waiting for transfers between devices: none -> 23.3 us  [local(): other = lax.ppermute(cells, axis, [(i, i ^ bit) for i in range(4)])]
    ppermute x0 -> x4, starting transfers between devices: none -> 11.9 us  [local(): other = lax.ppermute(cells, axis, [(i, i ^ bit) for i in range(4)])]
    all_to_all x2, blocking collectives: 53.2 us -> 57.6 us  [exchange(): return lax.all_to_all(value, axes, split_axis=0, concat_axis=0, tiled=True)]
  transfers between devices with their start and end apart: 5 -> 9, of which waited for: 4 -> 7; matrix products, arithmetic and copies ran while one was open for 0% -> 1% of each run, Pallas kernels for 1% -> 2%
where the time goes in v3:
time: 163 us; the launch traced here: 162 us
  blocking collectives  57.6 us (35%)
  waiting for transfers between devices  44.1 us (27%)
  starting transfers between devices  42.3 us (26%)
  Pallas kernels  14 us (9%)
  other arithmetic  2.11 us (1%)
    all_to_all x2, blocking collectives, exchange(): return lax.all_to_all(value, axes, split_axis=0, concat_axis=0, tiled=True)  57.6 us
    ppermute x4, waiting for transfers between devices, local(): other = lax.ppermute(cells, axis, [(i, i ^ bit) for i in range(4)])  23.3 us
    all_to_all x2, starting transfers between devices, exchange(): return lax.all_to_all(value, axes, split_axis=0, concat_axis=0, tiled=True)  22.4 us
    ppermute x4, starting transfers between devices, local(): other = lax.ppermute(cells, axis, [(i, i ^ bit) for i in range(4)])  11.9 us
    all_to_all x2, waiting for transfers between devices, exchange(): return lax.all_to_all(value, axes, split_axis=0, concat_axis=0, tiled=True)  8.61 us
    pallas_call x1, Pallas kernels, local(): call(solve_slot, shape(SLOTS * 2 * EACH, NZ), [VMEM] * 2 + [SMEM] * 3, sc...  8.38 us
    ppermute x1, waiting for transfers between devices, local(): west = lax.ppermute(masked, SPACE, up)  6.23 us
    ppermute x1, waiting for transfers between devices, local(): east = lax.ppermute(masked, SPACE, down)  5.95 us
  transfers between devices with their start and end apart: 9, of which 7 were waited for; matrix products, arithmetic and copies ran while one was open for 1% of the time, Pallas kernels for 2%

profile of v3, /device:TPU:8, one launch (start us, length us, event | category | flops | bytes accessed | tf_op | source)
XLA Modules:
  0.0 162.5 jit_solution(4260949071687238641)
XLA Ops:
  0.6 0.8 convert_bitcast_fusion
  1.5 1.1 bitcast_multiply_fusion.masked_ref
  2.6 0.0 copy-start
  2.6 0.0 copy-start.3
  2.6 4.7 %collective-permute-start = (f32[8,128,128]{2,1,0:T(8,128)S(1)}, f32[8,128,128]{2,1,0:T(8,128)S(1)}, u32[]{:S(2)}, u32[]{:S(2)}) collective-permute-start(f32[8,128,128]{2,1,0:T(8,128)S(1)} %bitcast_multiply_fusion.masked_ref), channel_id=1, source_target_pairs={{1,0},{2,1},{3,2},{4,3},{5,4},{6,5},{7,6},{8,7},{9,8},{10,9},{11,1... | collective-permute-start | bytes 1572872 | tf_op jit(solution)/shard_map/ppermute | solution.py:245
  7.3 1.9 %collective-permute-start.1 = (f32[8,128,128]{2,1,0:T(8,128)S(1)}, f32[8,128,128]{2,1,0:T(8,128)S(1)}, u32[]{:S(2)}, u32[]{:S(2)}) collective-permute-start(f32[8,128,128]{2,1,0:T(8,128)S(1)} %bitcast_multiply_fusion.masked_ref), channel_id=1, source_target_pairs={{0,1},{1,2},{2,3},{3,4},{4,5},{5,6},{6,7},{7,8},{8,9},{9,10},{10,1... | collective-permute-start | bytes 1572872 | tf_op jit(solution)/shard_map/ppermute | solution.py:244
  9.3 1.5 collective-permute-start.2
  10.8 0.6 copy-done.6
  11.5 1.1 shard_map.113
  12.5 5.9 %collective-permute-done.east_ref = f32[8,128,128]{2,1,0:T(8,128)S(1)} collective-permute-done((f32[8,128,128]{2,1,0:T(8,128)S(1)}, f32[8,128,128]{2,1,0:T(8,128)S(1)}, u32[]{:S(2)}, u32[]{:S(2)}) %collective-permute-start) | collective-permute-done | bytes 524320 | tf_op jit(solution)/shard_map/ppermute | solution.py:245
  18.5 6.2 %collective-permute-done.1.west_ref = f32[8,128,128]{2,1,0:T(8,128)S(1)} collective-permute-done((f32[8,128,128]{2,1,0:T(8,128)S(1)}, f32[8,128,128]{2,1,0:T(8,128)S(1)}, u32[]{:S(2)}, u32[]{:S(2)}) %collective-permute-start.1) | collective-permute-done | bytes 524320 | tf_op jit(solution)/shard_map/ppermute | solution.py:244
  24.7 1.3 shard_map.114
  26.0 16.7 %all-to-all-start = ((f32[32,40,128]{2,1,0:T(8,128)}), f32[32,40,128]{2,1,0:T(8,128)S(1)}, u32[]{:S(2)}, u32[]{:S(2)}) async-start(f32[32,40,128]{2,1,0:T(8,128)} %bitcast.10), calls=%async_computation | async-start | bytes 1310720 | tf_op jit(solution)/shard_map/all_to_all | solution.py:230
  42.7 0.0 copy-start.4
  42.7 2.1 %collective-permute-start.3 = (s32[1,1,40,128]{3,2,1,0:T(8,128)S(1)}, s32[1,1,40,128]{3,2,1,0:T(8,128)S(1)}, u32[]{:S(2)}, u32[]{:S(2)}) collective-permute-start(s32[1,1,40,128]{3,2,1,0:T(8,128)S(1)} %fusion), channel_id=1, source_target_pairs={{0,4},{4,0},{8,12},{12,8},{1,5},{5,1},{9,13},{13,9},{2,6},{6,2},{1... | collective-permute-start | bytes 61448 | tf_op jit(solution)/shard_map/ppermute | solution.py:252
  44.8 12.7 %collective-permute-done.3 = s32[1,1,40,128]{3,2,1,0:T(8,128)S(1)} collective-permute-done((s32[1,1,40,128]{3,2,1,0:T(8,128)S(1)}, s32[1,1,40,128]{3,2,1,0:T(8,128)S(1)}, u32[]{:S(2)}, u32[]{:S(2)}) %collective-permute-start.3) | collective-permute-done | bytes 20512 | tf_op jit(solution)/shard_map/ppermute | solution.py:252
  57.5 1.9 %collective-permute-start.4 = (s32[2,1,40,128]{3,2,1,0:T(8,128)S(1)}, s32[2,1,40,128]{3,2,1,0:T(8,128)S(1)}, u32[]{:S(2)}, u32[]{:S(2)}) collective-permute-start(s32[2,1,40,128]{3,2,1,0:T(8,128)S(1)} %pad_add_fusion.3), channel_id=1, source_target_pairs={{0,8},{4,12},{8,0},{12,4},{1,9},{5,13},{9,1},{13,5},{2,10},{6,14},... | collective-permute-start | bytes 122888 | tf_op jit(solution)/shard_map/ppermute | solution.py:252
  59.4 7.7 %all-to-all-done = f32[32,40,128]{2,1,0:T(8,128)S(1)} async-done(((f32[32,40,128]{2,1,0:T(8,128)}), f32[32,40,128]{2,1,0:T(8,128)S(1)}, u32[]{:S(2)}, u32[]{:S(2)}) %all-to-all-start) | async-done | bytes 655392 | tf_op jit(solution)/shard_map/all_to_all | solution.py:230
  67.2 1.7 %shard_map.115 = f32[1280,128]{1,0:T(8,128)} custom-call(f32[32,5,8,128]{3,2,1,0:T(8,128)S(1)} %bitcast.35, f32[256,256]{1,0:T(8,128)S(1)} %copy-done.4), custom_call_target="tpu_custom_call" | custom-call | flops 1000000 | bytes 2000000 | tf_op jit(solution)/shard_map/pallas_call | solution.py:271
  68.8 5.7 %all-to-all-start.1 = ((f32[128,1,1280]{2,1,0:T(1,128)}), f32[128,1,1280]{2,1,0:T(1,128)S(1)}, u32[]{:S(2)}, u32[]{:S(2)}) async-start(f32[128,1,1280]{2,1,0:T(1,128)} %bitcast.12), calls=%async_computation.1 | async-start | bytes 1310720 | tf_op jit(solution)/shard_map/all_to_all | solution.py:230
  74.6 3.4 %collective-permute-start.5 = (s32[4,1,40,128]{3,2,1,0:T(8,128)S(1)}, s32[4,1,40,128]{3,2,1,0:T(8,128)S(1)}, u32[]{:S(2)}, u32[]{:S(2)}) collective-permute-start(s32[4,1,40,128]{3,2,1,0:T(8,128)S(1)} %pad_add_fusion.2), channel_id=1, source_target_pairs={{0,1},{1,0},{2,3},{3,2},{4,5},{5,4},{6,7},{7,6},{8,9},{9,8},{10,11... | collective-permute-start | bytes 245768 | tf_op jit(solution)/shard_map/ppermute | solution.py:252
  78.0 4.7 %collective-permute-done.5 = s32[4,1,40,128]{3,2,1,0:T(8,128)S(1)} collective-permute-done((s32[4,1,40,128]{3,2,1,0:T(8,128)S(1)}, s32[4,1,40,128]{3,2,1,0:T(8,128)S(1)}, u32[]{:S(2)}, u32[]{:S(2)}) %collective-permute-start.5) | collective-permute-done | bytes 81952 | tf_op jit(solution)/shard_map/ppermute | solution.py:252
  82.7 4.5 %collective-permute-start.6 = (s32[4,2,40,128]{3,2,1,0:T(8,128)S(1)}, s32[4,2,40,128]{3,2,1,0:T(8,128)S(1)}, u32[]{:S(2)}, u32[]{:S(2)}) collective-permute-start(s32[4,2,40,128]{3,2,1,0:T(8,128)S(1)} %pad_add_fusion.1), channel_id=1, source_target_pairs={{0,2},{1,3},{2,0},{3,1},{4,6},{5,7},{6,4},{7,5},{8,10},{9,11},{10,... | collective-permute-start | bytes 491528 | tf_op jit(solution)/shard_map/ppermute | solution.py:252
  87.2 0.7 dynamic-slice_bitcast_fusion.shift_ref
  87.9 6.0 %collective-permute-done.6 = s32[4,2,40,128]{3,2,1,0:T(8,128)S(1)} collective-permute-done((s32[4,2,40,128]{3,2,1,0:T(8,128)S(1)}, s32[4,2,40,128]{3,2,1,0:T(8,128)S(1)}, u32[]{:S(2)}, u32[]{:S(2)}) %collective-permute-start.6) | collective-permute-done | bytes 163872 | tf_op jit(solution)/shard_map/ppermute | solution.py:252
  94.0 0.9 all-to-all-done.1
  94.9 8.4 %shard_map.116 = f32[1024,128]{1,0:T(8,128)S(1)} custom-call(f32[1280,128]{1,0:T(8,128)S(1)} %bitcast.34, s32[640,128]{1,0:T(8,128)S(1)} %bitcast.40, f32[8]{0:T(128)S(1)} %copy-done.7, f32[3,8]{1,0:T(4,128)S(1)} %copy-done.6, f32[4]{0:T(128)S(1)} %dynamic-slice_bitcast_fusion.shift_ref), custom_call_target="tpu_custom_call" | custom-call | flops 1000000 | bytes 2000000 | tf_op jit(solution)/shard_map/pallas_call | solution.py:274
  103.3 0.0 copy-start.2
  103.3 27.7 %all_to_all.36 = f32[128,8,128]{2,1,0:T(8,128)S(1)} all-to-all(f32[128,8,128]{2,1,0:T(8,128)S(1)} %bitcast.36), channel_id=1, replica_groups=mesh['yh'=2,'zh'=2,'zl'=4,'core'=2,'yl'=4,'x'=4] {'zl','core','yl','x'}, dimensions={0} | all-to-all | bytes 1048576 | tf_op jit(solution)/shard_map/all_to_all | solution.py:230
  130.9 0.7 shard_map.117
  131.6 30.0 %all_to_all.37 = f32[32,32,128]{2,1,0:T(8,128)S(1)} all-to-all(f32[32,32,128]{2,1,0:T(8,128)S(1)} %bitcast.38), channel_id=1, replica_groups=mesh['yh'=2,'zh'=2,'zl'=4,'core'=2,'yl'=4,'x'=4] {'yh','zh','zl','core'}, dimensions={0} | all-to-all | bytes 1048576 | tf_op jit(solution)/shard_map/all_to_all | solution.py:230
  161.6 0.9 shard_map.118
  (24 shorter events, 0.2 us)
Async XLA Ops:
  1.5 9.3 %copy-start.1 = (f32[8,1,128,128]{3,2,1,0:T(8,128)S(1)}, f32[8,1,128,128]{3,2,1,0:T(8,128)}, u32[]{:S(2)}) copy-start(f32[8,1,128,128]{3,2,1,0:T(8,128)} %param.11) | copy-start | bytes 1572868
  2.6 8.2 %copy-start = (s32[1,128,128]{2,1,0:T(8,128)S(1)}, s32[1,128,128]{2,1,0:T(8,128)}, u32[]{:S(2)}) copy-start(s32[1,128,128]{2,1,0:T(8,128)} %param.14) | copy-start | bytes 196612
  2.6 8.2 %copy-start.3 = (s32[1,128,128]{2,1,0:T(8,128)S(1)}, s32[1,128,128]{2,1,0:T(8,128)}, u32[]{:S(2)}) copy-start(s32[1,128,128]{2,1,0:T(8,128)} %param.13) | copy-start | bytes 196612
  2.6 15.9 %collective-permute-start = (f32[8,128,128]{2,1,0:T(8,128)S(1)}, f32[8,128,128]{2,1,0:T(8,128)S(1)}, u32[]{:S(2)}, u32[]{:S(2)}) collective-permute-start(f32[8,128,128]{2,1,0:T(8,128)S(1)} %bitcast_multiply_fusion.masked_ref), channel_id=1, source_target_pairs={{1,0},{2,1},{3,2},{4,3},{5,4},{6,5},{7,6},{8,7},{9,8},{10,9},{11,1... | collective-permute-start | bytes 1572872 | tf_op jit(solution)/shard_map/ppermute | solution.py:245
  7.3 17.4 %collective-permute-start.1 = (f32[8,128,128]{2,1,0:T(8,128)S(1)}, f32[8,128,128]{2,1,0:T(8,128)S(1)}, u32[]{:S(2)}, u32[]{:S(2)}) collective-permute-start(f32[8,128,128]{2,1,0:T(8,128)S(1)} %bitcast_multiply_fusion.masked_ref), channel_id=1, source_target_pairs={{0,1},{1,2},{2,3},{3,4},{4,5},{5,6},{6,7},{7,8},{8,9},{9,10},{10,1... | collective-permute-start | bytes 1572872 | tf_op jit(solution)/shard_map/ppermute | solution.py:244
  9.3 3.3 %collective-permute-start.2 = (f32[128,128]{1,0:T(8,128)S(1)}, f32[128,128]{1,0:T(8,128)S(1)}, u32[]{:S(2)}, u32[]{:S(2)}) collective-permute-start(f32[128,128]{1,0:T(8,128)S(1)} %slice_bitcast_fusion), channel_id=1, source_target_pairs={{0,16},{16,32},{32,48},{48,64},{64,80},{80,96},{96,112},{112,128},... | collective-permute-start | bytes 196616 | tf_op jit(solution)/shard_map/ppermute | solution.py:246
  10.8 0.7 copy-start.6
  10.8 0.7 copy-start.7
  11.5 13.3 %copy-start.5 = (f32[1,128,128]{2,1,0:T(8,128)S(1)}, f32[1,128,128]{2,1,0:T(8,128)}, u32[]{:S(2)}) copy-start(f32[1,128,128]{2,1,0:T(8,128)} %param.12) | copy-start | bytes 196612
  26.0 41.2 %all-to-all-start = ((f32[32,40,128]{2,1,0:T(8,128)}), f32[32,40,128]{2,1,0:T(8,128)S(1)}, u32[]{:S(2)}, u32[]{:S(2)}) async-start(f32[32,40,128]{2,1,0:T(8,128)} %bitcast.10), calls=%async_computation | async-start | bytes 1310720 | tf_op jit(solution)/shard_map/all_to_all | solution.py:230
  42.7 24.5 %copy-start.4 = (f32[256,256]{1,0:T(8,128)S(1)}, f32[256,256]{1,0:T(8,128)}, u32[]{:S(2)}) copy-start(f32[256,256]{1,0:T(8,128)} %constant.50.clone.table_ref) | copy-start | bytes 786436
  42.7 14.7 %collective-permute-start.3 = (s32[1,1,40,128]{3,2,1,0:T(8,128)S(1)}, s32[1,1,40,128]{3,2,1,0:T(8,128)S(1)}, u32[]{:S(2)}, u32[]{:S(2)}) collective-permute-start(s32[1,1,40,128]{3,2,1,0:T(8,128)S(1)} %fusion), channel_id=1, source_target_pairs={{0,4},{4,0},{8,12},{12,8},{1,5},{5,1},{9,13},{13,9},{2,6},{6,2},{1... | collective-permute-start | bytes 61448 | tf_op jit(solution)/shard_map/ppermute | solution.py:252
  57.5 17.1 %collective-permute-start.4 = (s32[2,1,40,128]{3,2,1,0:T(8,128)S(1)}, s32[2,1,40,128]{3,2,1,0:T(8,128)S(1)}, u32[]{:S(2)}, u32[]{:S(2)}) collective-permute-start(s32[2,1,40,128]{3,2,1,0:T(8,128)S(1)} %pad_add_fusion.3), channel_id=1, source_target_pairs={{0,8},{4,12},{8,0},{12,4},{1,9},{5,13},{9,1},{13,5},{2,10},{6,14},... | collective-permute-start | bytes 122888 | tf_op jit(solution)/shard_map/ppermute | solution.py:252
  68.8 26.0 %all-to-all-start.1 = ((f32[128,1,1280]{2,1,0:T(1,128)}), f32[128,1,1280]{2,1,0:T(1,128)S(1)}, u32[]{:S(2)}, u32[]{:S(2)}) async-start(f32[128,1,1280]{2,1,0:T(1,128)} %bitcast.12), calls=%async_computation.1 | async-start | bytes 1310720 | tf_op jit(solution)/shard_map/all_to_all | solution.py:230
  74.6 8.1 %collective-permute-start.5 = (s32[4,1,40,128]{3,2,1,0:T(8,128)S(1)}, s32[4,1,40,128]{3,2,1,0:T(8,128)S(1)}, u32[]{:S(2)}, u32[]{:S(2)}) collective-permute-start(s32[4,1,40,128]{3,2,1,0:T(8,128)S(1)} %pad_add_fusion.2), channel_id=1, source_target_pairs={{0,1},{1,0},{2,3},{3,2},{4,5},{5,4},{6,7},{7,6},{8,9},{9,8},{10,11... | collective-permute-start | bytes 245768 | tf_op jit(solution)/shard_map/ppermute | solution.py:252
  82.7 11.2 %collective-permute-start.6 = (s32[4,2,40,128]{3,2,1,0:T(8,128)S(1)}, s32[4,2,40,128]{3,2,1,0:T(8,128)S(1)}, u32[]{:S(2)}, u32[]{:S(2)}) collective-permute-start(s32[4,2,40,128]{3,2,1,0:T(8,128)S(1)} %pad_add_fusion.1), channel_id=1, source_target_pairs={{0,2},{1,3},{2,0},{3,1},{4,6},{5,7},{6,4},{7,5},{8,10},{9,11},{10,... | collective-permute-start | bytes 491528 | tf_op jit(solution)/shard_map/ppermute | solution.py:252
  103.3 27.7 %copy-start.2 = (f32[256,256]{1,0:T(8,128)S(1)}, f32[256,256]{1,0:T(8,128)}, u32[]{:S(2)}) copy-start(f32[256,256]{1,0:T(8,128)} %constant.52.clone.table_ref) | copy-start | bytes 786436

commit v4 on v3

--- a/solution.py
+++ b/solution.py
@@ -30,7 +30,7 @@
 SPACE = ("yl", "x")
 BLOCK = ("zl", "core", "yl", "x")
 
-GRANT = 24 << 20
+GRANT = 16 << 20
 VMEM = pl.BlockSpec(memory_space=pltpu.VMEM)
 SMEM = pl.BlockSpec(memory_space=pltpu.SMEM)
 F32 = jnp.float32
@@ -147,67 +147,81 @@
         out_ref[n] = rows_ref[pl.ds(n, NY, stride=LOCAL), :]
 
 
-def solve_slot(spectrum_ref, cells_ref, kappa_ref, drift_ref, shift_ref, sent_ref, source, field, coefficient):
+def prepare_slot(cells_ref, kappa_ref, drift_ref, shift_ref, coefficient_ref):
     edge = lax.broadcasted_iota(jnp.int32, (NX, NZ), 0)
     lane = lax.broadcasted_iota(jnp.int32, (NX, NZ), 1)
     first, second, turn = shift_ref[0], shift_ref[1], shift_ref[2]
-    for member in range(MEMBERS):
-        for row in range(WIDE_EACH):
-            at = member * NX * 2 * WIDE_EACH + row
-            for part in range(2):
-                rows = pl.ds(at + part * WIDE_EACH, NX, stride=2 * WIDE_EACH)
-                source[part, member * WIDE_EACH + row] = spectrum_ref[rows, :]
 
     def prepare(y, carry):
         classes = cells_ref[pl.ds(y, NX, stride=WIDE), :]
         weight = jnp.where(classes == SOLID, 0.0, 1.0)
         kappa, (flow_x, flow_y, flow_z) = look_up(classes, kappa_ref, drift_ref)
-        coefficient[0, y] = jnp.where(edge == NX - 1, 0.0, kappa - flow_x)
-        coefficient[1, y] = jnp.where(edge == 0, 0.0, kappa + flow_x)
-        coefficient[2, y] = kappa - flow_y
-        coefficient[3, y] = kappa + flow_y
-        coefficient[4, y] = jnp.where(lane == NZ - 1, 0.0, kappa - flow_z)
-        coefficient[5, y] = jnp.where(lane == 0, 0.0, kappa + flow_z)
+        coefficient_ref[0, y] = jnp.where(edge == NX - 1, 0.0, kappa - flow_x)
+        coefficient_ref[1, y] = jnp.where(edge == 0, 0.0, kappa + flow_x)
+        coefficient_ref[2, y] = kappa - flow_y
+        coefficient_ref[3, y] = kappa + flow_y
+        coefficient_ref[4, y] = jnp.where(lane == NZ - 1, 0.0, kappa - flow_z)
+        coefficient_ref[5, y] = jnp.where(lane == 0, 0.0, kappa + flow_z)
         real_first = first + 6.0 * kappa
         real_second = second + 6.0 * kappa
         over_first = weight / (real_first * real_first + turn * turn)
         over_second = weight / (real_second * real_second + turn * turn)
-        a, b, c = real_first * over_first, turn * over_first, real_second * over_second
-        coefficient[6, y] = a
-        coefficient[7, y] = b
-        coefficient[8, y] = c
-        one, two = source[0, y], source[1, y]
-        field[0, 0, y] = a * one + b * two
-        field[0, 1, y] = c * two - b * one
+        coefficient_ref[6, y] = real_first * over_first
+        coefficient_ref[7, y] = turn * over_first
+        coefficient_ref[8, y] = real_second * over_second
         return carry
 
     lax.fori_loop(0, WIDE, prepare, 0, unroll=2)
 
+
+def solve_slot(spectrum_ref, coefficient_ref, sent_ref, source, even, odd):
+    def scale(y, one, two):
+        a, b, c = coefficient_ref[6, y], coefficient_ref[7, y], coefficient_ref[8, y]
+        return a * one + b * two, c * two - b * one
+
+    blank = jnp.zeros((2, NX, NZ), F32)
+    even[0] = blank
+    even[WIDE + 1] = blank
+    for member in range(MEMBERS):
+        for row in range(WIDE_EACH):
+            at = member * NX * 2 * WIDE_EACH + row
+            y = member * WIDE_EACH + row
+            one = spectrum_ref[pl.ds(at, NX, stride=2 * WIDE_EACH), :]
+            two = spectrum_ref[pl.ds(at + WIDE_EACH, NX, stride=2 * WIDE_EACH), :]
+            source[y, 0] = one
+            source[y, 1] = two
+            even[y + 1, 0], even[y + 1, 1] = scale(y, one, two)
+
     for sweep in range(SWEEPS):
-        now, later = sweep % 2, (sweep + 1) % 2
+        now, later = (even, odd) if sweep % 2 == 0 else (odd, even)
+        begin = (sweep + 1) // 2 * 2
+        end = WIDE - begin
 
         def row(y, carry):
+            south, here = carry
+            north = (now[y + 2, 0], now[y + 2, 1])
             totals = []
             for part in range(2):
-                here = field[now, part, y]
-                total = source[part, y]
-                total += coefficient[0, y] * pltpu.roll(here, NX - 1, 0) + coefficient[1, y] * pltpu.roll(here, 1, 0)
-                total += coefficient[2, y] * field[now, part, y + 1] + coefficient[3, y] * field[now, part, y - 1]
-                total += coefficient[4, y] * pltpu.roll(here, NZ - 1, 1) + coefficient[5, y] * pltpu.roll(here, 1, 1)
+                mid = here[part]
+                total = source[y, part]
+                total += coefficient_ref[0, y] * pltpu.roll(mid, NX - 1, 0)
+                total += coefficient_ref[1, y] * pltpu.roll(mid, 1, 0)
+                total += coefficient_ref[2, y] * north[part] + coefficient_ref[3, y] * south[part]
+                total += coefficient_ref[4, y] * pltpu.roll(mid, NZ - 1, 1)
+                total += coefficient_ref[5, y] * pltpu.roll(mid, 1, 1)
                 totals.append(total)
-            one, two = totals
-            a, b, c = coefficient[6, y], coefficient[7, y], coefficient[8, y]
-            field[later, 0, y] = a * one + b * two
-            field[later, 1, y] = c * two - b * one
-            return carry
-
-        lax.fori_loop(sweep + 1, WIDE - 1 - sweep, row, 0, unroll=2)
-
+            later[y + 1, 0], later[y + 1, 1] = scale(y, *totals)
+            return here, north
+
+        start = tuple((now[begin + k, 0], now[begin + k, 1]) for k in range(2))
+        lax.fori_loop(begin, end, row, start, unroll=4)
+
+    field = even if SWEEPS % 2 == 0 else odd
     for member in range(MEMBERS):
         for row in range(EACH):
             for part in range(2):
                 at = member * NX * 2 * EACH + part * EACH + row
-                sent_ref[pl.ds(at, NX, stride=2 * EACH), :] = field[SWEEPS % 2, part, HALO + member * EACH + row]
+                sent_ref[pl.ds(at, NX, stride=2 * EACH), :] = field[HALO + member * EACH + row + 1, part]
 
 
 def call(kernel, out_shape, in_specs, scratch=(), flops=1_000_000, moved=2_000_000):
@@ -271,16 +285,17 @@
     sent = call(to_frequencies, shape(SLOTS * 2 * WIDE_EACH, NZ), [VMEM] * 2)(steps, jnp.asarray(forward))
     spectrum = exchange(sent.reshape(SLOTS, 1, 2 * WIDE_EACH * NZ), BLOCK).reshape(SLOTS * 2 * WIDE_EACH, NZ)
     mine = lax.dynamic_slice_in_dim(jnp.asarray(shift), lax.axis_index(BLOCK), 1, 0).reshape(4)
+    coefficient = call(prepare_slot, shape(9, WIDE, NX, NZ), [VMEM] + [SMEM] * 3)(cells, diffusivity, drift, mine)
     sent = call(
         solve_slot,
         shape(SLOTS * 2 * EACH, NZ),
-        [VMEM] * 2 + [SMEM] * 3,
+        [VMEM] * 2,
         scratch=[
-            pltpu.VMEM((2, WIDE, NX, NZ), F32),
-            pltpu.VMEM((2, 2, WIDE, NX, NZ), F32),
-            pltpu.VMEM((9, WIDE, NX, NZ), F32),
+            pltpu.VMEM((WIDE, 2, NX, NZ), F32),
+            pltpu.VMEM((WIDE + 2, 2, NX, NZ), F32),
+            pltpu.VMEM((WIDE + 2, 2, NX, NZ), F32),
         ],
-    )(spectrum, cells, diffusivity, drift, mine)
+    )(spectrum, coefficient)
     solved = exchange(sent, BLOCK)
     sent = call(to_steps, shape(GROUPS, EACH, LOCAL, NZ), [VMEM] * 2)(solved, jnp.asarray(back))
     rows = exchange(sent.reshape(GROUPS * EACH * LOCAL, NZ), TM)

time: 163 us -> 161 us (0.988)
  waiting for transfers between devices: 44.1 us -> 33.3 us
  starting transfers between devices: 42.3 us -> 48.5 us
  local copies, waits for them, and re-layouts: 1.4 us -> 5.65 us
  Pallas kernels: 14 us -> 12.2 us
    ppermute x1, waiting for transfers between devices: 5.95 us -> 1.18 us  [local(): east = lax.ppermute(masked, SPACE, down)]
    unnamed x16 -> x24, local copies, waits for them, and re-layouts: 0.67 us -> 4.93 us
    all_to_all x2, waiting for transfers between devices: 8.61 us -> 5.56 us  [exchange(): return lax.all_to_all(value, axes, split_axis=0, concat_axis=0, tiled=True)]
    all_to_all x2, starting transfers between devices: 22.4 us -> 25.4 us  [exchange(): return lax.all_to_all(value, axes, split_axis=0, concat_axis=0, tiled=True)]
    ppermute x1, waiting for transfers between devices: 6.23 us -> 3.22 us  [local(): west = lax.ppermute(masked, SPACE, up)]
    ppermute x4, starting transfers between devices: 11.9 us -> 13.9 us  [local(): other = lax.ppermute(cells, axis, [(i, i ^ bit) for i in range(4)])]
    pallas_call x1 -> x2, Pallas kernels: 8.38 us -> 6.67 us  [the longest x1 5.1 us: local(): call(solve_slot, shape(SLOTS * 2 * EACH, NZ), [VMEM] * 2, scratch=[pltpu....]
  transfers between devices with their start and end apart: 9 -> 9, of which waited for: 7 -> 6; matrix products, arithmetic and copies ran while one was open for 1% -> 1% of each run, Pallas kernels for 2% -> 3%
where the time goes in v4:
time: 161 us; the launch traced here: 160 us
  blocking collectives  57.2 us (36%)
  starting transfers between devices  48.5 us (30%)
  waiting for transfers between devices  33.3 us (21%)
  Pallas kernels  12.2 us (8%)
  local copies, waits for them, and re-layouts  5.65 us (4%)
  other arithmetic  2.15 us (1%)
    all_to_all x2, blocking collectives, exchange(): return lax.all_to_all(value, axes, split_axis=0, concat_axis=0, tiled=True)  57.2 us
    all_to_all x2, starting transfers between devices, exchange(): return lax.all_to_all(value, axes, split_axis=0, concat_axis=0, tiled=True)  25.4 us
    ppermute x4, waiting for transfers between devices, local(): other = lax.ppermute(cells, axis, [(i, i ^ bit) for i in range(4)])  23.3 us
    ppermute x4, starting transfers between devices, local(): other = lax.ppermute(cells, axis, [(i, i ^ bit) for i in range(4)])  13.9 us
    all_to_all x2, waiting for transfers between devices, exchange(): return lax.all_to_all(value, axes, split_axis=0, concat_axis=0, tiled=True)  5.56 us
    pallas_call x1, Pallas kernels, local(): call(solve_slot, shape(SLOTS * 2 * EACH, NZ), [VMEM] * 2, scratch=[pltpu....  5.1 us
    unnamed x24, local copies, waits for them, and re-layouts  4.93 us
    ppermute x1, starting transfers between devices, local(): east = lax.ppermute(masked, SPACE, down)  4.55 us
  transfers between devices with their start and end apart: 9, of which 6 were waited for; matrix products, arithmetic and copies ran while one was open for 1% of the time, Pallas kernels for 3%

profile of v4, /device:TPU:8, one launch (start us, length us, event | category | flops | bytes accessed | tf_op | source)
XLA Modules:
  0.0 160.0 jit_solution(13037172178651158560)
XLA Ops:
  0.7 0.9 convert_bitcast_fusion
  1.6 1.1 bitcast_multiply_fusion.masked_ref
  2.7 3.4 %collective-permute-start.1 = (f32[8,128,128]{2,1,0:T(8,128)S(1)}, f32[8,128,128]{2,1,0:T(8,128)S(1)}, u32[]{:S(2)}, u32[]{:S(2)}) collective-permute-start(f32[8,128,128]{2,1,0:T(8,128)S(1)} %bitcast_multiply_fusion.masked_ref), channel_id=1, source_target_pairs={{0,1},{1,2},{2,3},{3,4},{4,5},{5,6},{6,7},{7,8},{8,9},{9,10},{10,1... | collective-permute-start | bytes 1572872 | tf_op jit(solution)/shard_map/ppermute | solution.py:258
  6.1 4.6 %collective-permute-start = (f32[8,128,128]{2,1,0:T(8,128)S(1)}, f32[8,128,128]{2,1,0:T(8,128)S(1)}, u32[]{:S(2)}, u32[]{:S(2)}) collective-permute-start(f32[8,128,128]{2,1,0:T(8,128)S(1)} %bitcast_multiply_fusion.masked_ref), channel_id=1, source_target_pairs={{1,0},{2,1},{3,2},{4,3},{5,4},{6,5},{7,6},{8,7},{9,8},{10,9},{11,1... | collective-permute-start | bytes 1572872 | tf_op jit(solution)/shard_map/ppermute | solution.py:259
  10.7 1.3 collective-permute-start.2
  12.0 0.8 copy-done
  12.8 1.0 copy-done.2
  13.9 0.8 copy-done.4
  14.7 0.7 copy-done.8
  16.0 1.1 shard_map.113
  17.1 3.2 %collective-permute-done.1.west_ref = f32[8,128,128]{2,1,0:T(8,128)S(1)} collective-permute-done((f32[8,128,128]{2,1,0:T(8,128)S(1)}, f32[8,128,128]{2,1,0:T(8,128)S(1)}, u32[]{:S(2)}, u32[]{:S(2)}) %collective-permute-start.1) | collective-permute-done | bytes 524320 | tf_op jit(solution)/shard_map/ppermute | solution.py:258
  20.3 1.2 collective-permute-done.east_ref
  21.5 0.8 copy-done.7
  22.4 1.3 shard_map.114
  23.6 16.5 %all-to-all-start = ((f32[32,40,128]{2,1,0:T(8,128)}), f32[32,40,128]{2,1,0:T(8,128)S(1)}, u32[]{:S(2)}, u32[]{:S(2)}) async-start(f32[32,40,128]{2,1,0:T(8,128)} %bitcast.10), calls=%async_computation | async-start | bytes 1310720 | tf_op jit(solution)/shard_map/all_to_all | solution.py:244
  40.3 1.9 %collective-permute-start.3 = (s32[1,1,40,128]{3,2,1,0:T(8,128)S(1)}, s32[1,1,40,128]{3,2,1,0:T(8,128)S(1)}, u32[]{:S(2)}, u32[]{:S(2)}) collective-permute-start(s32[1,1,40,128]{3,2,1,0:T(8,128)S(1)} %fusion), channel_id=1, source_target_pairs={{0,4},{4,0},{8,12},{12,8},{1,5},{5,1},{9,13},{13,9},{2,6},{6,2},{1... | collective-permute-start | bytes 61448 | tf_op jit(solution)/shard_map/ppermute | solution.py:266
  42.2 13.2 %collective-permute-done.3 = s32[1,1,40,128]{3,2,1,0:T(8,128)S(1)} collective-permute-done((s32[1,1,40,128]{3,2,1,0:T(8,128)S(1)}, s32[1,1,40,128]{3,2,1,0:T(8,128)S(1)}, u32[]{:S(2)}, u32[]{:S(2)}) %collective-permute-start.3) | collective-permute-done | bytes 20512 | tf_op jit(solution)/shard_map/ppermute | solution.py:266
  55.4 3.8 %collective-permute-start.4 = (s32[2,1,40,128]{3,2,1,0:T(8,128)S(1)}, s32[2,1,40,128]{3,2,1,0:T(8,128)S(1)}, u32[]{:S(2)}, u32[]{:S(2)}) collective-permute-start(s32[2,1,40,128]{3,2,1,0:T(8,128)S(1)} %pad_add_fusion.3), channel_id=1, source_target_pairs={{0,8},{4,12},{8,0},{12,4},{1,9},{5,13},{9,1},{13,5},{2,10},{6,14},... | collective-permute-start | bytes 122888 | tf_op jit(solution)/shard_map/ppermute | solution.py:266
  59.2 5.6 %all-to-all-done = f32[32,40,128]{2,1,0:T(8,128)S(1)} async-done(((f32[32,40,128]{2,1,0:T(8,128)}), f32[32,40,128]{2,1,0:T(8,128)S(1)}, u32[]{:S(2)}, u32[]{:S(2)}) %all-to-all-start) | async-done | bytes 655392 | tf_op jit(solution)/shard_map/all_to_all | solution.py:244
  64.8 1.7 %shard_map.115 = f32[1280,128]{1,0:T(8,128)} custom-call(f32[32,5,8,128]{3,2,1,0:T(8,128)S(1)} %bitcast.34, f32[256,256]{1,0:T(8,128)S(1)} %copy-done.6), custom_call_target="tpu_custom_call" | custom-call | flops 1000000 | bytes 2000000 | tf_op jit(solution)/shard_map/pallas_call | solution.py:285
  66.4 8.9 %all-to-all-start.1 = ((f32[128,1,1280]{2,1,0:T(1,128)}), f32[128,1,1280]{2,1,0:T(1,128)}, u32[]{:S(2)}, u32[]{:S(2)}) async-start(f32[128,1,1280]{2,1,0:T(1,128)} %bitcast.12), calls=%async_computation.1 | async-start | bytes 1310720 | tf_op jit(solution)/shard_map/all_to_all | solution.py:244
  75.3 3.4 %collective-permute-start.5 = (s32[4,1,40,128]{3,2,1,0:T(8,128)S(1)}, s32[4,1,40,128]{3,2,1,0:T(8,128)S(1)}, u32[]{:S(2)}, u32[]{:S(2)}) collective-permute-start(s32[4,1,40,128]{3,2,1,0:T(8,128)S(1)} %pad_add_fusion.2), channel_id=1, source_target_pairs={{0,1},{1,0},{2,3},{3,2},{4,5},{5,4},{6,7},{7,6},{8,9},{9,8},{10,11... | collective-permute-start | bytes 245768 | tf_op jit(solution)/shard_map/ppermute | solution.py:266
  78.7 4.6 %collective-permute-done.5 = s32[4,1,40,128]{3,2,1,0:T(8,128)S(1)} collective-permute-done((s32[4,1,40,128]{3,2,1,0:T(8,128)S(1)}, s32[4,1,40,128]{3,2,1,0:T(8,128)S(1)}, u32[]{:S(2)}, u32[]{:S(2)}) %collective-permute-start.5) | collective-permute-done | bytes 81952 | tf_op jit(solution)/shard_map/ppermute | solution.py:266
  83.4 4.8 %collective-permute-start.6 = (s32[4,2,40,128]{3,2,1,0:T(8,128)S(1)}, s32[4,2,40,128]{3,2,1,0:T(8,128)S(1)}, u32[]{:S(2)}, u32[]{:S(2)}) collective-permute-start(s32[4,2,40,128]{3,2,1,0:T(8,128)S(1)} %pad_add_fusion.1), channel_id=1, source_target_pairs={{0,2},{1,3},{2,0},{3,1},{4,6},{5,7},{6,4},{7,5},{8,10},{9,11},{10,... | collective-permute-start | bytes 491528 | tf_op jit(solution)/shard_map/ppermute | solution.py:266
  88.3 0.7 dynamic-slice_bitcast_fusion.shift_ref
  89.0 5.5 %collective-permute-done.6 = s32[4,2,40,128]{3,2,1,0:T(8,128)S(1)} collective-permute-done((s32[4,2,40,128]{3,2,1,0:T(8,128)S(1)}, s32[4,2,40,128]{3,2,1,0:T(8,128)S(1)}, u32[]{:S(2)}, u32[]{:S(2)}) %collective-permute-start.6) | collective-permute-done | bytes 163872 | tf_op jit(solution)/shard_map/ppermute | solution.py:266
  94.5 1.6 shard_map.116.coefficient_ref
  96.1 5.1 %shard_map.117 = f32[1024,128]{1,0:T(8,128)S(1)} custom-call(f32[1280,128]{1,0:T(8,128)} %bitcast.13.spectrum_ref, f32[9,40,16,128]{3,2,1,0:T(8,128)S(1)} %shard_map.116.coefficient_ref), custom_call_target="tpu_custom_call" | custom-call | flops 1000000 | bytes 2000000 | tf_op jit(solution)/shard_map/pallas_call | solution.py:289
  101.2 28.2 %all_to_all.36 = f32[128,8,128]{2,1,0:T(8,128)S(1)} all-to-all(f32[128,8,128]{2,1,0:T(8,128)S(1)} %bitcast.38), channel_id=1, replica_groups=mesh['yh'=2,'zh'=2,'zl'=4,'core'=2,'yl'=4,'x'=4] {'zl','core','yl','x'}, dimensions={0} | all-to-all | bytes 1048576 | tf_op jit(solution)/shard_map/all_to_all | solution.py:244
  129.5 0.7 shard_map.118
  130.2 29.0 %all_to_all.37 = f32[32,32,128]{2,1,0:T(8,128)S(1)} all-to-all(f32[32,32,128]{2,1,0:T(8,128)S(1)} %bitcast.36), channel_id=1, replica_groups=mesh['yh'=2,'zh'=2,'zl'=4,'core'=2,'yl'=4,'x'=4] {'yh','zh','zl','core'}, dimensions={0} | all-to-all | bytes 1048576 | tf_op jit(solution)/shard_map/all_to_all | solution.py:244
  159.1 0.9 shard_map.119
  (33 shorter events, 0.9 us)
Async XLA Ops:
  0.6 39.6 %copy-start.1 = (s32[1,128,128]{2,1,0:T(8,128)S(1)}, s32[1,128,128]{2,1,0:T(8,128)}, u32[]{:S(2)}) copy-start(s32[1,128,128]{2,1,0:T(8,128)} %param.14) | copy-start | bytes 196612
  0.6 39.6 %copy-start.5 = (s32[1,128,128]{2,1,0:T(8,128)S(1)}, s32[1,128,128]{2,1,0:T(8,128)}, u32[]{:S(2)}) copy-start(s32[1,128,128]{2,1,0:T(8,128)} %param.13) | copy-start | bytes 196612
  1.6 63.2 %copy-start.6 = (f32[256,256]{1,0:T(8,128)S(1)}, f32[256,256]{1,0:T(8,128)}, u32[]{:S(2)}) copy-start(f32[256,256]{1,0:T(8,128)} %constant.50.clone.table_ref) | copy-start | bytes 786436
  2.7 17.7 %collective-permute-start.1 = (f32[8,128,128]{2,1,0:T(8,128)S(1)}, f32[8,128,128]{2,1,0:T(8,128)S(1)}, u32[]{:S(2)}, u32[]{:S(2)}) collective-permute-start(f32[8,128,128]{2,1,0:T(8,128)S(1)} %bitcast_multiply_fusion.masked_ref), channel_id=1, source_target_pairs={{0,1},{1,2},{2,3},{3,4},{4,5},{5,6},{6,7},{7,8},{8,9},{9,10},{10,1... | collective-permute-start | bytes 1572872 | tf_op jit(solution)/shard_map/ppermute | solution.py:258
  6.1 15.4 %collective-permute-start = (f32[8,128,128]{2,1,0:T(8,128)S(1)}, f32[8,128,128]{2,1,0:T(8,128)S(1)}, u32[]{:S(2)}, u32[]{:S(2)}) collective-permute-start(f32[8,128,128]{2,1,0:T(8,128)S(1)} %bitcast_multiply_fusion.masked_ref), channel_id=1, source_target_pairs={{1,0},{2,1},{3,2},{4,3},{5,4},{6,5},{7,6},{8,7},{9,8},{10,9},{11,1... | collective-permute-start | bytes 1572872 | tf_op jit(solution)/shard_map/ppermute | solution.py:259
  10.7 6.5 %collective-permute-start.2 = (f32[128,128]{1,0:T(8,128)S(1)}, f32[128,128]{1,0:T(8,128)S(1)}, u32[]{:S(2)}, u32[]{:S(2)}) collective-permute-start(f32[128,128]{1,0:T(8,128)S(1)} %slice_bitcast_fusion), channel_id=1, source_target_pairs={{0,16},{16,32},{32,48},{48,64},{64,80},{80,96},{96,112},{112,128},... | collective-permute-start | bytes 196616 | tf_op jit(solution)/shard_map/ppermute | solution.py:260
  12.0 0.8 copy-start
  12.8 1.0 copy-start.2
  13.9 0.8 copy-start.4
  14.7 0.7 copy-start.8
  15.4 0.7 copy-start.10
  21.5 0.8 copy-start.7
  23.6 41.2 %all-to-all-start = ((f32[32,40,128]{2,1,0:T(8,128)}), f32[32,40,128]{2,1,0:T(8,128)S(1)}, u32[]{:S(2)}, u32[]{:S(2)}) async-start(f32[32,40,128]{2,1,0:T(8,128)} %bitcast.10), calls=%async_computation | async-start | bytes 1310720 | tf_op jit(solution)/shard_map/all_to_all | solution.py:244
  40.2 54.4 %copy-start.9 = (f32[3,8]{1,0:T(4,128)S(1)}, f32[3,8]{1,0:T(4,128)}, u32[]{:S(2)}) copy-start(f32[3,8]{1,0:T(4,128)} %drift_ref.3) | copy-start | bytes 292
  40.2 54.3 %copy-start.11 = (f32[8]{0:T(128)S(1)}, f32[8]{0:T(128)}, u32[]{:S(2)}) copy-start(f32[8]{0:T(128)} %kappa_ref.3) | copy-start | bytes 100
  40.3 15.1 %collective-permute-start.3 = (s32[1,1,40,128]{3,2,1,0:T(8,128)S(1)}, s32[1,1,40,128]{3,2,1,0:T(8,128)S(1)}, u32[]{:S(2)}, u32[]{:S(2)}) collective-permute-start(s32[1,1,40,128]{3,2,1,0:T(8,128)S(1)} %fusion), channel_id=1, source_target_pairs={{0,4},{4,0},{8,12},{12,8},{1,5},{5,1},{9,13},{13,9},{2,6},{6,2},{1... | collective-permute-start | bytes 61448 | tf_op jit(solution)/shard_map/ppermute | solution.py:266
  55.4 19.9 %collective-permute-start.4 = (s32[2,1,40,128]{3,2,1,0:T(8,128)S(1)}, s32[2,1,40,128]{3,2,1,0:T(8,128)S(1)}, u32[]{:S(2)}, u32[]{:S(2)}) collective-permute-start(s32[2,1,40,128]{3,2,1,0:T(8,128)S(1)} %pad_add_fusion.3), channel_id=1, source_target_pairs={{0,8},{4,12},{8,0},{12,4},{1,9},{5,13},{9,1},{13,5},{2,10},{6,14},... | collective-permute-start | bytes 122888 | tf_op jit(solution)/shard_map/ppermute | solution.py:266
  66.4 29.7 %all-to-all-start.1 = ((f32[128,1,1280]{2,1,0:T(1,128)}), f32[128,1,1280]{2,1,0:T(1,128)}, u32[]{:S(2)}, u32[]{:S(2)}) async-start(f32[128,1,1280]{2,1,0:T(1,128)} %bitcast.12), calls=%async_computation.1 | async-start | bytes 1310720 | tf_op jit(solution)/shard_map/all_to_all | solution.py:244
  75.3 8.0 %collective-permute-start.5 = (s32[4,1,40,128]{3,2,1,0:T(8,128)S(1)}, s32[4,1,40,128]{3,2,1,0:T(8,128)S(1)}, u32[]{:S(2)}, u32[]{:S(2)}) collective-permute-start(s32[4,1,40,128]{3,2,1,0:T(8,128)S(1)} %pad_add_fusion.2), channel_id=1, source_target_pairs={{0,1},{1,0},{2,3},{3,2},{4,5},{5,4},{6,7},{7,6},{8,9},{9,8},{10,11... | collective-permute-start | bytes 245768 | tf_op jit(solution)/shard_map/ppermute | solution.py:266
  83.4 11.1 %collective-permute-start.6 = (s32[4,2,40,128]{3,2,1,0:T(8,128)S(1)}, s32[4,2,40,128]{3,2,1,0:T(8,128)S(1)}, u32[]{:S(2)}, u32[]{:S(2)}) collective-permute-start(s32[4,2,40,128]{3,2,1,0:T(8,128)S(1)} %pad_add_fusion.1), channel_id=1, source_target_pairs={{0,2},{1,3},{2,0},{3,1},{4,6},{5,7},{6,4},{7,5},{8,10},{9,11},{10,... | collective-permute-start | bytes 491528 | tf_op jit(solution)/shard_map/ppermute | solution.py:266
  96.1 33.4 %copy-start.3 = (f32[256,256]{1,0:T(8,128)S(1)}, f32[256,256]{1,0:T(8,128)}, u32[]{:S(2)}) copy-start(f32[256,256]{1,0:T(8,128)} %constant.52.clone.table_ref) | copy-start | bytes 786436

commit v5 on v4

--- a/solution.py
+++ b/solution.py
@@ -60,19 +60,17 @@
     return forward.astype(np.float32), back.T.astype(np.float32).copy(), shift.astype(np.float32)
 
 
-def look_up(classes, kappa_ref, drift_ref):
-    kappa = jnp.full(classes.shape, kappa_ref[0], F32)
-    flows = [jnp.full(classes.shape, drift_ref[axis, 0], F32) for axis in range(3)]
+def look_up(classes, class_ref):
+    found = [jnp.full(classes.shape, class_ref[kind, 0], F32) for kind in range(4)]
     for level in range(1, CLASSES):
         match = classes == level
-        kappa = jnp.where(match, kappa_ref[level], kappa)
-        flows = [jnp.where(match, drift_ref[axis, level], flows[axis]) for axis in range(3)]
-    return kappa, [kappa * flow for flow in flows]
-
-
-def local_terms(masked_ref, forcing_ref, classes_ref, mask_ref, kappa_ref, drift_ref, part_ref, side_ref):
-    weight = mask_ref[...].astype(F32)
-    kappa, (flow_x, flow_y, flow_z) = look_up(classes_ref[...], kappa_ref, drift_ref)
+        found = [jnp.where(match, class_ref[kind, level], found[kind]) for kind in range(4)]
+    kappa, *tilts = found
+    return jnp.where(classes == SOLID, 0.0, 1.0), kappa, [kappa * tilt for tilt in tilts]
+
+
+def local_terms(masked_ref, forcing_ref, cells_ref, class_ref, part_ref, side_ref):
+    weight, kappa, (flow_x, flow_y, flow_z) = look_up(cells_ref[...], class_ref)
     row = lax.broadcasted_iota(jnp.int32, (NY, NZ), 0)
     lane = lax.broadcasted_iota(jnp.int32, (NY, NZ), 1)
     side_ref[0] = weight * (kappa - flow_x)
@@ -147,15 +145,13 @@
         out_ref[n] = rows_ref[pl.ds(n, NY, stride=LOCAL), :]
 
 
-def prepare_slot(cells_ref, kappa_ref, drift_ref, shift_ref, coefficient_ref):
+def prepare_slot(cells_ref, class_ref, shift_ref, coefficient_ref):
     edge = lax.broadcasted_iota(jnp.int32, (NX, NZ), 0)
     lane = lax.broadcasted_iota(jnp.int32, (NX, NZ), 1)
     first, second, turn = shift_ref[0], shift_ref[1], shift_ref[2]
 
     def prepare(y, carry):
-        classes = cells_ref[pl.ds(y, NX, stride=WIDE), :]
-        weight = jnp.where(classes == SOLID, 0.0, 1.0)
-        kappa, (flow_x, flow_y, flow_z) = look_up(classes, kappa_ref, drift_ref)
+        weight, kappa, (flow_x, flow_y, flow_z) = look_up(cells_ref[pl.ds(y, NX, stride=WIDE), :], class_ref)
         coefficient_ref[0, y] = jnp.where(edge == NX - 1, 0.0, kappa - flow_x)
         coefficient_ref[1, y] = jnp.where(edge == 0, 0.0, kappa + flow_x)
         coefficient_ref[2, y] = kappa - flow_y
@@ -252,14 +248,17 @@
     classes = classes.reshape(NY, NZ)
     open_mask = open_mask.reshape(NY, NZ)
 
-    masked = iterate * open_mask.astype(F32)
+    cells = lax.optimization_barrier(jnp.where(open_mask == 1, classes, SOLID))
+    masked = iterate * (cells != SOLID).astype(F32)
+    per_class = jnp.concatenate([diffusivity[None], drift])
     up = [(i, i + 1) for i in range(NX - 1)]
     down = [(j, i) for i, j in up]
     west = lax.ppermute(masked, SPACE, up)
     east = lax.ppermute(masked, SPACE, down)
     arrived = lax.ppermute(masked[LOCAL - 1], TM, [(i, i + 1) for i in range(GROUPS - 1)])
 
-    cells = jnp.pad(jnp.where(open_mask == 1, classes, SOLID), ((HALO, HALO), (0, 0)), constant_values=SOLID)
+    plane = cells
+    cells = jnp.pad(cells, ((HALO, HALO), (0, 0)), constant_values=SOLID)
     cells = lax.dynamic_slice_in_dim(cells, lax.axis_index(("yh", "zh")) * SPAN, WIDE, 0)
     cells = cells.reshape(1, 1, WIDE, NZ)
     for axis, dim, bit in (("yl", 0, 1), ("yl", 0, 2), ("x", 1, 1), ("x", 1, 2)):
@@ -272,8 +271,8 @@
     part, side = call(
         local_terms,
         (shape(LOCAL, NY, NZ), shape(3, NY, NZ)),
-        [VMEM] * 4 + [SMEM] * 2,
-    )(masked, forcing, classes, open_mask, diffusivity, drift)
+        [VMEM] * 3 + [SMEM],
+    )(masked, forcing, plane, per_class)
     first = (lax.axis_index(TM) == 0).astype(jnp.int32).reshape(1)
     residual, sent = call(
         finish_residual,
@@ -285,7 +284,7 @@
     sent = call(to_frequencies, shape(SLOTS * 2 * WIDE_EACH, NZ), [VMEM] * 2)(steps, jnp.asarray(forward))
     spectrum = exchange(sent.reshape(SLOTS, 1, 2 * WIDE_EACH * NZ), BLOCK).reshape(SLOTS * 2 * WIDE_EACH, NZ)
     mine = lax.dynamic_slice_in_dim(jnp.asarray(shift), lax.axis_index(BLOCK), 1, 0).reshape(4)
-    coefficient = call(prepare_slot, shape(9, WIDE, NX, NZ), [VMEM] + [SMEM] * 3)(cells, diffusivity, drift, mine)
+    coefficient = call(prepare_slot, shape(9, WIDE, NX, NZ), [VMEM] + [SMEM] * 2)(cells, per_class, mine)
     sent = call(
         solve_slot,
         shape(SLOTS * 2 * EACH, NZ),

time: 161 us -> 161 us (level)
  local copies, waits for them, and re-layouts: 5.65 us -> 2.61 us
  waiting for transfers between devices: 33.3 us -> 35.7 us
    unnamed x24 -> x8, local copies, waits for them, and re-layouts: 4.93 us -> 1.89 us
    ppermute x1, waiting for transfers between devices: 3.22 us -> 5.55 us  [local(): west = lax.ppermute(masked, SPACE, up)]
where the time goes in v5:
time: 161 us; the launch traced here: 160 us
  blocking collectives  57.2 us (36%)
  starting transfers between devices  48.5 us (30%)
  waiting for transfers between devices  35.7 us (22%)
  Pallas kernels  12.2 us (8%)
  other arithmetic  2.82 us (2%)
  local copies, waits for them, and re-layouts  2.61 us (2%)
    all_to_all x2, blocking collectives, exchange(): return lax.all_to_all(value, axes, split_axis=0, concat_axis=0, tiled=True)  57.2 us
    all_to_all x2, starting transfers between devices, exchange(): return lax.all_to_all(value, axes, split_axis=0, concat_axis=0, tiled=True)  25.4 us
    ppermute x4, waiting for transfers between devices, local(): other = lax.ppermute(cells, axis, [(i, i ^ bit) for i in range(4)])  23.4 us
    ppermute x4, starting transfers between devices, local(): other = lax.ppermute(cells, axis, [(i, i ^ bit) for i in range(4)])  13.9 us
    all_to_all x2, waiting for transfers between devices, exchange(): return lax.all_to_all(value, axes, split_axis=0, concat_axis=0, tiled=True)  5.56 us
    ppermute x1, waiting for transfers between devices, local(): west = lax.ppermute(masked, SPACE, up)  5.55 us
    pallas_call x1, Pallas kernels, local(): call(solve_slot, shape(SLOTS * 2 * EACH, NZ), [VMEM] * 2, scratch=[pltpu....  5.1 us
    ppermute x1, starting transfers between devices, local(): east = lax.ppermute(masked, SPACE, down)  4.55 us
  transfers between devices with their start and end apart: 9, of which 6 were waited for; matrix products, arithmetic and copies ran while one was open for 1% of the time, Pallas kernels for 3%

profile of v5, /device:TPU:8, one launch (start us, length us, event | category | flops | bytes accessed | tf_op | source)
XLA Modules:
  0.0 160.0 jit_solution(12937805708475144118)
XLA Ops:
  0.6 0.9 select_bitcast_fusion.cells_ref
  1.5 0.0 copy-start.2
  1.5 1.1 bitcast_multiply_fusion.masked_ref
  2.7 3.4 %collective-permute-start.1 = (f32[8,128,128]{2,1,0:T(8,128)S(1)}, f32[8,128,128]{2,1,0:T(8,128)S(1)}, u32[]{:S(2)}, u32[]{:S(2)}) collective-permute-start(f32[8,128,128]{2,1,0:T(8,128)S(1)} %bitcast_multiply_fusion.masked_ref), channel_id=1, source_target_pairs={{0,1},{1,2},{2,3},{3,4},{4,5},{5,6},{6,7},{7,8},{8,9},{9,10},{10,1... | collective-permute-start | bytes 1572872 | tf_op jit(solution)/shard_map/ppermute | solution.py:256
  6.1 4.6 %collective-permute-start = (f32[8,128,128]{2,1,0:T(8,128)S(1)}, f32[8,128,128]{2,1,0:T(8,128)S(1)}, u32[]{:S(2)}, u32[]{:S(2)}) collective-permute-start(f32[8,128,128]{2,1,0:T(8,128)S(1)} %bitcast_multiply_fusion.masked_ref), channel_id=1, source_target_pairs={{1,0},{2,1},{3,2},{4,3},{5,4},{6,5},{7,6},{8,7},{9,8},{10,9},{11,1... | collective-permute-start | bytes 1572872 | tf_op jit(solution)/shard_map/ppermute | solution.py:257
  10.7 1.3 collective-permute-start.2
  12.0 0.7 pad_maximum_fusion.class_ref
  12.7 1.0 copy-done
  13.7 1.1 shard_map.113
  14.8 5.5 %collective-permute-done.1.west_ref = f32[8,128,128]{2,1,0:T(8,128)S(1)} collective-permute-done((f32[8,128,128]{2,1,0:T(8,128)S(1)}, f32[8,128,128]{2,1,0:T(8,128)S(1)}, u32[]{:S(2)}, u32[]{:S(2)}) %collective-permute-start.1) | collective-permute-done | bytes 524320 | tf_op jit(solution)/shard_map/ppermute | solution.py:256
  20.3 1.2 collective-permute-done.east_ref
  21.5 0.8 copy-done.3
  22.4 1.3 shard_map.114
  23.6 16.5 %all-to-all-start = ((f32[32,40,128]{2,1,0:T(8,128)}), f32[32,40,128]{2,1,0:T(8,128)S(1)}, u32[]{:S(2)}, u32[]{:S(2)}) async-start(f32[32,40,128]{2,1,0:T(8,128)} %bitcast.9), calls=%async_computation | async-start | bytes 1310720 | tf_op jit(solution)/shard_map/all_to_all | solution.py:240
  40.2 1.9 %collective-permute-start.3 = (s32[1,1,40,128]{3,2,1,0:T(8,128)S(1)}, s32[1,1,40,128]{3,2,1,0:T(8,128)S(1)}, u32[]{:S(2)}, u32[]{:S(2)}) collective-permute-start(s32[1,1,40,128]{3,2,1,0:T(8,128)S(1)} %fusion), channel_id=1, source_target_pairs={{0,4},{4,0},{8,12},{12,8},{1,5},{5,1},{9,13},{13,9},{2,6},{6,2},{1... | collective-permute-start | bytes 61448 | tf_op jit(solution)/shard_map/ppermute | solution.py:265
  42.1 13.3 %collective-permute-done.3 = s32[1,1,40,128]{3,2,1,0:T(8,128)S(1)} collective-permute-done((s32[1,1,40,128]{3,2,1,0:T(8,128)S(1)}, s32[1,1,40,128]{3,2,1,0:T(8,128)S(1)}, u32[]{:S(2)}, u32[]{:S(2)}) %collective-permute-start.3) | collective-permute-done | bytes 20512 | tf_op jit(solution)/shard_map/ppermute | solution.py:265
  55.4 3.8 %collective-permute-start.4 = (s32[2,1,40,128]{3,2,1,0:T(8,128)S(1)}, s32[2,1,40,128]{3,2,1,0:T(8,128)S(1)}, u32[]{:S(2)}, u32[]{:S(2)}) collective-permute-start(s32[2,1,40,128]{3,2,1,0:T(8,128)S(1)} %pad_add_fusion.3), channel_id=1, source_target_pairs={{0,8},{4,12},{8,0},{12,4},{1,9},{5,13},{9,1},{13,5},{2,10},{6,14},... | collective-permute-start | bytes 122888 | tf_op jit(solution)/shard_map/ppermute | solution.py:265
  59.2 5.6 %all-to-all-done = f32[32,40,128]{2,1,0:T(8,128)S(1)} async-done(((f32[32,40,128]{2,1,0:T(8,128)}), f32[32,40,128]{2,1,0:T(8,128)S(1)}, u32[]{:S(2)}, u32[]{:S(2)}) %all-to-all-start) | async-done | bytes 655392 | tf_op jit(solution)/shard_map/all_to_all | solution.py:240
  64.8 1.6 %shard_map.115 = f32[1280,128]{1,0:T(8,128)} custom-call(f32[32,5,8,128]{3,2,1,0:T(8,128)S(1)} %bitcast.31, f32[256,256]{1,0:T(8,128)S(1)} %copy-done.2), custom_call_target="tpu_custom_call" | custom-call | flops 1000000 | bytes 2000000 | tf_op jit(solution)/shard_map/pallas_call | solution.py:284
  66.4 8.9 %all-to-all-start.1 = ((f32[128,1,1280]{2,1,0:T(1,128)}), f32[128,1,1280]{2,1,0:T(1,128)}, u32[]{:S(2)}, u32[]{:S(2)}) async-start(f32[128,1,1280]{2,1,0:T(1,128)} %bitcast.11), calls=%async_computation.1 | async-start | bytes 1310720 | tf_op jit(solution)/shard_map/all_to_all | solution.py:240
  75.3 3.4 %collective-permute-start.5 = (s32[4,1,40,128]{3,2,1,0:T(8,128)S(1)}, s32[4,1,40,128]{3,2,1,0:T(8,128)S(1)}, u32[]{:S(2)}, u32[]{:S(2)}) collective-permute-start(s32[4,1,40,128]{3,2,1,0:T(8,128)S(1)} %pad_add_fusion.2), channel_id=1, source_target_pairs={{0,1},{1,0},{2,3},{3,2},{4,5},{5,4},{6,7},{7,6},{8,9},{9,8},{10,11... | collective-permute-start | bytes 245768 | tf_op jit(solution)/shard_map/ppermute | solution.py:265
  78.7 4.6 %collective-permute-done.5 = s32[4,1,40,128]{3,2,1,0:T(8,128)S(1)} collective-permute-done((s32[4,1,40,128]{3,2,1,0:T(8,128)S(1)}, s32[4,1,40,128]{3,2,1,0:T(8,128)S(1)}, u32[]{:S(2)}, u32[]{:S(2)}) %collective-permute-start.5) | collective-permute-done | bytes 81952 | tf_op jit(solution)/shard_map/ppermute | solution.py:265
  83.4 4.8 %collective-permute-start.6 = (s32[4,2,40,128]{3,2,1,0:T(8,128)S(1)}, s32[4,2,40,128]{3,2,1,0:T(8,128)S(1)}, u32[]{:S(2)}, u32[]{:S(2)}) collective-permute-start(s32[4,2,40,128]{3,2,1,0:T(8,128)S(1)} %pad_add_fusion.1), channel_id=1, source_target_pairs={{0,2},{1,3},{2,0},{3,1},{4,6},{5,7},{6,4},{7,5},{8,10},{9,11},{10,... | collective-permute-start | bytes 491528 | tf_op jit(solution)/shard_map/ppermute | solution.py:265
  88.2 0.7 dynamic-slice_bitcast_fusion.shift_ref
  88.9 5.5 %collective-permute-done.6 = s32[4,2,40,128]{3,2,1,0:T(8,128)S(1)} collective-permute-done((s32[4,2,40,128]{3,2,1,0:T(8,128)S(1)}, s32[4,2,40,128]{3,2,1,0:T(8,128)S(1)}, u32[]{:S(2)}, u32[]{:S(2)}) %collective-permute-start.6) | collective-permute-done | bytes 163872 | tf_op jit(solution)/shard_map/ppermute | solution.py:265
  94.5 1.6 shard_map.116.coefficient_ref
  96.1 0.0 copy-start.1
  96.1 5.1 %shard_map.117 = f32[1024,128]{1,0:T(8,128)S(1)} custom-call(f32[1280,128]{1,0:T(8,128)} %bitcast.12.spectrum_ref, f32[9,40,16,128]{3,2,1,0:T(8,128)S(1)} %shard_map.116.coefficient_ref), custom_call_target="tpu_custom_call" | custom-call | flops 1000000 | bytes 2000000 | tf_op jit(solution)/shard_map/pallas_call | solution.py:288
  101.2 28.2 %all_to_all.36 = f32[128,8,128]{2,1,0:T(8,128)S(1)} all-to-all(f32[128,8,128]{2,1,0:T(8,128)S(1)} %bitcast.35), channel_id=1, replica_groups=mesh['yh'=2,'zh'=2,'zl'=4,'core'=2,'yl'=4,'x'=4] {'zl','core','yl','x'}, dimensions={0} | all-to-all | bytes 1048576 | tf_op jit(solution)/shard_map/all_to_all | solution.py:240
  129.4 0.7 shard_map.118
  130.1 29.0 %all_to_all.37 = f32[32,32,128]{2,1,0:T(8,128)S(1)} all-to-all(f32[32,32,128]{2,1,0:T(8,128)S(1)} %bitcast.33), channel_id=1, replica_groups=mesh['yh'=2,'zh'=2,'zl'=4,'core'=2,'yl'=4,'x'=4] {'yh','zh','zl','core'}, dimensions={0} | all-to-all | bytes 1048576 | tf_op jit(solution)/shard_map/all_to_all | solution.py:240
  159.1 0.9 shard_map.119
  (18 shorter events, 0.2 us)
Async XLA Ops:
  1.5 63.3 %copy-start.2 = (f32[256,256]{1,0:T(8,128)S(1)}, f32[256,256]{1,0:T(8,128)}, u32[]{:S(2)}) copy-start(f32[256,256]{1,0:T(8,128)} %constant.51.clone.table_ref) | copy-start | bytes 786436
  2.7 17.7 %collective-permute-start.1 = (f32[8,128,128]{2,1,0:T(8,128)S(1)}, f32[8,128,128]{2,1,0:T(8,128)S(1)}, u32[]{:S(2)}, u32[]{:S(2)}) collective-permute-start(f32[8,128,128]{2,1,0:T(8,128)S(1)} %bitcast_multiply_fusion.masked_ref), channel_id=1, source_target_pairs={{0,1},{1,2},{2,3},{3,4},{4,5},{5,6},{6,7},{7,8},{8,9},{9,10},{10,1... | collective-permute-start | bytes 1572872 | tf_op jit(solution)/shard_map/ppermute | solution.py:256
  6.1 15.4 %collective-permute-start = (f32[8,128,128]{2,1,0:T(8,128)S(1)}, f32[8,128,128]{2,1,0:T(8,128)S(1)}, u32[]{:S(2)}, u32[]{:S(2)}) collective-permute-start(f32[8,128,128]{2,1,0:T(8,128)S(1)} %bitcast_multiply_fusion.masked_ref), channel_id=1, source_target_pairs={{1,0},{2,1},{3,2},{4,3},{5,4},{6,5},{7,6},{8,7},{9,8},{10,9},{11,1... | collective-permute-start | bytes 1572872 | tf_op jit(solution)/shard_map/ppermute | solution.py:257
  10.7 4.1 %collective-permute-start.2 = (f32[128,128]{1,0:T(8,128)S(1)}, f32[128,128]{1,0:T(8,128)S(1)}, u32[]{:S(2)}, u32[]{:S(2)}) collective-permute-start(f32[128,128]{1,0:T(8,128)S(1)} %slice_bitcast_fusion), channel_id=1, source_target_pairs={{0,16},{16,32},{32,48},{48,64},{64,80},{80,96},{96,112},{112,128},... | collective-permute-start | bytes 196616 | tf_op jit(solution)/shard_map/ppermute | solution.py:258
  12.7 1.0 copy-start
  21.5 0.8 copy-start.3
  23.6 41.2 %all-to-all-start = ((f32[32,40,128]{2,1,0:T(8,128)}), f32[32,40,128]{2,1,0:T(8,128)S(1)}, u32[]{:S(2)}, u32[]{:S(2)}) async-start(f32[32,40,128]{2,1,0:T(8,128)} %bitcast.9), calls=%async_computation | async-start | bytes 1310720 | tf_op jit(solution)/shard_map/all_to_all | solution.py:240
  40.2 15.2 %collective-permute-start.3 = (s32[1,1,40,128]{3,2,1,0:T(8,128)S(1)}, s32[1,1,40,128]{3,2,1,0:T(8,128)S(1)}, u32[]{:S(2)}, u32[]{:S(2)}) collective-permute-start(s32[1,1,40,128]{3,2,1,0:T(8,128)S(1)} %fusion), channel_id=1, source_target_pairs={{0,4},{4,0},{8,12},{12,8},{1,5},{5,1},{9,13},{13,9},{2,6},{6,2},{1... | collective-permute-start | bytes 61448 | tf_op jit(solution)/shard_map/ppermute | solution.py:265
  55.4 19.9 %collective-permute-start.4 = (s32[2,1,40,128]{3,2,1,0:T(8,128)S(1)}, s32[2,1,40,128]{3,2,1,0:T(8,128)S(1)}, u32[]{:S(2)}, u32[]{:S(2)}) collective-permute-start(s32[2,1,40,128]{3,2,1,0:T(8,128)S(1)} %pad_add_fusion.3), channel_id=1, source_target_pairs={{0,8},{4,12},{8,0},{12,4},{1,9},{5,13},{9,1},{13,5},{2,10},{6,14},... | collective-permute-start | bytes 122888 | tf_op jit(solution)/shard_map/ppermute | solution.py:265
  66.4 29.7 %all-to-all-start.1 = ((f32[128,1,1280]{2,1,0:T(1,128)}), f32[128,1,1280]{2,1,0:T(1,128)}, u32[]{:S(2)}, u32[]{:S(2)}) async-start(f32[128,1,1280]{2,1,0:T(1,128)} %bitcast.11), calls=%async_computation.1 | async-start | bytes 1310720 | tf_op jit(solution)/shard_map/all_to_all | solution.py:240
  75.3 8.0 %collective-permute-start.5 = (s32[4,1,40,128]{3,2,1,0:T(8,128)S(1)}, s32[4,1,40,128]{3,2,1,0:T(8,128)S(1)}, u32[]{:S(2)}, u32[]{:S(2)}) collective-permute-start(s32[4,1,40,128]{3,2,1,0:T(8,128)S(1)} %pad_add_fusion.2), channel_id=1, source_target_pairs={{0,1},{1,0},{2,3},{3,2},{4,5},{5,4},{6,7},{7,6},{8,9},{9,8},{10,11... | collective-permute-start | bytes 245768 | tf_op jit(solution)/shard_map/ppermute | solution.py:265
  83.4 11.1 %collective-permute-start.6 = (s32[4,2,40,128]{3,2,1,0:T(8,128)S(1)}, s32[4,2,40,128]{3,2,1,0:T(8,128)S(1)}, u32[]{:S(2)}, u32[]{:S(2)}) collective-permute-start(s32[4,2,40,128]{3,2,1,0:T(8,128)S(1)} %pad_add_fusion.1), channel_id=1, source_target_pairs={{0,2},{1,3},{2,0},{3,1},{4,6},{5,7},{6,4},{7,5},{8,10},{9,11},{10,... | collective-permute-start | bytes 491528 | tf_op jit(solution)/shard_map/ppermute | solution.py:265
  96.1 33.4 %copy-start.1 = (f32[256,256]{1,0:T(8,128)S(1)}, f32[256,256]{1,0:T(8,128)}, u32[]{:S(2)}) copy-start(f32[256,256]{1,0:T(8,128)} %constant.53.clone.table_ref) | copy-start | bytes 786436

commit v6 on v5

--- a/solution.py
+++ b/solution.py
@@ -69,7 +69,7 @@
     return jnp.where(classes == SOLID, 0.0, 1.0), kappa, [kappa * tilt for tilt in tilts]
 
 
-def local_terms(masked_ref, forcing_ref, cells_ref, class_ref, part_ref, side_ref):
+def local_terms(masked_ref, forcing_ref, cells_ref, start_ref, class_ref, first_ref, part_ref, side_ref):
     weight, kappa, (flow_x, flow_y, flow_z) = look_up(cells_ref[...], class_ref)
     row = lax.broadcasted_iota(jnp.int32, (NY, NZ), 0)
     lane = lax.broadcasted_iota(jnp.int32, (NY, NZ), 1)
@@ -86,19 +86,16 @@
         total = weight * forcing_ref[n] - middle * here
         total += north * pltpu.roll(here, NY - 1, 0) + south * pltpu.roll(here, 1, 0)
         total += upper * pltpu.roll(here, NZ - 1, 1) + lower * pltpu.roll(here, 1, 1)
-        if n:
-            total += masked_ref[n - 1]
+        total += masked_ref[n - 1] if n else weight * jnp.where(first_ref[0] == 1, start_ref[...], 0.0)
         part_ref[n] = total
 
 
-def finish_residual(part_ref, side_ref, east_ref, west_ref, start_ref, arrived_ref, first_ref, residual_ref, sent_ref):
+def finish_residual(part_ref, side_ref, east_ref, west_ref, arrived_ref, residual_ref, sent_ref):
     east, west, weight = side_ref[0], side_ref[1], side_ref[2]
-    begins = first_ref[0]
-    step_before = weight * jnp.where(begins == 1, start_ref[...], arrived_ref[...])
     for n in range(LOCAL):
         total = part_ref[n] + east * east_ref[n] + west * west_ref[n]
         if n == 0:
-            total += step_before
+            total += weight * arrived_ref[...]
         residual_ref[n] = total
         for quarter in range(QUARTERS):
             low = max(quarter * SPAN - HALO, 0)
@@ -268,17 +265,17 @@
         cells = jnp.concatenate(pair, axis=dim)
     cells = cells.reshape(NX * WIDE, NZ)
 
+    first = (lax.axis_index(TM) == 0).astype(jnp.int32).reshape(1)
     part, side = call(
         local_terms,
         (shape(LOCAL, NY, NZ), shape(3, NY, NZ)),
-        [VMEM] * 3 + [SMEM],
-    )(masked, forcing, plane, per_class)
-    first = (lax.axis_index(TM) == 0).astype(jnp.int32).reshape(1)
+        [VMEM] * 4 + [SMEM] * 2,
+    )(masked, forcing, plane, start_field, per_class, first)
     residual, sent = call(
         finish_residual,
         (shape(LOCAL, NY, NZ), shape(QUARTERS * WIDE * LOCAL, NZ)),
-        [VMEM] * 6 + [SMEM],
-    )(part, side, east, west, start_field, arrived, first)
+        [VMEM] * 5,
+    )(part, side, east, west, arrived)
 
     steps = exchange(sent, TM).reshape(GROUPS, WIDE_EACH, LOCAL, NZ)
     sent = call(to_frequencies, shape(SLOTS * 2 * WIDE_EACH, NZ), [VMEM] * 2)(steps, jnp.asarray(forward))

time: 161 us -> 160 us (level)
  no operation moved by 1% of the time
where the time goes in v6:
time: 160 us; the launch traced here: 159 us
  blocking collectives  57.2 us (36%)
  starting transfers between devices  48.5 us (30%)
  waiting for transfers between devices  34.8 us (22%)
  Pallas kernels  12.2 us (8%)
  other arithmetic  2.82 us (2%)
  local copies, waits for them, and re-layouts  2.61 us (2%)
    all_to_all x2, blocking collectives, exchange(): return lax.all_to_all(value, axes, split_axis=0, concat_axis=0, tiled=True)  57.2 us
    all_to_all x2, starting transfers between devices, exchange(): return lax.all_to_all(value, axes, split_axis=0, concat_axis=0, tiled=True)  25.4 us
    ppermute x4, waiting for transfers between devices, local(): other = lax.ppermute(cells, axis, [(i, i ^ bit) for i in range(4)])  23.4 us
    ppermute x4, starting transfers between devices, local(): other = lax.ppermute(cells, axis, [(i, i ^ bit) for i in range(4)])  13.9 us
    all_to_all x2, waiting for transfers between devices, exchange(): return lax.all_to_all(value, axes, split_axis=0, concat_axis=0, tiled=True)  5.56 us
    pallas_call x1, Pallas kernels, local(): call(solve_slot, shape(SLOTS * 2 * EACH, NZ), [VMEM] * 2, scratch=[pltpu....  5.1 us
    ppermute x1, waiting for transfers between devices, local(): west = lax.ppermute(masked, SPACE, up)  4.68 us
    ppermute x1, starting transfers between devices, local(): east = lax.ppermute(masked, SPACE, down)  4.55 us
  transfers between devices with their start and end apart: 9, of which 6 were waited for; matrix products, arithmetic and copies ran while one was open for 1% of the time, Pallas kernels for 3%

profile of v6, /device:TPU:8, one launch (start us, length us, event | category | flops | bytes accessed | tf_op | source)
XLA Modules:
  0.0 159.1 jit_solution(11313416271029481381)
XLA Ops:
  0.6 0.9 select_bitcast_fusion.cells_ref
  1.5 0.0 copy-start.2
  1.5 1.1 bitcast_multiply_fusion.masked_ref
  2.7 3.4 %collective-permute-start.1 = (f32[8,128,128]{2,1,0:T(8,128)S(1)}, f32[8,128,128]{2,1,0:T(8,128)S(1)}, u32[]{:S(2)}, u32[]{:S(2)}) collective-permute-start(f32[8,128,128]{2,1,0:T(8,128)S(1)} %bitcast_multiply_fusion.masked_ref), channel_id=1, source_target_pairs={{0,1},{1,2},{2,3},{3,4},{4,5},{5,6},{6,7},{7,8},{8,9},{9,10},{10,1... | collective-permute-start | bytes 1572872 | tf_op jit(solution)/shard_map/ppermute | solution.py:253
  6.1 4.6 %collective-permute-start = (f32[8,128,128]{2,1,0:T(8,128)S(1)}, f32[8,128,128]{2,1,0:T(8,128)S(1)}, u32[]{:S(2)}, u32[]{:S(2)}) collective-permute-start(f32[8,128,128]{2,1,0:T(8,128)S(1)} %bitcast_multiply_fusion.masked_ref), channel_id=1, source_target_pairs={{1,0},{2,1},{3,2},{4,3},{5,4},{6,5},{7,6},{8,7},{9,8},{10,9},{11,1... | collective-permute-start | bytes 1572872 | tf_op jit(solution)/shard_map/ppermute | solution.py:254
  10.7 1.3 collective-permute-start.2
  12.0 0.7 pad_maximum_fusion.class_ref
  12.7 1.0 copy-done
  13.7 0.8 copy-done.3
  14.5 1.1 shard_map.113
  15.7 4.7 %collective-permute-done.1.west_ref = f32[8,128,128]{2,1,0:T(8,128)S(1)} collective-permute-done((f32[8,128,128]{2,1,0:T(8,128)S(1)}, f32[8,128,128]{2,1,0:T(8,128)S(1)}, u32[]{:S(2)}, u32[]{:S(2)}) %collective-permute-start.1) | collective-permute-done | bytes 524320 | tf_op jit(solution)/shard_map/ppermute | solution.py:253
  20.3 1.2 collective-permute-done.east_ref
  21.5 1.2 shard_map.114
  22.8 16.5 %all-to-all-start = ((f32[32,40,128]{2,1,0:T(8,128)}), f32[32,40,128]{2,1,0:T(8,128)S(1)}, u32[]{:S(2)}, u32[]{:S(2)}) async-start(f32[32,40,128]{2,1,0:T(8,128)} %bitcast.9), calls=%async_computation | async-start | bytes 1310720 | tf_op jit(solution)/shard_map/all_to_all | solution.py:237
  39.3 1.9 %collective-permute-start.3 = (s32[1,1,40,128]{3,2,1,0:T(8,128)S(1)}, s32[1,1,40,128]{3,2,1,0:T(8,128)S(1)}, u32[]{:S(2)}, u32[]{:S(2)}) collective-permute-start(s32[1,1,40,128]{3,2,1,0:T(8,128)S(1)} %fusion), channel_id=1, source_target_pairs={{0,4},{4,0},{8,12},{12,8},{1,5},{5,1},{9,13},{13,9},{2,6},{6,2},{1... | collective-permute-start | bytes 61448 | tf_op jit(solution)/shard_map/ppermute | solution.py:262
  41.3 13.3 %collective-permute-done.3 = s32[1,1,40,128]{3,2,1,0:T(8,128)S(1)} collective-permute-done((s32[1,1,40,128]{3,2,1,0:T(8,128)S(1)}, s32[1,1,40,128]{3,2,1,0:T(8,128)S(1)}, u32[]{:S(2)}, u32[]{:S(2)}) %collective-permute-start.3) | collective-permute-done | bytes 20512 | tf_op jit(solution)/shard_map/ppermute | solution.py:262
  54.6 3.8 %collective-permute-start.4 = (s32[2,1,40,128]{3,2,1,0:T(8,128)S(1)}, s32[2,1,40,128]{3,2,1,0:T(8,128)S(1)}, u32[]{:S(2)}, u32[]{:S(2)}) collective-permute-start(s32[2,1,40,128]{3,2,1,0:T(8,128)S(1)} %pad_add_fusion.3), channel_id=1, source_target_pairs={{0,8},{4,12},{8,0},{12,4},{1,9},{5,13},{9,1},{13,5},{2,10},{6,14},... | collective-permute-start | bytes 122888 | tf_op jit(solution)/shard_map/ppermute | solution.py:262
  58.4 5.6 %all-to-all-done = f32[32,40,128]{2,1,0:T(8,128)S(1)} async-done(((f32[32,40,128]{2,1,0:T(8,128)}), f32[32,40,128]{2,1,0:T(8,128)S(1)}, u32[]{:S(2)}, u32[]{:S(2)}) %all-to-all-start) | async-done | bytes 655392 | tf_op jit(solution)/shard_map/all_to_all | solution.py:237
  63.9 1.6 %shard_map.115 = f32[1280,128]{1,0:T(8,128)} custom-call(f32[32,5,8,128]{3,2,1,0:T(8,128)S(1)} %bitcast.31, f32[256,256]{1,0:T(8,128)S(1)} %copy-done.2), custom_call_target="tpu_custom_call" | custom-call | flops 1000000 | bytes 2000000 | tf_op jit(solution)/shard_map/pallas_call | solution.py:281
  65.6 8.9 %all-to-all-start.1 = ((f32[128,1,1280]{2,1,0:T(1,128)}), f32[128,1,1280]{2,1,0:T(1,128)}, u32[]{:S(2)}, u32[]{:S(2)}) async-start(f32[128,1,1280]{2,1,0:T(1,128)} %bitcast.11), calls=%async_computation.1 | async-start | bytes 1310720 | tf_op jit(solution)/shard_map/all_to_all | solution.py:237
  74.5 3.4 %collective-permute-start.5 = (s32[4,1,40,128]{3,2,1,0:T(8,128)S(1)}, s32[4,1,40,128]{3,2,1,0:T(8,128)S(1)}, u32[]{:S(2)}, u32[]{:S(2)}) collective-permute-start(s32[4,1,40,128]{3,2,1,0:T(8,128)S(1)} %pad_add_fusion.2), channel_id=1, source_target_pairs={{0,1},{1,0},{2,3},{3,2},{4,5},{5,4},{6,7},{7,6},{8,9},{9,8},{10,11... | collective-permute-start | bytes 245768 | tf_op jit(solution)/shard_map/ppermute | solution.py:262
  77.9 4.6 %collective-permute-done.5 = s32[4,1,40,128]{3,2,1,0:T(8,128)S(1)} collective-permute-done((s32[4,1,40,128]{3,2,1,0:T(8,128)S(1)}, s32[4,1,40,128]{3,2,1,0:T(8,128)S(1)}, u32[]{:S(2)}, u32[]{:S(2)}) %collective-permute-start.5) | collective-permute-done | bytes 81952 | tf_op jit(solution)/shard_map/ppermute | solution.py:262
  82.5 4.8 %collective-permute-start.6 = (s32[4,2,40,128]{3,2,1,0:T(8,128)S(1)}, s32[4,2,40,128]{3,2,1,0:T(8,128)S(1)}, u32[]{:S(2)}, u32[]{:S(2)}) collective-permute-start(s32[4,2,40,128]{3,2,1,0:T(8,128)S(1)} %pad_add_fusion.1), channel_id=1, source_target_pairs={{0,2},{1,3},{2,0},{3,1},{4,6},{5,7},{6,4},{7,5},{8,10},{9,11},{10,... | collective-permute-start | bytes 491528 | tf_op jit(solution)/shard_map/ppermute | solution.py:262
  87.4 0.7 dynamic-slice_bitcast_fusion.shift_ref
  88.1 5.5 %collective-permute-done.6 = s32[4,2,40,128]{3,2,1,0:T(8,128)S(1)} collective-permute-done((s32[4,2,40,128]{3,2,1,0:T(8,128)S(1)}, s32[4,2,40,128]{3,2,1,0:T(8,128)S(1)}, u32[]{:S(2)}, u32[]{:S(2)}) %collective-permute-start.6) | collective-permute-done | bytes 163872 | tf_op jit(solution)/shard_map/ppermute | solution.py:262
  93.6 1.6 shard_map.116.coefficient_ref
  95.2 0.0 copy-start.1
  95.2 5.1 %shard_map.117 = f32[1024,128]{1,0:T(8,128)S(1)} custom-call(f32[1280,128]{1,0:T(8,128)} %bitcast.12.spectrum_ref, f32[9,40,16,128]{3,2,1,0:T(8,128)S(1)} %shard_map.116.coefficient_ref), custom_call_target="tpu_custom_call" | custom-call | flops 1000000 | bytes 2000000 | tf_op jit(solution)/shard_map/pallas_call | solution.py:285
  100.3 28.2 %all_to_all.36 = f32[128,8,128]{2,1,0:T(8,128)S(1)} all-to-all(f32[128,8,128]{2,1,0:T(8,128)S(1)} %bitcast.35), channel_id=1, replica_groups=mesh['yh'=2,'zh'=2,'zl'=4,'core'=2,'yl'=4,'x'=4] {'zl','core','yl','x'}, dimensions={0} | all-to-all | bytes 1048576 | tf_op jit(solution)/shard_map/all_to_all | solution.py:237
  128.6 0.7 shard_map.118
  129.2 29.0 %all_to_all.37 = f32[32,32,128]{2,1,0:T(8,128)S(1)} all-to-all(f32[32,32,128]{2,1,0:T(8,128)S(1)} %bitcast.33), channel_id=1, replica_groups=mesh['yh'=2,'zh'=2,'zl'=4,'core'=2,'yl'=4,'x'=4] {'yh','zh','zl','core'}, dimensions={0} | all-to-all | bytes 1048576 | tf_op jit(solution)/shard_map/all_to_all | solution.py:237
  158.2 0.9 shard_map.119
  (18 shorter events, 0.2 us)
Async XLA Ops:
  1.5 62.4 %copy-start.2 = (f32[256,256]{1,0:T(8,128)S(1)}, f32[256,256]{1,0:T(8,128)}, u32[]{:S(2)}) copy-start(f32[256,256]{1,0:T(8,128)} %constant.51.clone.table_ref) | copy-start | bytes 786436
  2.7 17.7 %collective-permute-start.1 = (f32[8,128,128]{2,1,0:T(8,128)S(1)}, f32[8,128,128]{2,1,0:T(8,128)S(1)}, u32[]{:S(2)}, u32[]{:S(2)}) collective-permute-start(f32[8,128,128]{2,1,0:T(8,128)S(1)} %bitcast_multiply_fusion.masked_ref), channel_id=1, source_target_pairs={{0,1},{1,2},{2,3},{3,4},{4,5},{5,6},{6,7},{7,8},{8,9},{9,10},{10,1... | collective-permute-start | bytes 1572872 | tf_op jit(solution)/shard_map/ppermute | solution.py:253
  6.1 15.4 %collective-permute-start = (f32[8,128,128]{2,1,0:T(8,128)S(1)}, f32[8,128,128]{2,1,0:T(8,128)S(1)}, u32[]{:S(2)}, u32[]{:S(2)}) collective-permute-start(f32[8,128,128]{2,1,0:T(8,128)S(1)} %bitcast_multiply_fusion.masked_ref), channel_id=1, source_target_pairs={{1,0},{2,1},{3,2},{4,3},{5,4},{6,5},{7,6},{8,7},{9,8},{10,9},{11,1... | collective-permute-start | bytes 1572872 | tf_op jit(solution)/shard_map/ppermute | solution.py:254
  10.7 5.0 %collective-permute-start.2 = (f32[128,128]{1,0:T(8,128)S(1)}, f32[128,128]{1,0:T(8,128)S(1)}, u32[]{:S(2)}, u32[]{:S(2)}) collective-permute-start(f32[128,128]{1,0:T(8,128)S(1)} %slice_bitcast_fusion), channel_id=1, source_target_pairs={{0,16},{16,32},{32,48},{48,64},{64,80},{80,96},{96,112},{112,128},... | collective-permute-start | bytes 196616 | tf_op jit(solution)/shard_map/ppermute | solution.py:255
  12.7 1.0 copy-start
  13.7 0.8 copy-start.3
  22.8 41.2 %all-to-all-start = ((f32[32,40,128]{2,1,0:T(8,128)}), f32[32,40,128]{2,1,0:T(8,128)S(1)}, u32[]{:S(2)}, u32[]{:S(2)}) async-start(f32[32,40,128]{2,1,0:T(8,128)} %bitcast.9), calls=%async_computation | async-start | bytes 1310720 | tf_op jit(solution)/shard_map/all_to_all | solution.py:237
  39.3 15.2 %collective-permute-start.3 = (s32[1,1,40,128]{3,2,1,0:T(8,128)S(1)}, s32[1,1,40,128]{3,2,1,0:T(8,128)S(1)}, u32[]{:S(2)}, u32[]{:S(2)}) collective-permute-start(s32[1,1,40,128]{3,2,1,0:T(8,128)S(1)} %fusion), channel_id=1, source_target_pairs={{0,4},{4,0},{8,12},{12,8},{1,5},{5,1},{9,13},{13,9},{2,6},{6,2},{1... | collective-permute-start | bytes 61448 | tf_op jit(solution)/shard_map/ppermute | solution.py:262
  54.6 19.9 %collective-permute-start.4 = (s32[2,1,40,128]{3,2,1,0:T(8,128)S(1)}, s32[2,1,40,128]{3,2,1,0:T(8,128)S(1)}, u32[]{:S(2)}, u32[]{:S(2)}) collective-permute-start(s32[2,1,40,128]{3,2,1,0:T(8,128)S(1)} %pad_add_fusion.3), channel_id=1, source_target_pairs={{0,8},{4,12},{8,0},{12,4},{1,9},{5,13},{9,1},{13,5},{2,10},{6,14},... | collective-permute-start | bytes 122888 | tf_op jit(solution)/shard_map/ppermute | solution.py:262
  65.6 29.7 %all-to-all-start.1 = ((f32[128,1,1280]{2,1,0:T(1,128)}), f32[128,1,1280]{2,1,0:T(1,128)}, u32[]{:S(2)}, u32[]{:S(2)}) async-start(f32[128,1,1280]{2,1,0:T(1,128)} %bitcast.11), calls=%async_computation.1 | async-start | bytes 1310720 | tf_op jit(solution)/shard_map/all_to_all | solution.py:237
  74.5 8.0 %collective-permute-start.5 = (s32[4,1,40,128]{3,2,1,0:T(8,128)S(1)}, s32[4,1,40,128]{3,2,1,0:T(8,128)S(1)}, u32[]{:S(2)}, u32[]{:S(2)}) collective-permute-start(s32[4,1,40,128]{3,2,1,0:T(8,128)S(1)} %pad_add_fusion.2), channel_id=1, source_target_pairs={{0,1},{1,0},{2,3},{3,2},{4,5},{5,4},{6,7},{7,6},{8,9},{9,8},{10,11... | collective-permute-start | bytes 245768 | tf_op jit(solution)/shard_map/ppermute | solution.py:262
  82.5 11.1 %collective-permute-start.6 = (s32[4,2,40,128]{3,2,1,0:T(8,128)S(1)}, s32[4,2,40,128]{3,2,1,0:T(8,128)S(1)}, u32[]{:S(2)}, u32[]{:S(2)}) collective-permute-start(s32[4,2,40,128]{3,2,1,0:T(8,128)S(1)} %pad_add_fusion.1), channel_id=1, source_target_pairs={{0,2},{1,3},{2,0},{3,1},{4,6},{5,7},{6,4},{7,5},{8,10},{9,11},{10,... | collective-permute-start | bytes 491528 | tf_op jit(solution)/shard_map/ppermute | solution.py:262
  95.2 33.4 %copy-start.1 = (f32[256,256]{1,0:T(8,128)S(1)}, f32[256,256]{1,0:T(8,128)}, u32[]{:S(2)}) copy-start(f32[256,256]{1,0:T(8,128)} %constant.53.clone.table_ref) | copy-start | bytes 786436

commit v7 on v6

--- a/solution.py
+++ b/solution.py
@@ -258,11 +258,18 @@
     cells = jnp.pad(cells, ((HALO, HALO), (0, 0)), constant_values=SOLID)
     cells = lax.dynamic_slice_in_dim(cells, lax.axis_index(("yh", "zh")) * SPAN, WIDE, 0)
     cells = cells.reshape(1, 1, WIDE, NZ)
-    for axis, dim, bit in (("yl", 0, 1), ("yl", 0, 2), ("x", 1, 1), ("x", 1, 2)):
-        other = lax.ppermute(cells, axis, [(i, i ^ bit) for i in range(4)])
-        upper = (lax.axis_index(axis) & bit) != 0
-        pair = [jnp.where(upper, other, cells), jnp.where(upper, cells, other)]
-        cells = jnp.concatenate(pair, axis=dim)
+    for hop in range(2):
+        other = lax.ppermute(cells, "yl", [(i, i ^ (hop + 1)) for i in range(4)])
+        upper = (lax.axis_index("yl") & (hop + 1)) != 0
+        cells = jnp.concatenate([jnp.where(upper, other, cells), jnp.where(upper, cells, other)], axis=0)
+    column = lax.axis_index("x")
+    held = [cells]
+    for apart in range(1, 4):
+        held.append(lax.ppermute(cells, "x", [(i, i ^ apart) for i in range(4)]))
+    cells = jnp.concatenate(
+        [lax.select_n(column ^ at, *held) for at in range(4)],
+        axis=1,
+    )
     cells = cells.reshape(NX * WIDE, NZ)
 
     first = (lax.axis_index(TM) == 0).astype(jnp.int32).reshape(1)

time: 160 us -> 171 us (1.069)
  waiting for transfers between devices: 34.8 us -> 43 us
  starting transfers between devices: 48.5 us -> 50.7 us
    all_to_all x2, waiting for transfers between devices: 5.56 us -> 22.6 us  [exchange(): return lax.all_to_all(value, axes, split_axis=0, concat_axis=0, tiled=True)]
    ppermute x4 -> x5, waiting for transfers between devices: 23.4 us -> 14.5 us  [the longest x2 10.8 us: local(): other = lax.ppermute(cells, 'yl', [(i, i ^ hop + 1) for i in range(4)])]
    ppermute x4 -> x5, starting transfers between devices: 13.9 us -> 16.2 us  [the longest x3 9.97 us: local(): held.append(lax.ppermute(cells, 'x', [(i, i ^ apart) for i in range(4)]))]
  transfers between devices with their start and end apart: 9 -> 10, of which waited for: 6 -> 6; matrix products, arithmetic and copies ran while one was open for 1% -> 1% of each run, Pallas kernels for 3% -> 3%
where the time goes in v7:
time: 171 us; the launch traced here: 170 us
  blocking collectives  57.5 us (34%)
  starting transfers between devices  50.7 us (30%)
  waiting for transfers between devices  43 us (25%)
  Pallas kernels  12.2 us (7%)
  other arithmetic  2.83 us (2%)
  local copies, waits for them, and re-layouts  2.61 us (2%)
    all_to_all x2, blocking collectives, exchange(): return lax.all_to_all(value, axes, split_axis=0, concat_axis=0, tiled=True)  57.5 us
    all_to_all x2, starting transfers between devices, exchange(): return lax.all_to_all(value, axes, split_axis=0, concat_axis=0, tiled=True)  25.3 us
    all_to_all x2, waiting for transfers between devices, exchange(): return lax.all_to_all(value, axes, split_axis=0, concat_axis=0, tiled=True)  22.6 us
    ppermute x2, waiting for transfers between devices, local(): other = lax.ppermute(cells, 'yl', [(i, i ^ hop + 1) for i in range(4)])  10.8 us
    ppermute x3, starting transfers between devices, local(): held.append(lax.ppermute(cells, 'x', [(i, i ^ apart) for i in range(4)]))  9.97 us
    ppermute x2, starting transfers between devices, local(): other = lax.ppermute(cells, 'yl', [(i, i ^ hop + 1) for i in range(4)])  6.19 us
    pallas_call x1, Pallas kernels, local(): call(solve_slot, shape(SLOTS * 2 * EACH, NZ), [VMEM] * 2, scratch=[pltpu....  5.1 us
    ppermute x1, waiting for transfers between devices, local(): west = lax.ppermute(masked, SPACE, up)  4.68 us
  transfers between devices with their start and end apart: 10, of which 6 were waited for; matrix products, arithmetic and copies ran while one was open for 1% of the time, Pallas kernels for 3%

profile of v7, /device:TPU:8, one launch (start us, length us, event | category | flops | bytes accessed | tf_op | source)
XLA Modules:
  0.0 169.8 jit_solution(60407888209990658)
XLA Ops:
  0.6 0.9 select_bitcast_fusion.cells_ref
  1.5 0.0 copy-start.2
  1.5 1.1 bitcast_multiply_fusion.masked_ref
  2.7 3.4 %collective-permute-start.1 = (f32[8,128,128]{2,1,0:T(8,128)S(1)}, f32[8,128,128]{2,1,0:T(8,128)S(1)}, u32[]{:S(2)}, u32[]{:S(2)}) collective-permute-start(f32[8,128,128]{2,1,0:T(8,128)S(1)} %bitcast_multiply_fusion.masked_ref), channel_id=1, source_target_pairs={{0,1},{1,2},{2,3},{3,4},{4,5},{5,6},{6,7},{7,8},{8,9},{9,10},{10,1... | collective-permute-start | bytes 1572872 | tf_op jit(solution)/shard_map/ppermute | solution.py:253
  6.1 4.6 %collective-permute-start = (f32[8,128,128]{2,1,0:T(8,128)S(1)}, f32[8,128,128]{2,1,0:T(8,128)S(1)}, u32[]{:S(2)}, u32[]{:S(2)}) collective-permute-start(f32[8,128,128]{2,1,0:T(8,128)S(1)} %bitcast_multiply_fusion.masked_ref), channel_id=1, source_target_pairs={{1,0},{2,1},{3,2},{4,3},{5,4},{6,5},{7,6},{8,7},{9,8},{10,9},{11,1... | collective-permute-start | bytes 1572872 | tf_op jit(solution)/shard_map/ppermute | solution.py:254
  10.6 1.3 collective-permute-start.2
  12.0 0.7 pad_maximum_fusion.class_ref
  12.7 1.0 copy-done
  13.7 0.8 copy-done.3
  14.5 1.1 shard_map.113
  15.7 4.7 %collective-permute-done.1.west_ref = f32[8,128,128]{2,1,0:T(8,128)S(1)} collective-permute-done((f32[8,128,128]{2,1,0:T(8,128)S(1)}, f32[8,128,128]{2,1,0:T(8,128)S(1)}, u32[]{:S(2)}, u32[]{:S(2)}) %collective-permute-start.1) | collective-permute-done | bytes 524320 | tf_op jit(solution)/shard_map/ppermute | solution.py:253
  20.3 1.2 collective-permute-done.east_ref
  21.5 1.2 shard_map.114
  22.8 16.5 %all-to-all-start = ((f32[32,40,128]{2,1,0:T(8,128)}), f32[32,40,128]{2,1,0:T(8,128)S(1)}, u32[]{:S(2)}, u32[]{:S(2)}) async-start(f32[32,40,128]{2,1,0:T(8,128)} %bitcast.9), calls=%async_computation | async-start | bytes 1310720 | tf_op jit(solution)/shard_map/all_to_all | solution.py:237
  39.3 1.9 %collective-permute-start.3 = (s32[1,1,40,128]{3,2,1,0:T(8,128)S(1)}, s32[1,1,40,128]{3,2,1,0:T(8,128)S(1)}, u32[]{:S(2)}, u32[]{:S(2)}) collective-permute-start(s32[1,1,40,128]{3,2,1,0:T(8,128)S(1)} %fusion), channel_id=1, source_target_pairs={{0,4},{4,0},{8,12},{12,8},{1,5},{5,1},{9,13},{13,9},{2,6},{6,2},{1... | collective-permute-start | bytes 61448 | tf_op jit(solution)/shard_map/ppermute | solution.py:262
  41.3 22.6 %all-to-all-done = f32[32,40,128]{2,1,0:T(8,128)S(1)} async-done(((f32[32,40,128]{2,1,0:T(8,128)}), f32[32,40,128]{2,1,0:T(8,128)S(1)}, u32[]{:S(2)}, u32[]{:S(2)}) %all-to-all-start) | async-done | bytes 655392 | tf_op jit(solution)/shard_map/all_to_all | solution.py:237
  63.9 1.6 shard_map.115
  65.6 8.8 %all-to-all-start.1 = ((f32[128,1,1280]{2,1,0:T(1,128)}), f32[128,1,1280]{2,1,0:T(1,128)}, u32[]{:S(2)}, u32[]{:S(2)}) async-start(f32[128,1,1280]{2,1,0:T(1,128)} %bitcast.11), calls=%async_computation.1 | async-start | bytes 1310720 | tf_op jit(solution)/shard_map/all_to_all | solution.py:237
  74.4 4.3 %collective-permute-start.4 = (s32[2,1,40,128]{3,2,1,0:T(8,128)S(1)}, s32[2,1,40,128]{3,2,1,0:T(8,128)S(1)}, u32[]{:S(2)}, u32[]{:S(2)}) collective-permute-start(s32[2,1,40,128]{3,2,1,0:T(8,128)S(1)} %pad_add_fusion.2), channel_id=1, source_target_pairs={{0,8},{4,12},{8,0},{12,4},{1,9},{5,13},{9,1},{13,5},{2,10},{6,14},... | collective-permute-start | bytes 122888 | tf_op jit(solution)/shard_map/ppermute | solution.py:262
  78.7 10.8 %collective-permute-done.4 = s32[2,1,40,128]{3,2,1,0:T(8,128)S(1)} collective-permute-done((s32[2,1,40,128]{3,2,1,0:T(8,128)S(1)}, s32[2,1,40,128]{3,2,1,0:T(8,128)S(1)}, u32[]{:S(2)}, u32[]{:S(2)}) %collective-permute-start.4) | collective-permute-done | bytes 40992 | tf_op jit(solution)/shard_map/ppermute | solution.py:262
  89.5 5.0 %collective-permute-start.6 = (s32[4,1,40,128]{3,2,1,0:T(8,128)S(1)}, s32[4,1,40,128]{3,2,1,0:T(8,128)S(1)}, u32[]{:S(2)}, u32[]{:S(2)}) collective-permute-start(s32[4,1,40,128]{3,2,1,0:T(8,128)S(1)} %pad_add_fusion.1), channel_id=1, source_target_pairs={{0,2},{1,3},{2,0},{3,1},{4,6},{5,7},{6,4},{7,5},{8,10},{9,11},{10,... | collective-permute-start | bytes 245768 | tf_op jit(solution)/shard_map/ppermute | solution.py:268
  94.5 3.1 %collective-permute-start.7 = (s32[4,1,40,128]{3,2,1,0:T(8,128)S(1)}, s32[4,1,40,128]{3,2,1,0:T(8,128)S(1)}, u32[]{:S(2)}, u32[]{:S(2)}) collective-permute-start(s32[4,1,40,128]{3,2,1,0:T(8,128)S(1)} %pad_add_fusion.1), channel_id=1, source_target_pairs={{0,3},{1,2},{2,1},{3,0},{4,7},{5,6},{6,5},{7,4},{8,11},{9,10},{10,... | collective-permute-start | bytes 245768 | tf_op jit(solution)/shard_map/ppermute | solution.py:268
  97.6 1.9 %collective-permute-start.5 = (s32[4,1,40,128]{3,2,1,0:T(8,128)S(1)}, s32[4,1,40,128]{3,2,1,0:T(8,128)S(1)}, u32[]{:S(2)}, u32[]{:S(2)}) collective-permute-start(s32[4,1,40,128]{3,2,1,0:T(8,128)S(1)} %pad_add_fusion.1), channel_id=1, source_target_pairs={{0,1},{1,0},{2,3},{3,2},{4,5},{5,4},{6,7},{7,6},{8,9},{9,8},{10,11... | collective-permute-start | bytes 245768 | tf_op jit(solution)/shard_map/ppermute | solution.py:268
  99.5 0.7 dynamic-slice_bitcast_fusion.shift_ref
  100.2 1.8 %collective-permute-done.7 = s32[4,1,40,128]{3,2,1,0:T(8,128)S(1)} collective-permute-done((s32[4,1,40,128]{3,2,1,0:T(8,128)S(1)}, s32[4,1,40,128]{3,2,1,0:T(8,128)S(1)}, u32[]{:S(2)}, u32[]{:S(2)}) %collective-permute-start.7) | collective-permute-done | bytes 81952 | tf_op jit(solution)/shard_map/ppermute | solution.py:268
  102.1 1.9 %collective-permute-done.5 = s32[4,1,40,128]{3,2,1,0:T(8,128)S(1)} collective-permute-done((s32[4,1,40,128]{3,2,1,0:T(8,128)S(1)}, s32[4,1,40,128]{3,2,1,0:T(8,128)S(1)}, u32[]{:S(2)}, u32[]{:S(2)}) %collective-permute-start.5) | collective-permute-done | bytes 81952 | tf_op jit(solution)/shard_map/ppermute | solution.py:268
  104.0 1.6 shard_map.116.coefficient_ref
  105.6 5.1 %shard_map.117 = f32[1024,128]{1,0:T(8,128)S(1)} custom-call(f32[1280,128]{1,0:T(8,128)} %bitcast.12.spectrum_ref, f32[9,40,16,128]{3,2,1,0:T(8,128)S(1)} %shard_map.116.coefficient_ref), custom_call_target="tpu_custom_call" | custom-call | flops 1000000 | bytes 2000000 | tf_op jit(solution)/shard_map/pallas_call | solution.py:292
  110.7 30.0 %all_to_all.36 = f32[128,8,128]{2,1,0:T(8,128)S(1)} all-to-all(f32[128,8,128]{2,1,0:T(8,128)S(1)} %bitcast.35), channel_id=1, replica_groups=mesh['yh'=2,'zh'=2,'zl'=4,'core'=2,'yl'=4,'x'=4] {'zl','core','yl','x'}, dimensions={0} | all-to-all | bytes 1048576 | tf_op jit(solution)/shard_map/all_to_all | solution.py:237
  140.7 0.7 shard_map.118
  141.4 27.5 %all_to_all.37 = f32[32,32,128]{2,1,0:T(8,128)S(1)} all-to-all(f32[32,32,128]{2,1,0:T(8,128)S(1)} %bitcast.33), channel_id=1, replica_groups=mesh['yh'=2,'zh'=2,'zl'=4,'core'=2,'yl'=4,'x'=4] {'yh','zh','zl','core'}, dimensions={0} | all-to-all | bytes 1048576 | tf_op jit(solution)/shard_map/all_to_all | solution.py:237
  168.9 0.9 shard_map.119
  (19 shorter events, 0.2 us)
Async XLA Ops:
  1.5 62.4 %copy-start.2 = (f32[256,256]{1,0:T(8,128)S(1)}, f32[256,256]{1,0:T(8,128)}, u32[]{:S(2)}) copy-start(f32[256,256]{1,0:T(8,128)} %constant.53.clone.table_ref) | copy-start | bytes 786436
  2.7 17.7 %collective-permute-start.1 = (f32[8,128,128]{2,1,0:T(8,128)S(1)}, f32[8,128,128]{2,1,0:T(8,128)S(1)}, u32[]{:S(2)}, u32[]{:S(2)}) collective-permute-start(f32[8,128,128]{2,1,0:T(8,128)S(1)} %bitcast_multiply_fusion.masked_ref), channel_id=1, source_target_pairs={{0,1},{1,2},{2,3},{3,4},{4,5},{5,6},{6,7},{7,8},{8,9},{9,10},{10,1... | collective-permute-start | bytes 1572872 | tf_op jit(solution)/shard_map/ppermute | solution.py:253
  6.1 15.4 %collective-permute-start = (f32[8,128,128]{2,1,0:T(8,128)S(1)}, f32[8,128,128]{2,1,0:T(8,128)S(1)}, u32[]{:S(2)}, u32[]{:S(2)}) collective-permute-start(f32[8,128,128]{2,1,0:T(8,128)S(1)} %bitcast_multiply_fusion.masked_ref), channel_id=1, source_target_pairs={{1,0},{2,1},{3,2},{4,3},{5,4},{6,5},{7,6},{8,7},{9,8},{10,9},{11,1... | collective-permute-start | bytes 1572872 | tf_op jit(solution)/shard_map/ppermute | solution.py:254
  10.6 5.0 %collective-permute-start.2 = (f32[128,128]{1,0:T(8,128)S(1)}, f32[128,128]{1,0:T(8,128)S(1)}, u32[]{:S(2)}, u32[]{:S(2)}) collective-permute-start(f32[128,128]{1,0:T(8,128)S(1)} %slice_bitcast_fusion), channel_id=1, source_target_pairs={{0,16},{16,32},{32,48},{48,64},{64,80},{80,96},{96,112},{112,128},... | collective-permute-start | bytes 196616 | tf_op jit(solution)/shard_map/ppermute | solution.py:255
  12.7 1.0 copy-start
  13.7 0.8 copy-start.3
  22.8 41.2 %all-to-all-start = ((f32[32,40,128]{2,1,0:T(8,128)}), f32[32,40,128]{2,1,0:T(8,128)S(1)}, u32[]{:S(2)}, u32[]{:S(2)}) async-start(f32[32,40,128]{2,1,0:T(8,128)} %bitcast.9), calls=%async_computation | async-start | bytes 1310720 | tf_op jit(solution)/shard_map/all_to_all | solution.py:237
  39.3 35.0 %collective-permute-start.3 = (s32[1,1,40,128]{3,2,1,0:T(8,128)S(1)}, s32[1,1,40,128]{3,2,1,0:T(8,128)S(1)}, u32[]{:S(2)}, u32[]{:S(2)}) collective-permute-start(s32[1,1,40,128]{3,2,1,0:T(8,128)S(1)} %fusion), channel_id=1, source_target_pairs={{0,4},{4,0},{8,12},{12,8},{1,5},{5,1},{9,13},{13,9},{2,6},{6,2},{1... | collective-permute-start | bytes 61448 | tf_op jit(solution)/shard_map/ppermute | solution.py:262
  65.6 40.1 %all-to-all-start.1 = ((f32[128,1,1280]{2,1,0:T(1,128)}), f32[128,1,1280]{2,1,0:T(1,128)}, u32[]{:S(2)}, u32[]{:S(2)}) async-start(f32[128,1,1280]{2,1,0:T(1,128)} %bitcast.11), calls=%async_computation.1 | async-start | bytes 1310720 | tf_op jit(solution)/shard_map/all_to_all | solution.py:237
  74.4 15.1 %collective-permute-start.4 = (s32[2,1,40,128]{3,2,1,0:T(8,128)S(1)}, s32[2,1,40,128]{3,2,1,0:T(8,128)S(1)}, u32[]{:S(2)}, u32[]{:S(2)}) collective-permute-start(s32[2,1,40,128]{3,2,1,0:T(8,128)S(1)} %pad_add_fusion.2), channel_id=1, source_target_pairs={{0,8},{4,12},{8,0},{12,4},{1,9},{5,13},{9,1},{13,5},{2,10},{6,14},... | collective-permute-start | bytes 122888 | tf_op jit(solution)/shard_map/ppermute | solution.py:262
  89.5 10.7 %collective-permute-start.6 = (s32[4,1,40,128]{3,2,1,0:T(8,128)S(1)}, s32[4,1,40,128]{3,2,1,0:T(8,128)S(1)}, u32[]{:S(2)}, u32[]{:S(2)}) collective-permute-start(s32[4,1,40,128]{3,2,1,0:T(8,128)S(1)} %pad_add_fusion.1), channel_id=1, source_target_pairs={{0,2},{1,3},{2,0},{3,1},{4,6},{5,7},{6,4},{7,5},{8,10},{9,11},{10,... | collective-permute-start | bytes 245768 | tf_op jit(solution)/shard_map/ppermute | solution.py:268
  94.5 7.5 %collective-permute-start.7 = (s32[4,1,40,128]{3,2,1,0:T(8,128)S(1)}, s32[4,1,40,128]{3,2,1,0:T(8,128)S(1)}, u32[]{:S(2)}, u32[]{:S(2)}) collective-permute-start(s32[4,1,40,128]{3,2,1,0:T(8,128)S(1)} %pad_add_fusion.1), channel_id=1, source_target_pairs={{0,3},{1,2},{2,1},{3,0},{4,7},{5,6},{6,5},{7,4},{8,11},{9,10},{10,... | collective-permute-start | bytes 245768 | tf_op jit(solution)/shard_map/ppermute | solution.py:268
  97.6 6.3 %collective-permute-start.5 = (s32[4,1,40,128]{3,2,1,0:T(8,128)S(1)}, s32[4,1,40,128]{3,2,1,0:T(8,128)S(1)}, u32[]{:S(2)}, u32[]{:S(2)}) collective-permute-start(s32[4,1,40,128]{3,2,1,0:T(8,128)S(1)} %pad_add_fusion.1), channel_id=1, source_target_pairs={{0,1},{1,0},{2,3},{3,2},{4,5},{5,4},{6,7},{7,6},{8,9},{9,8},{10,11... | collective-permute-start | bytes 245768 | tf_op jit(solution)/shard_map/ppermute | solution.py:268
  105.6 35.1 %copy-start.1 = (f32[256,256]{1,0:T(8,128)S(1)}, f32[256,256]{1,0:T(8,128)}, u32[]{:S(2)}) copy-start(f32[256,256]{1,0:T(8,128)} %constant.55.clone.table_ref) | copy-start | bytes 786436

commit v8 on v5

--- a/solution.py
+++ b/solution.py
@@ -146,78 +146,98 @@
 
 
 def prepare_slot(cells_ref, class_ref, shift_ref, coefficient_ref):
-    edge = lax.broadcasted_iota(jnp.int32, (NX, NZ), 0)
-    lane = lax.broadcasted_iota(jnp.int32, (NX, NZ), 1)
+    sublane = lax.broadcasted_iota(jnp.int32, (NX // 2, NZ), 0)
+    lane = lax.broadcasted_iota(jnp.int32, (NX // 2, NZ), 1)
     first, second, turn = shift_ref[0], shift_ref[1], shift_ref[2]
 
     def prepare(y, carry):
-        weight, kappa, (flow_x, flow_y, flow_z) = look_up(cells_ref[pl.ds(y, NX, stride=WIDE), :], class_ref)
-        coefficient_ref[0, y] = jnp.where(edge == NX - 1, 0.0, kappa - flow_x)
-        coefficient_ref[1, y] = jnp.where(edge == 0, 0.0, kappa + flow_x)
-        coefficient_ref[2, y] = kappa - flow_y
-        coefficient_ref[3, y] = kappa + flow_y
-        coefficient_ref[4, y] = jnp.where(lane == NZ - 1, 0.0, kappa - flow_z)
-        coefficient_ref[5, y] = jnp.where(lane == 0, 0.0, kappa + flow_z)
-        real_first = first + 6.0 * kappa
-        real_second = second + 6.0 * kappa
-        over_first = weight / (real_first * real_first + turn * turn)
-        over_second = weight / (real_second * real_second + turn * turn)
-        coefficient_ref[6, y] = real_first * over_first
-        coefficient_ref[7, y] = turn * over_first
-        coefficient_ref[8, y] = real_second * over_second
+        for odd in range(2):
+            classes = cells_ref[pl.ds(y + odd * WIDE, NX // 2, stride=2 * WIDE), :]
+            weight, kappa, (flow_x, flow_y, flow_z) = look_up(classes, class_ref)
+            east, west = kappa - flow_x, kappa + flow_x
+            if odd:
+                east = jnp.where(sublane == NX // 2 - 1, 0.0, east)
+            else:
+                west = jnp.where(sublane == 0, 0.0, west)
+            coefficient_ref[0, y, odd] = east
+            coefficient_ref[1, y, odd] = west
+            coefficient_ref[2, y, odd] = kappa - flow_y
+            coefficient_ref[3, y, odd] = kappa + flow_y
+            coefficient_ref[4, y, odd] = jnp.where(lane == NZ - 1, 0.0, kappa - flow_z)
+            coefficient_ref[5, y, odd] = jnp.where(lane == 0, 0.0, kappa + flow_z)
+            real_first = first + 6.0 * kappa
+            real_second = second + 6.0 * kappa
+            over_first = weight / (real_first * real_first + turn * turn)
+            over_second = weight / (real_second * real_second + turn * turn)
+            coefficient_ref[6, y, odd] = real_first * over_first
+            coefficient_ref[7, y, odd] = turn * over_first
+            coefficient_ref[8, y, odd] = real_second * over_second
         return carry
 
     lax.fori_loop(0, WIDE, prepare, 0, unroll=2)
 
 
 def solve_slot(spectrum_ref, coefficient_ref, sent_ref, source, even, odd):
-    def scale(y, one, two):
-        a, b, c = coefficient_ref[6, y], coefficient_ref[7, y], coefficient_ref[8, y]
+    tile = NX // 2
+
+    def scale(y, half, one, two):
+        a, b, c = (coefficient_ref[kind, y, half] for kind in (6, 7, 8))
         return a * one + b * two, c * two - b * one
 
-    blank = jnp.zeros((2, NX, NZ), F32)
-    even[0] = blank
-    even[WIDE + 1] = blank
+    blank = jnp.zeros((2, 2, tile, NZ), F32)
+    for field in (even, odd):
+        field[0] = blank
+        field[WIDE + 1] = blank
+    rows = 2 * WIDE_EACH
     for member in range(MEMBERS):
         for row in range(WIDE_EACH):
-            at = member * NX * 2 * WIDE_EACH + row
             y = member * WIDE_EACH + row
-            one = spectrum_ref[pl.ds(at, NX, stride=2 * WIDE_EACH), :]
-            two = spectrum_ref[pl.ds(at + WIDE_EACH, NX, stride=2 * WIDE_EACH), :]
-            source[y, 0] = one
-            source[y, 1] = two
-            even[y + 1, 0], even[y + 1, 1] = scale(y, one, two)
+            for half in range(2):
+                at = (member * NX + half) * rows + row
+                one = spectrum_ref[pl.ds(at, tile, stride=2 * rows), :]
+                two = spectrum_ref[pl.ds(at + WIDE_EACH, tile, stride=2 * rows), :]
+                source[y, 0, half] = one
+                source[y, 1, half] = two
+                even[y + 1, 0, half], even[y + 1, 1, half] = scale(y, half, one, two)
 
     for sweep in range(SWEEPS):
         now, later = (even, odd) if sweep % 2 == 0 else (odd, even)
-        begin = (sweep + 1) // 2 * 2
+        begin = HALO if sweep == SWEEPS - 1 else 0
         end = WIDE - begin
 
         def row(y, carry):
             south, here = carry
-            north = (now[y + 2, 0], now[y + 2, 1])
-            totals = []
-            for part in range(2):
-                mid = here[part]
-                total = source[y, part]
-                total += coefficient_ref[0, y] * pltpu.roll(mid, NX - 1, 0)
-                total += coefficient_ref[1, y] * pltpu.roll(mid, 1, 0)
-                total += coefficient_ref[2, y] * north[part] + coefficient_ref[3, y] * south[part]
-                total += coefficient_ref[4, y] * pltpu.roll(mid, NZ - 1, 1)
-                total += coefficient_ref[5, y] * pltpu.roll(mid, 1, 1)
-                totals.append(total)
-            later[y + 1, 0], later[y + 1, 1] = scale(y, *totals)
+            north = tuple(tuple(now[y + 2, part, half] for half in range(2)) for part in range(2))
+            for half in range(2):
+                totals = []
+                for part in range(2):
+                    mid, across = here[part][half], here[part][1 - half]
+                    east = pltpu.roll(across, tile - 1, 0) if half else across
+                    west = across if half else pltpu.roll(across, 1, 0)
+                    total = source[y, part, half]
+                    total += coefficient_ref[0, y, half] * east + coefficient_ref[1, y, half] * west
+                    total += coefficient_ref[2, y, half] * north[part][half]
+                    total += coefficient_ref[3, y, half] * south[part][half]
+                    total += coefficient_ref[4, y, half] * pltpu.roll(mid, NZ - 1, 1)
+                    total += coefficient_ref[5, y, half] * pltpu.roll(mid, 1, 1)
+                    totals.append(total)
+                later[y + 1, 0, half], later[y + 1, 1, half] = scale(y, half, *totals)
             return here, north
 
-        start = tuple((now[begin + k, 0], now[begin + k, 1]) for k in range(2))
-        lax.fori_loop(begin, end, row, start, unroll=4)
+        start = tuple(
+            tuple(tuple(now[begin + k, part, half] for half in range(2)) for part in range(2)) for k in range(2)
+        )
+        lax.fori_loop(begin, end, row, start, unroll=8)
 
     field = even if SWEEPS % 2 == 0 else odd
+    rows = 2 * EACH
     for member in range(MEMBERS):
         for row in range(EACH):
             for part in range(2):
-                at = member * NX * 2 * EACH + part * EACH + row
-                sent_ref[pl.ds(at, NX, stride=2 * EACH), :] = field[HALO + member * EACH + row + 1, part]
+                for half in range(2):
+                    at = (member * NX + half) * rows + part * EACH + row
+                    value = field[HALO + member * EACH + row + 1, part, half]
+                    sent_ref[pl.ds(at, tile, stride=2 * rows), :] = value
 
 
 def call(kernel, out_shape, in_specs, scratch=(), flops=1_000_000, moved=2_000_000):
@@ -284,15 +304,15 @@
     sent = call(to_frequencies, shape(SLOTS * 2 * WIDE_EACH, NZ), [VMEM] * 2)(steps, jnp.asarray(forward))
     spectrum = exchange(sent.reshape(SLOTS, 1, 2 * WIDE_EACH * NZ), BLOCK).reshape(SLOTS * 2 * WIDE_EACH, NZ)
     mine = lax.dynamic_slice_in_dim(jnp.asarray(shift), lax.axis_index(BLOCK), 1, 0).reshape(4)
-    coefficient = call(prepare_slot, shape(9, WIDE, NX, NZ), [VMEM] + [SMEM] * 2)(cells, per_class, mine)
+    coefficient = call(prepare_slot, shape(9, WIDE, 2, NX // 2, NZ), [VMEM] + [SMEM] * 2)(cells, per_class, mine)
     sent = call(
         solve_slot,
         shape(SLOTS * 2 * EACH, NZ),
         [VMEM] * 2,
         scratch=[
-            pltpu.VMEM((WIDE, 2, NX, NZ), F32),
-            pltpu.VMEM((WIDE + 2, 2, NX, NZ), F32),
-            pltpu.VMEM((WIDE + 2, 2, NX, NZ), F32),
+            pltpu.VMEM((WIDE, 2, 2, NX // 2, NZ), F32),
+            pltpu.VMEM((WIDE + 2, 2, 2, NX // 2, NZ), F32),
+            pltpu.VMEM((WIDE + 2, 2, 2, NX // 2, NZ), F32),
         ],
     )(spectrum, coefficient)
     solved = exchange(sent, BLOCK)

time: 161 us -> 160 us (level)
  no operation moved by 1% of the time
where the time goes in v8:
time: 160 us; the launch traced here: 159 us
  blocking collectives  57.2 us (36%)
  starting transfers between devices  48.5 us (30%)
  waiting for transfers between devices  35.7 us (22%)
  Pallas kernels  11.1 us (7%)
  other arithmetic  2.82 us (2%)
  local copies, waits for them, and re-layouts  2.61 us (2%)
    all_to_all x2, blocking collectives, exchange(): return lax.all_to_all(value, axes, split_axis=0, concat_axis=0, tiled=True)  57.2 us
    all_to_all x2, starting transfers between devices, exchange(): return lax.all_to_all(value, axes, split_axis=0, concat_axis=0, tiled=True)  25.4 us
    ppermute x4, waiting for transfers between devices, local(): other = lax.ppermute(cells, axis, [(i, i ^ bit) for i in range(4)])  23.4 us
    ppermute x4, starting transfers between devices, local(): other = lax.ppermute(cells, axis, [(i, i ^ bit) for i in range(4)])  13.9 us
    all_to_all x2, waiting for transfers between devices, exchange(): return lax.all_to_all(value, axes, split_axis=0, concat_axis=0, tiled=True)  5.56 us
    ppermute x1, waiting for transfers between devices, local(): west = lax.ppermute(masked, SPACE, up)  5.55 us
    ppermute x1, starting transfers between devices, local(): east = lax.ppermute(masked, SPACE, down)  4.55 us
    pallas_call x1, Pallas kernels, local(): call(solve_slot, shape(SLOTS * 2 * EACH, NZ), [VMEM] * 2, scratch=[pltpu....  4.01 us
  transfers between devices with their start and end apart: 9, of which 6 were waited for; matrix products, arithmetic and copies ran while one was open for 1% of the time, Pallas kernels for 3%

profile of v8, /device:TPU:8, one launch (start us, length us, event | category | flops | bytes accessed | tf_op | source)
XLA Modules:
  0.0 158.9 jit_solution(3398739828235538514)
XLA Ops:
  0.6 0.9 select_bitcast_fusion.cells_ref
  1.5 0.0 copy-start.2
  1.5 1.1 bitcast_multiply_fusion.masked_ref
  2.7 3.4 %collective-permute-start.1 = (f32[8,128,128]{2,1,0:T(8,128)S(1)}, f32[8,128,128]{2,1,0:T(8,128)S(1)}, u32[]{:S(2)}, u32[]{:S(2)}) collective-permute-start(f32[8,128,128]{2,1,0:T(8,128)S(1)} %bitcast_multiply_fusion.masked_ref), channel_id=1, source_target_pairs={{0,1},{1,2},{2,3},{3,4},{4,5},{5,6},{6,7},{7,8},{8,9},{9,10},{10,1... | collective-permute-start | bytes 1572872 | tf_op jit(solution)/shard_map/ppermute | solution.py:276
  6.1 4.6 %collective-permute-start = (f32[8,128,128]{2,1,0:T(8,128)S(1)}, f32[8,128,128]{2,1,0:T(8,128)S(1)}, u32[]{:S(2)}, u32[]{:S(2)}) collective-permute-start(f32[8,128,128]{2,1,0:T(8,128)S(1)} %bitcast_multiply_fusion.masked_ref), channel_id=1, source_target_pairs={{1,0},{2,1},{3,2},{4,3},{5,4},{6,5},{7,6},{8,7},{9,8},{10,9},{11,1... | collective-permute-start | bytes 1572872 | tf_op jit(solution)/shard_map/ppermute | solution.py:277
  10.7 1.3 collective-permute-start.2
  12.0 0.7 pad_maximum_fusion.class_ref
  12.7 1.0 copy-done
  13.7 1.1 shard_map.113
  14.8 5.5 %collective-permute-done.1.west_ref = f32[8,128,128]{2,1,0:T(8,128)S(1)} collective-permute-done((f32[8,128,128]{2,1,0:T(8,128)S(1)}, f32[8,128,128]{2,1,0:T(8,128)S(1)}, u32[]{:S(2)}, u32[]{:S(2)}) %collective-permute-start.1) | collective-permute-done | bytes 524320 | tf_op jit(solution)/shard_map/ppermute | solution.py:276
  20.3 1.2 collective-permute-done.east_ref
  21.5 0.8 copy-done.3
  22.4 1.3 shard_map.114
  23.6 16.5 %all-to-all-start = ((f32[32,40,128]{2,1,0:T(8,128)}), f32[32,40,128]{2,1,0:T(8,128)S(1)}, u32[]{:S(2)}, u32[]{:S(2)}) async-start(f32[32,40,128]{2,1,0:T(8,128)} %bitcast.9), calls=%async_computation | async-start | bytes 1310720 | tf_op jit(solution)/shard_map/all_to_all | solution.py:260
  40.2 1.9 %collective-permute-start.3 = (s32[1,1,40,128]{3,2,1,0:T(8,128)S(1)}, s32[1,1,40,128]{3,2,1,0:T(8,128)S(1)}, u32[]{:S(2)}, u32[]{:S(2)}) collective-permute-start(s32[1,1,40,128]{3,2,1,0:T(8,128)S(1)} %fusion), channel_id=1, source_target_pairs={{0,4},{4,0},{8,12},{12,8},{1,5},{5,1},{9,13},{13,9},{2,6},{6,2},{1... | collective-permute-start | bytes 61448 | tf_op jit(solution)/shard_map/ppermute | solution.py:285
  42.1 13.3 %collective-permute-done.3 = s32[1,1,40,128]{3,2,1,0:T(8,128)S(1)} collective-permute-done((s32[1,1,40,128]{3,2,1,0:T(8,128)S(1)}, s32[1,1,40,128]{3,2,1,0:T(8,128)S(1)}, u32[]{:S(2)}, u32[]{:S(2)}) %collective-permute-start.3) | collective-permute-done | bytes 20512 | tf_op jit(solution)/shard_map/ppermute | solution.py:285
  55.4 3.8 %collective-permute-start.4 = (s32[2,1,40,128]{3,2,1,0:T(8,128)S(1)}, s32[2,1,40,128]{3,2,1,0:T(8,128)S(1)}, u32[]{:S(2)}, u32[]{:S(2)}) collective-permute-start(s32[2,1,40,128]{3,2,1,0:T(8,128)S(1)} %pad_add_fusion.3), channel_id=1, source_target_pairs={{0,8},{4,12},{8,0},{12,4},{1,9},{5,13},{9,1},{13,5},{2,10},{6,14},... | collective-permute-start | bytes 122888 | tf_op jit(solution)/shard_map/ppermute | solution.py:285
  59.2 5.6 %all-to-all-done = f32[32,40,128]{2,1,0:T(8,128)S(1)} async-done(((f32[32,40,128]{2,1,0:T(8,128)}), f32[32,40,128]{2,1,0:T(8,128)S(1)}, u32[]{:S(2)}, u32[]{:S(2)}) %all-to-all-start) | async-done | bytes 655392 | tf_op jit(solution)/shard_map/all_to_all | solution.py:260
  64.8 1.6 %shard_map.115 = f32[1280,128]{1,0:T(8,128)} custom-call(f32[32,5,8,128]{3,2,1,0:T(8,128)S(1)} %bitcast.31, f32[256,256]{1,0:T(8,128)S(1)} %copy-done.2), custom_call_target="tpu_custom_call" | custom-call | flops 1000000 | bytes 2000000 | tf_op jit(solution)/shard_map/pallas_call | solution.py:304
  66.4 8.9 %all-to-all-start.1 = ((f32[128,1,1280]{2,1,0:T(1,128)}), f32[128,1,1280]{2,1,0:T(1,128)}, u32[]{:S(2)}, u32[]{:S(2)}) async-start(f32[128,1,1280]{2,1,0:T(1,128)} %bitcast.11), calls=%async_computation.1 | async-start | bytes 1310720 | tf_op jit(solution)/shard_map/all_to_all | solution.py:260
  75.3 3.4 %collective-permute-start.5 = (s32[4,1,40,128]{3,2,1,0:T(8,128)S(1)}, s32[4,1,40,128]{3,2,1,0:T(8,128)S(1)}, u32[]{:S(2)}, u32[]{:S(2)}) collective-permute-start(s32[4,1,40,128]{3,2,1,0:T(8,128)S(1)} %pad_add_fusion.2), channel_id=1, source_target_pairs={{0,1},{1,0},{2,3},{3,2},{4,5},{5,4},{6,7},{7,6},{8,9},{9,8},{10,11... | collective-permute-start | bytes 245768 | tf_op jit(solution)/shard_map/ppermute | solution.py:285
  78.7 4.6 %collective-permute-done.5 = s32[4,1,40,128]{3,2,1,0:T(8,128)S(1)} collective-permute-done((s32[4,1,40,128]{3,2,1,0:T(8,128)S(1)}, s32[4,1,40,128]{3,2,1,0:T(8,128)S(1)}, u32[]{:S(2)}, u32[]{:S(2)}) %collective-permute-start.5) | collective-permute-done | bytes 81952 | tf_op jit(solution)/shard_map/ppermute | solution.py:285
  83.4 4.8 %collective-permute-start.6 = (s32[4,2,40,128]{3,2,1,0:T(8,128)S(1)}, s32[4,2,40,128]{3,2,1,0:T(8,128)S(1)}, u32[]{:S(2)}, u32[]{:S(2)}) collective-permute-start(s32[4,2,40,128]{3,2,1,0:T(8,128)S(1)} %pad_add_fusion.1), channel_id=1, source_target_pairs={{0,2},{1,3},{2,0},{3,1},{4,6},{5,7},{6,4},{7,5},{8,10},{9,11},{10,... | collective-permute-start | bytes 491528 | tf_op jit(solution)/shard_map/ppermute | solution.py:285
  88.2 0.7 dynamic-slice_bitcast_fusion.shift_ref
  88.9 5.5 %collective-permute-done.6 = s32[4,2,40,128]{3,2,1,0:T(8,128)S(1)} collective-permute-done((s32[4,2,40,128]{3,2,1,0:T(8,128)S(1)}, s32[4,2,40,128]{3,2,1,0:T(8,128)S(1)}, u32[]{:S(2)}, u32[]{:S(2)}) %collective-permute-start.6) | collective-permute-done | bytes 163872 | tf_op jit(solution)/shard_map/ppermute | solution.py:285
  94.5 1.6 shard_map.116.coefficient_ref
  96.1 0.0 copy-start.1
  96.1 4.0 %shard_map.117 = f32[1024,128]{1,0:T(8,128)S(1)} custom-call(f32[1280,128]{1,0:T(8,128)} %bitcast.12.spectrum_ref, f32[9,40,2,8,128]{4,3,2,1,0:T(8,128)S(1)} %shard_map.116.coefficient_ref), custom_call_target="tpu_custom_call" | custom-call | flops 1000000 | bytes 2000000 | tf_op jit(solution)/shard_map/pallas_call | solution.py:308
  100.1 28.2 %all_to_all.36 = f32[128,8,128]{2,1,0:T(8,128)S(1)} all-to-all(f32[128,8,128]{2,1,0:T(8,128)S(1)} %bitcast.35), channel_id=1, replica_groups=mesh['yh'=2,'zh'=2,'zl'=4,'core'=2,'yl'=4,'x'=4] {'zl','core','yl','x'}, dimensions={0} | all-to-all | bytes 1048576 | tf_op jit(solution)/shard_map/all_to_all | solution.py:260
  128.3 0.7 shard_map.118
  129.0 29.0 %all_to_all.37 = f32[32,32,128]{2,1,0:T(8,128)S(1)} all-to-all(f32[32,32,128]{2,1,0:T(8,128)S(1)} %bitcast.33), channel_id=1, replica_groups=mesh['yh'=2,'zh'=2,'zl'=4,'core'=2,'yl'=4,'x'=4] {'yh','zh','zl','core'}, dimensions={0} | all-to-all | bytes 1048576 | tf_op jit(solution)/shard_map/all_to_all | solution.py:260
  158.0 0.9 shard_map.119
  (18 shorter events, 0.2 us)
Async XLA Ops:
  1.5 63.3 %copy-start.2 = (f32[256,256]{1,0:T(8,128)S(1)}, f32[256,256]{1,0:T(8,128)}, u32[]{:S(2)}) copy-start(f32[256,256]{1,0:T(8,128)} %constant.51.clone.table_ref) | copy-start | bytes 786436
  2.7 17.7 %collective-permute-start.1 = (f32[8,128,128]{2,1,0:T(8,128)S(1)}, f32[8,128,128]{2,1,0:T(8,128)S(1)}, u32[]{:S(2)}, u32[]{:S(2)}) collective-permute-start(f32[8,128,128]{2,1,0:T(8,128)S(1)} %bitcast_multiply_fusion.masked_ref), channel_id=1, source_target_pairs={{0,1},{1,2},{2,3},{3,4},{4,5},{5,6},{6,7},{7,8},{8,9},{9,10},{10,1... | collective-permute-start | bytes 1572872 | tf_op jit(solution)/shard_map/ppermute | solution.py:276
  6.1 15.4 %collective-permute-start = (f32[8,128,128]{2,1,0:T(8,128)S(1)}, f32[8,128,128]{2,1,0:T(8,128)S(1)}, u32[]{:S(2)}, u32[]{:S(2)}) collective-permute-start(f32[8,128,128]{2,1,0:T(8,128)S(1)} %bitcast_multiply_fusion.masked_ref), channel_id=1, source_target_pairs={{1,0},{2,1},{3,2},{4,3},{5,4},{6,5},{7,6},{8,7},{9,8},{10,9},{11,1... | collective-permute-start | bytes 1572872 | tf_op jit(solution)/shard_map/ppermute | solution.py:277
  10.7 4.1 %collective-permute-start.2 = (f32[128,128]{1,0:T(8,128)S(1)}, f32[128,128]{1,0:T(8,128)S(1)}, u32[]{:S(2)}, u32[]{:S(2)}) collective-permute-start(f32[128,128]{1,0:T(8,128)S(1)} %slice_bitcast_fusion), channel_id=1, source_target_pairs={{0,16},{16,32},{32,48},{48,64},{64,80},{80,96},{96,112},{112,128},... | collective-permute-start | bytes 196616 | tf_op jit(solution)/shard_map/ppermute | solution.py:278
  12.7 1.0 copy-start
  21.5 0.8 copy-start.3
  23.6 41.2 %all-to-all-start = ((f32[32,40,128]{2,1,0:T(8,128)}), f32[32,40,128]{2,1,0:T(8,128)S(1)}, u32[]{:S(2)}, u32[]{:S(2)}) async-start(f32[32,40,128]{2,1,0:T(8,128)} %bitcast.9), calls=%async_computation | async-start | bytes 1310720 | tf_op jit(solution)/shard_map/all_to_all | solution.py:260
  40.2 15.2 %collective-permute-start.3 = (s32[1,1,40,128]{3,2,1,0:T(8,128)S(1)}, s32[1,1,40,128]{3,2,1,0:T(8,128)S(1)}, u32[]{:S(2)}, u32[]{:S(2)}) collective-permute-start(s32[1,1,40,128]{3,2,1,0:T(8,128)S(1)} %fusion), channel_id=1, source_target_pairs={{0,4},{4,0},{8,12},{12,8},{1,5},{5,1},{9,13},{13,9},{2,6},{6,2},{1... | collective-permute-start | bytes 61448 | tf_op jit(solution)/shard_map/ppermute | solution.py:285
  55.4 19.9 %collective-permute-start.4 = (s32[2,1,40,128]{3,2,1,0:T(8,128)S(1)}, s32[2,1,40,128]{3,2,1,0:T(8,128)S(1)}, u32[]{:S(2)}, u32[]{:S(2)}) collective-permute-start(s32[2,1,40,128]{3,2,1,0:T(8,128)S(1)} %pad_add_fusion.3), channel_id=1, source_target_pairs={{0,8},{4,12},{8,0},{12,4},{1,9},{5,13},{9,1},{13,5},{2,10},{6,14},... | collective-permute-start | bytes 122888 | tf_op jit(solution)/shard_map/ppermute | solution.py:285
  66.4 29.7 %all-to-all-start.1 = ((f32[128,1,1280]{2,1,0:T(1,128)}), f32[128,1,1280]{2,1,0:T(1,128)}, u32[]{:S(2)}, u32[]{:S(2)}) async-start(f32[128,1,1280]{2,1,0:T(1,128)} %bitcast.11), calls=%async_computation.1 | async-start | bytes 1310720 | tf_op jit(solution)/shard_map/all_to_all | solution.py:260
  75.3 8.0 %collective-permute-start.5 = (s32[4,1,40,128]{3,2,1,0:T(8,128)S(1)}, s32[4,1,40,128]{3,2,1,0:T(8,128)S(1)}, u32[]{:S(2)}, u32[]{:S(2)}) collective-permute-start(s32[4,1,40,128]{3,2,1,0:T(8,128)S(1)} %pad_add_fusion.2), channel_id=1, source_target_pairs={{0,1},{1,0},{2,3},{3,2},{4,5},{5,4},{6,7},{7,6},{8,9},{9,8},{10,11... | collective-permute-start | bytes 245768 | tf_op jit(solution)/shard_map/ppermute | solution.py:285
  83.4 11.1 %collective-permute-start.6 = (s32[4,2,40,128]{3,2,1,0:T(8,128)S(1)}, s32[4,2,40,128]{3,2,1,0:T(8,128)S(1)}, u32[]{:S(2)}, u32[]{:S(2)}) collective-permute-start(s32[4,2,40,128]{3,2,1,0:T(8,128)S(1)} %pad_add_fusion.1), channel_id=1, source_target_pairs={{0,2},{1,3},{2,0},{3,1},{4,6},{5,7},{6,4},{7,5},{8,10},{9,11},{10,... | collective-permute-start | bytes 491528 | tf_op jit(solution)/shard_map/ppermute | solution.py:285
  96.1 32.3 %copy-start.1 = (f32[256,256]{1,0:T(8,128)S(1)}, f32[256,256]{1,0:T(8,128)}, u32[]{:S(2)}) copy-start(f32[256,256]{1,0:T(8,128)} %constant.53.clone.table_ref) | copy-start | bytes 786436

commit v9 on v8

--- a/solution.py
+++ b/solution.py
@@ -281,11 +281,15 @@
     cells = jnp.pad(cells, ((HALO, HALO), (0, 0)), constant_values=SOLID)
     cells = lax.dynamic_slice_in_dim(cells, lax.axis_index(("yh", "zh")) * SPAN, WIDE, 0)
     cells = cells.reshape(1, 1, WIDE, NZ)
-    for axis, dim, bit in (("yl", 0, 1), ("yl", 0, 2), ("x", 1, 1), ("x", 1, 2)):
-        other = lax.ppermute(cells, axis, [(i, i ^ bit) for i in range(4)])
-        upper = (lax.axis_index(axis) & bit) != 0
-        pair = [jnp.where(upper, other, cells), jnp.where(upper, cells, other)]
-        cells = jnp.concatenate(pair, axis=dim)
+    held = [cells]
+    for apart in range(1, 4):
+        held.append(lax.ppermute(cells, "yl", [(i, i ^ apart) for i in range(4)]))
+    mine_y = lax.axis_index("yl")
+    cells = jnp.concatenate([lax.select_n(mine_y ^ at, *held) for at in range(4)], axis=0)
+    for hop in range(2):
+        other = lax.ppermute(cells, "x", [(i, i ^ (hop + 1)) for i in range(4)])
+        upper = (lax.axis_index("x") & (hop + 1)) != 0
+        cells = jnp.concatenate([jnp.where(upper, other, cells), jnp.where(upper, cells, other)], axis=1)
     cells = cells.reshape(NX * WIDE, NZ)
 
     part, side = call(

time: 160 us -> 159 us (level)
  starting transfers between devices: 48.5 us -> 53.5 us
  waiting for transfers between devices: 35.7 us -> 31.3 us
    ppermute x4 -> x5, waiting for transfers between devices: 23.4 us -> 10.1 us  [the longest x2 10.1 us: local(): other = lax.ppermute(cells, 'x', [(i, i ^ hop + 1) for i in range(4)])]
    all_to_all x2, waiting for transfers between devices: 5.56 us -> 14.4 us  [exchange(): return lax.all_to_all(value, axes, split_axis=0, concat_axis=0, tiled=True)]
    ppermute x4 -> x5, starting transfers between devices: 13.9 us -> 18.4 us  [the longest x3 10.1 us: local(): held.append(lax.ppermute(cells, 'yl', [(i, i ^ apart) for i in range(4)]))]
  transfers between devices with their start and end apart: 9 -> 10, of which waited for: 6 -> 5; matrix products, arithmetic and copies ran while one was open for 1% -> 1% of each run, Pallas kernels for 3% -> 3%
where the time goes in v9:
time: 159 us; the launch traced here: 158 us
  blocking collectives  55.8 us (35%)
  starting transfers between devices  53.5 us (34%)
  waiting for transfers between devices  31.3 us (20%)
  Pallas kernels  11.1 us (7%)
  other arithmetic  2.82 us (2%)
  local copies, waits for them, and re-layouts  2.61 us (2%)
    all_to_all x2, blocking collectives, exchange(): return lax.all_to_all(value, axes, split_axis=0, concat_axis=0, tiled=True)  55.8 us
    all_to_all x2, starting transfers between devices, exchange(): return lax.all_to_all(value, axes, split_axis=0, concat_axis=0, tiled=True)  25.9 us
    all_to_all x2, waiting for transfers between devices, exchange(): return lax.all_to_all(value, axes, split_axis=0, concat_axis=0, tiled=True)  14.4 us
    ppermute x3, starting transfers between devices, local(): held.append(lax.ppermute(cells, 'yl', [(i, i ^ apart) for i in range(4)]))  10.1 us
    ppermute x2, waiting for transfers between devices, local(): other = lax.ppermute(cells, 'x', [(i, i ^ hop + 1) for i in range(4)])  10.1 us
    ppermute x2, starting transfers between devices, local(): other = lax.ppermute(cells, 'x', [(i, i ^ hop + 1) for i in range(4)])  8.27 us
    ppermute x1, waiting for transfers between devices, local(): west = lax.ppermute(masked, SPACE, up)  5.55 us
    ppermute x1, starting transfers between devices, local(): east = lax.ppermute(masked, SPACE, down)  4.55 us
  transfers between devices with their start and end apart: 10, of which 5 were waited for; matrix products, arithmetic and copies ran while one was open for 1% of the time, Pallas kernels for 3%

profile of v9, /device:TPU:8, one launch (start us, length us, event | category | flops | bytes accessed | tf_op | source)
XLA Modules:
  0.0 158.1 jit_solution(9686608268654197820)
XLA Ops:
  0.6 0.9 select_bitcast_fusion.cells_ref
  1.5 0.0 copy-start.2
  1.5 1.1 bitcast_multiply_fusion.masked_ref
  2.7 3.4 %collective-permute-start.1 = (f32[8,128,128]{2,1,0:T(8,128)S(1)}, f32[8,128,128]{2,1,0:T(8,128)S(1)}, u32[]{:S(2)}, u32[]{:S(2)}) collective-permute-start(f32[8,128,128]{2,1,0:T(8,128)S(1)} %bitcast_multiply_fusion.masked_ref), channel_id=1, source_target_pairs={{0,1},{1,2},{2,3},{3,4},{4,5},{5,6},{6,7},{7,8},{8,9},{9,10},{10,1... | collective-permute-start | bytes 1572872 | tf_op jit(solution)/shard_map/ppermute | solution.py:276
  6.1 4.6 %collective-permute-start = (f32[8,128,128]{2,1,0:T(8,128)S(1)}, f32[8,128,128]{2,1,0:T(8,128)S(1)}, u32[]{:S(2)}, u32[]{:S(2)}) collective-permute-start(f32[8,128,128]{2,1,0:T(8,128)S(1)} %bitcast_multiply_fusion.masked_ref), channel_id=1, source_target_pairs={{1,0},{2,1},{3,2},{4,3},{5,4},{6,5},{7,6},{8,7},{9,8},{10,9},{11,1... | collective-permute-start | bytes 1572872 | tf_op jit(solution)/shard_map/ppermute | solution.py:277
  10.6 1.3 collective-permute-start.2
  12.0 0.7 pad_maximum_fusion.class_ref
  12.7 1.0 copy-done
  13.7 1.1 shard_map.113
  14.8 5.5 %collective-permute-done.1.west_ref = f32[8,128,128]{2,1,0:T(8,128)S(1)} collective-permute-done((f32[8,128,128]{2,1,0:T(8,128)S(1)}, f32[8,128,128]{2,1,0:T(8,128)S(1)}, u32[]{:S(2)}, u32[]{:S(2)}) %collective-permute-start.1) | collective-permute-done | bytes 524320 | tf_op jit(solution)/shard_map/ppermute | solution.py:276
  20.3 1.2 collective-permute-done.east_ref
  21.5 0.8 copy-done.3
  22.4 1.3 shard_map.114
  23.6 16.5 %all-to-all-start = ((f32[32,40,128]{2,1,0:T(8,128)}), f32[32,40,128]{2,1,0:T(8,128)S(1)}, u32[]{:S(2)}, u32[]{:S(2)}) async-start(f32[32,40,128]{2,1,0:T(8,128)} %bitcast.9), calls=%async_computation | async-start | bytes 1310720 | tf_op jit(solution)/shard_map/all_to_all | solution.py:260
  40.2 4.5 %collective-permute-start.4 = (s32[1,1,40,128]{3,2,1,0:T(8,128)S(1)}, s32[1,1,40,128]{3,2,1,0:T(8,128)S(1)}, u32[]{:S(2)}, u32[]{:S(2)}) collective-permute-start(s32[1,1,40,128]{3,2,1,0:T(8,128)S(1)} %fusion), channel_id=1, source_target_pairs={{0,8},{4,12},{8,0},{12,4},{1,9},{5,13},{9,1},{13,5},{2,10},{6,14},... | collective-permute-start | bytes 61448 | tf_op jit(solution)/shard_map/ppermute | solution.py:286
  44.7 1.9 %collective-permute-start.5 = (s32[1,1,40,128]{3,2,1,0:T(8,128)S(1)}, s32[1,1,40,128]{3,2,1,0:T(8,128)S(1)}, u32[]{:S(2)}, u32[]{:S(2)}) collective-permute-start(s32[1,1,40,128]{3,2,1,0:T(8,128)S(1)} %fusion), channel_id=1, source_target_pairs={{0,12},{4,8},{8,4},{12,0},{1,13},{5,9},{9,5},{13,1},{2,14},{6,10},... | collective-permute-start | bytes 61448 | tf_op jit(solution)/shard_map/ppermute | solution.py:286
  46.6 3.7 %collective-permute-start.3 = (s32[1,1,40,128]{3,2,1,0:T(8,128)S(1)}, s32[1,1,40,128]{3,2,1,0:T(8,128)S(1)}, u32[]{:S(2)}, u32[]{:S(2)}) collective-permute-start(s32[1,1,40,128]{3,2,1,0:T(8,128)S(1)} %fusion), channel_id=1, source_target_pairs={{0,4},{4,0},{8,12},{12,8},{1,5},{5,1},{9,13},{13,9},{2,6},{6,2},{1... | collective-permute-start | bytes 61448 | tf_op jit(solution)/shard_map/ppermute | solution.py:286
  50.3 14.4 %all-to-all-done = f32[32,40,128]{2,1,0:T(8,128)S(1)} async-done(((f32[32,40,128]{2,1,0:T(8,128)}), f32[32,40,128]{2,1,0:T(8,128)S(1)}, u32[]{:S(2)}, u32[]{:S(2)}) %all-to-all-start) | async-done | bytes 655392 | tf_op jit(solution)/shard_map/all_to_all | solution.py:260
  64.8 1.6 %shard_map.115 = f32[1280,128]{1,0:T(8,128)} custom-call(f32[32,5,8,128]{3,2,1,0:T(8,128)S(1)} %bitcast.31, f32[256,256]{1,0:T(8,128)S(1)} %copy-done.2), custom_call_target="tpu_custom_call" | custom-call | flops 1000000 | bytes 2000000 | tf_op jit(solution)/shard_map/pallas_call | solution.py:308
  66.4 9.4 %all-to-all-start.1 = ((f32[128,1,1280]{2,1,0:T(1,128)}), f32[128,1,1280]{2,1,0:T(1,128)}, u32[]{:S(2)}, u32[]{:S(2)}) async-start(f32[128,1,1280]{2,1,0:T(1,128)} %bitcast.11), calls=%async_computation.1 | async-start | bytes 1310720 | tf_op jit(solution)/shard_map/all_to_all | solution.py:260
  75.9 3.4 %collective-permute-start.6 = (s32[4,1,40,128]{3,2,1,0:T(8,128)S(1)}, s32[4,1,40,128]{3,2,1,0:T(8,128)S(1)}, u32[]{:S(2)}, u32[]{:S(2)}) collective-permute-start(s32[4,1,40,128]{3,2,1,0:T(8,128)S(1)} %pad_add_fusion.2), channel_id=1, source_target_pairs={{0,1},{1,0},{2,3},{3,2},{4,5},{5,4},{6,7},{7,6},{8,9},{9,8},{10,11... | collective-permute-start | bytes 245768 | tf_op jit(solution)/shard_map/ppermute | solution.py:290
  79.3 4.6 %collective-permute-done.6 = s32[4,1,40,128]{3,2,1,0:T(8,128)S(1)} collective-permute-done((s32[4,1,40,128]{3,2,1,0:T(8,128)S(1)}, s32[4,1,40,128]{3,2,1,0:T(8,128)S(1)}, u32[]{:S(2)}, u32[]{:S(2)}) %collective-permute-start.6) | collective-permute-done | bytes 81952 | tf_op jit(solution)/shard_map/ppermute | solution.py:290
  84.0 4.9 %collective-permute-start.7 = (s32[4,2,40,128]{3,2,1,0:T(8,128)S(1)}, s32[4,2,40,128]{3,2,1,0:T(8,128)S(1)}, u32[]{:S(2)}, u32[]{:S(2)}) collective-permute-start(s32[4,2,40,128]{3,2,1,0:T(8,128)S(1)} %pad_add_fusion.1), channel_id=1, source_target_pairs={{0,2},{1,3},{2,0},{3,1},{4,6},{5,7},{6,4},{7,5},{8,10},{9,11},{10,... | collective-permute-start | bytes 491528 | tf_op jit(solution)/shard_map/ppermute | solution.py:290
  88.9 0.7 dynamic-slice_bitcast_fusion.shift_ref
  89.6 5.4 %collective-permute-done.7 = s32[4,2,40,128]{3,2,1,0:T(8,128)S(1)} collective-permute-done((s32[4,2,40,128]{3,2,1,0:T(8,128)S(1)}, s32[4,2,40,128]{3,2,1,0:T(8,128)S(1)}, u32[]{:S(2)}, u32[]{:S(2)}) %collective-permute-start.7) | collective-permute-done | bytes 163872 | tf_op jit(solution)/shard_map/ppermute | solution.py:290
  95.1 1.6 shard_map.116.coefficient_ref
  96.7 0.0 copy-start.1
  96.7 4.0 %shard_map.117 = f32[1024,128]{1,0:T(8,128)S(1)} custom-call(f32[1280,128]{1,0:T(8,128)} %bitcast.12.spectrum_ref, f32[9,40,2,8,128]{4,3,2,1,0:T(8,128)S(1)} %shard_map.116.coefficient_ref), custom_call_target="tpu_custom_call" | custom-call | flops 1000000 | bytes 2000000 | tf_op jit(solution)/shard_map/pallas_call | solution.py:312
  100.7 28.2 %all_to_all.36 = f32[128,8,128]{2,1,0:T(8,128)S(1)} all-to-all(f32[128,8,128]{2,1,0:T(8,128)S(1)} %bitcast.35), channel_id=1, replica_groups=mesh['yh'=2,'zh'=2,'zl'=4,'core'=2,'yl'=4,'x'=4] {'zl','core','yl','x'}, dimensions={0} | all-to-all | bytes 1048576 | tf_op jit(solution)/shard_map/all_to_all | solution.py:260
  128.9 0.7 shard_map.118
  129.5 27.7 %all_to_all.37 = f32[32,32,128]{2,1,0:T(8,128)S(1)} all-to-all(f32[32,32,128]{2,1,0:T(8,128)S(1)} %bitcast.33), channel_id=1, replica_groups=mesh['yh'=2,'zh'=2,'zl'=4,'core'=2,'yl'=4,'x'=4] {'yh','zh','zl','core'}, dimensions={0} | all-to-all | bytes 1048576 | tf_op jit(solution)/shard_map/all_to_all | solution.py:260
  157.2 0.9 shard_map.119
  (18 shorter events, 0.2 us)
Async XLA Ops:
  1.5 63.3 %copy-start.2 = (f32[256,256]{1,0:T(8,128)S(1)}, f32[256,256]{1,0:T(8,128)}, u32[]{:S(2)}) copy-start(f32[256,256]{1,0:T(8,128)} %constant.53.clone.table_ref) | copy-start | bytes 786436
  2.7 17.7 %collective-permute-start.1 = (f32[8,128,128]{2,1,0:T(8,128)S(1)}, f32[8,128,128]{2,1,0:T(8,128)S(1)}, u32[]{:S(2)}, u32[]{:S(2)}) collective-permute-start(f32[8,128,128]{2,1,0:T(8,128)S(1)} %bitcast_multiply_fusion.masked_ref), channel_id=1, source_target_pairs={{0,1},{1,2},{2,3},{3,4},{4,5},{5,6},{6,7},{7,8},{8,9},{9,10},{10,1... | collective-permute-start | bytes 1572872 | tf_op jit(solution)/shard_map/ppermute | solution.py:276
  6.1 15.4 %collective-permute-start = (f32[8,128,128]{2,1,0:T(8,128)S(1)}, f32[8,128,128]{2,1,0:T(8,128)S(1)}, u32[]{:S(2)}, u32[]{:S(2)}) collective-permute-start(f32[8,128,128]{2,1,0:T(8,128)S(1)} %bitcast_multiply_fusion.masked_ref), channel_id=1, source_target_pairs={{1,0},{2,1},{3,2},{4,3},{5,4},{6,5},{7,6},{8,7},{9,8},{10,9},{11,1... | collective-permute-start | bytes 1572872 | tf_op jit(solution)/shard_map/ppermute | solution.py:277
  10.6 4.1 %collective-permute-start.2 = (f32[128,128]{1,0:T(8,128)S(1)}, f32[128,128]{1,0:T(8,128)S(1)}, u32[]{:S(2)}, u32[]{:S(2)}) collective-permute-start(f32[128,128]{1,0:T(8,128)S(1)} %slice_bitcast_fusion), channel_id=1, source_target_pairs={{0,16},{16,32},{32,48},{48,64},{64,80},{80,96},{96,112},{112,128},... | collective-permute-start | bytes 196616 | tf_op jit(solution)/shard_map/ppermute | solution.py:278
  12.7 1.0 copy-start
  21.5 0.8 copy-start.3
  23.6 41.2 %all-to-all-start = ((f32[32,40,128]{2,1,0:T(8,128)}), f32[32,40,128]{2,1,0:T(8,128)S(1)}, u32[]{:S(2)}, u32[]{:S(2)}) async-start(f32[32,40,128]{2,1,0:T(8,128)} %bitcast.9), calls=%async_computation | async-start | bytes 1310720 | tf_op jit(solution)/shard_map/all_to_all | solution.py:260
  40.2 35.6 %collective-permute-start.4 = (s32[1,1,40,128]{3,2,1,0:T(8,128)S(1)}, s32[1,1,40,128]{3,2,1,0:T(8,128)S(1)}, u32[]{:S(2)}, u32[]{:S(2)}) collective-permute-start(s32[1,1,40,128]{3,2,1,0:T(8,128)S(1)} %fusion), channel_id=1, source_target_pairs={{0,8},{4,12},{8,0},{12,4},{1,9},{5,13},{9,1},{13,5},{2,10},{6,14},... | collective-permute-start | bytes 61448 | tf_op jit(solution)/shard_map/ppermute | solution.py:286
  44.7 31.1 %collective-permute-start.5 = (s32[1,1,40,128]{3,2,1,0:T(8,128)S(1)}, s32[1,1,40,128]{3,2,1,0:T(8,128)S(1)}, u32[]{:S(2)}, u32[]{:S(2)}) collective-permute-start(s32[1,1,40,128]{3,2,1,0:T(8,128)S(1)} %fusion), channel_id=1, source_target_pairs={{0,12},{4,8},{8,4},{12,0},{1,13},{5,9},{9,5},{13,1},{2,14},{6,10},... | collective-permute-start | bytes 61448 | tf_op jit(solution)/shard_map/ppermute | solution.py:286
  46.6 29.2 %collective-permute-start.3 = (s32[1,1,40,128]{3,2,1,0:T(8,128)S(1)}, s32[1,1,40,128]{3,2,1,0:T(8,128)S(1)}, u32[]{:S(2)}, u32[]{:S(2)}) collective-permute-start(s32[1,1,40,128]{3,2,1,0:T(8,128)S(1)} %fusion), channel_id=1, source_target_pairs={{0,4},{4,0},{8,12},{12,8},{1,5},{5,1},{9,13},{13,9},{2,6},{6,2},{1... | collective-permute-start | bytes 61448 | tf_op jit(solution)/shard_map/ppermute | solution.py:286
  66.4 30.3 %all-to-all-start.1 = ((f32[128,1,1280]{2,1,0:T(1,128)}), f32[128,1,1280]{2,1,0:T(1,128)}, u32[]{:S(2)}, u32[]{:S(2)}) async-start(f32[128,1,1280]{2,1,0:T(1,128)} %bitcast.11), calls=%async_computation.1 | async-start | bytes 1310720 | tf_op jit(solution)/shard_map/all_to_all | solution.py:260
  75.9 8.0 %collective-permute-start.6 = (s32[4,1,40,128]{3,2,1,0:T(8,128)S(1)}, s32[4,1,40,128]{3,2,1,0:T(8,128)S(1)}, u32[]{:S(2)}, u32[]{:S(2)}) collective-permute-start(s32[4,1,40,128]{3,2,1,0:T(8,128)S(1)} %pad_add_fusion.2), channel_id=1, source_target_pairs={{0,1},{1,0},{2,3},{3,2},{4,5},{5,4},{6,7},{7,6},{8,9},{9,8},{10,11... | collective-permute-start | bytes 245768 | tf_op jit(solution)/shard_map/ppermute | solution.py:290
  84.0 11.1 %collective-permute-start.7 = (s32[4,2,40,128]{3,2,1,0:T(8,128)S(1)}, s32[4,2,40,128]{3,2,1,0:T(8,128)S(1)}, u32[]{:S(2)}, u32[]{:S(2)}) collective-permute-start(s32[4,2,40,128]{3,2,1,0:T(8,128)S(1)} %pad_add_fusion.1), channel_id=1, source_target_pairs={{0,2},{1,3},{2,0},{3,1},{4,6},{5,7},{6,4},{7,5},{8,10},{9,11},{10,... | collective-permute-start | bytes 491528 | tf_op jit(solution)/shard_map/ppermute | solution.py:290
  96.7 32.2 %copy-start.1 = (f32[256,256]{1,0:T(8,128)S(1)}, f32[256,256]{1,0:T(8,128)}, u32[]{:S(2)}) copy-start(f32[256,256]{1,0:T(8,128)} %constant.55.clone.table_ref) | copy-start | bytes 786436
